TPU v7x, 32 devices: a whole 2x2x4 slice. The times are simulated.
32 devices in a mesh: scene: 2 (over x), frame: 16 (over z, y, core).
Axes of the slice: x: 2, y: 2, z: 4, core: 2. Of those that a mesh axis runs over, the one named last changes fastest.
Arguments:
- tokens: bfloat16 [2, 2304, 1024], P('scene', 'frame'), may hold values from -6 to 6
- patch_counts: int32 [2, 16], P('scene', 'frame'), may hold values from 43 to 139, as said below
- first_gain: bfloat16 [2, 1024], replicated, may hold values from 0.25 to 1.75
- first_shift: bfloat16 [2, 1024], replicated, may hold values from -3 to 3
- joint_weight: bfloat16 [2, 1024, 3072], replicated, may hold values from -0.1875 to 0.1875
- joint_bias: bfloat16 [2, 3072], replicated, may hold values from -3 to 3
- query_gain: bfloat16 [2, 64], replicated, may hold values from 0.796875 to 1.796875
- query_shift: bfloat16 [2, 64], replicated, may hold values from -3 to 3
- key_gain: bfloat16 [2, 64], replicated, may hold values from 0.796875 to 1.796875
- mixer_weight: bfloat16 [2, 1024, 1024], replicated, may hold values from -2 to 2
- mixer_bias: bfloat16 [2, 1024], replicated, may hold values from -3 to 3
- mixer_scale: bfloat16 [2, 1024], replicated, may hold values from 0.25 to 1.75
- second_gain: bfloat16 [2, 1024], replicated, may hold values from 0.25 to 1.75
- second_shift: bfloat16 [2, 1024], replicated, may hold values from -3 to 3
- inner_weight: bfloat16 [2, 1024, 4096], replicated, may hold values from -0.1875 to 0.1875
- inner_bias: bfloat16 [2, 4096], replicated, may hold values from -3 to 3
- outer_weight: bfloat16 [2, 4096, 1024], replicated, may hold values from -0.09375 to 0.09375
- outer_bias: bfloat16 [2, 1024], replicated, may hold values from -3 to 3
- outer_scale: bfloat16 [2, 1024], replicated, may hold values from 0.25 to 1.75
- cotangent: bfloat16 [2, 2304, 1024], P('scene', 'frame'), may hold values from -6 to 6
Outputs:
- layer_out: bfloat16 [2, 2304, 1024], P('scene', 'frame')
- grad_tokens: bfloat16 [2, 2304, 1024], P('scene', 'frame')
- grad_first_gain: float32 [2, 1024], replicated
- grad_first_shift: float32 [2, 1024], replicated
- grad_joint_weight: float32 [2, 1024, 3072], P(None, ('scene', 'frame'))
- grad_joint_bias: float32 [2, 3072], replicated
- grad_query_gain: float32 [2, 64], replicated
- grad_query_shift: float32 [2, 64], replicated
- grad_key_gain: float32 [2, 64], replicated
- grad_mixer_weight: float32 [2, 1024, 1024], P(None, ('scene', 'frame'))
- grad_mixer_bias: float32 [2, 1024], replicated
- grad_mixer_scale: float32 [2, 1024], replicated
- grad_second_gain: float32 [2, 1024], replicated
- grad_second_shift: float32 [2, 1024], replicated
- grad_inner_weight: float32 [2, 1024, 4096], P(None, ('scene', 'frame'))
- grad_inner_bias: float32 [2, 4096], replicated
- grad_outer_weight: float32 [2, 4096, 1024], P(None, ('scene', 'frame'))
- grad_outer_bias: float32 [2, 1024], replicated
- grad_outer_scale: float32 [2, 1024], replicated
Inputs may be any that keep to these rules, and one draw needn't show every extreme that they name: `patch_counts`: A frame's 5 camera and register tokens and then its patches fill the first slots of its 144; in every scene some frame has the most patches and some the fewest.
All inputs are finite; a program needn't handle non-finite values.
Results may differ from a plain program's by a relative error of at most 0.014.
Values may be sent and summed in bfloat16 or wider, within the bound.
A program may use at most 384 MiB of HBM per device.

v0:
```python
from functools import partial

import jax
import jax.numpy as jnp
from jax import lax
from jax.experimental import pallas as pl
from jax.experimental.pallas import tpu as pltpu
from jax.sharding import PartitionSpec as P

SPECIAL = 5
CHUNK = 512
LANES = 128
SLAB = 256
norm_eps = 1e-06
head_eps = 1e-05
closed_score = -10000.0
f32 = jnp.float32
bf16 = jnp.bfloat16


def nn(a, b):
    return lax.dot_general(a, b, (((1,), (0,)), ((), ())), preferred_element_type=f32)


def nt(a, b):
    return lax.dot_general(a, b, (((1,), (1,)), ((), ())), preferred_element_type=f32)


def tn(a, b):
    return lax.dot_general(a, b, (((0,), (0,)), ((), ())), preferred_element_type=f32)


def row(ref, index):
    return ref[...].astype(f32)[index : index + 1, :]


def col_sum(value):
    return jnp.sum(value, axis=0, keepdims=True)


def center_norm(value, eps):
    centered = value - jnp.mean(value, axis=-1, keepdims=True)
    spread = lax.rsqrt(jnp.mean(centered * centered, axis=-1, keepdims=True) + eps)
    return centered * spread, spread


def norm_back(grad_hat, hat, spread):
    mean_grad = jnp.mean(grad_hat, axis=-1, keepdims=True)
    mean_both = jnp.mean(grad_hat * hat, axis=-1, keepdims=True)
    return spread * (grad_hat - mean_grad - hat * mean_both)


def seg_matrix(width, head, value):
    shift = head.bit_length() - 1
    first = lax.shift_right_logical(lax.broadcasted_iota(jnp.int32, (width, width), 0), shift)
    second = lax.shift_right_logical(lax.broadcasted_iota(jnp.int32, (width, width), 1), shift)
    return jnp.where(first == second, value, 0.0).astype(bf16)


def seg_dot(value, matrix):
    high = value.astype(bf16)
    low = (value - high.astype(f32)).astype(bf16)
    return nn(high, matrix) + nn(low, matrix)


def seg_norm(value, mean_matrix):
    centered = value - seg_dot(value, mean_matrix)
    spread = lax.rsqrt(seg_dot(centered * centered, mean_matrix) + head_eps)
    return centered * spread, spread


def first_lanes(rows):
    return lax.broadcasted_iota(jnp.int32, (rows, LANES), 1) < LANES // 2


def turn(value):
    return pltpu.roll(value, LANES // 2, value.ndim - 1)


def pack_pair(slab):
    half = slab.shape[0] // 2
    top, bottom = slab[:half], slab[half:]
    low = first_lanes(half)
    return jnp.where(low, top, turn(bottom)), jnp.where(low, turn(top), bottom)


def unpack_pair(even, odd):
    low = first_lanes(even.shape[0])
    top = jnp.where(low, even, turn(odd))
    bottom = jnp.where(low, turn(even), odd)
    return jnp.concatenate([top, bottom], axis=0)


def erf(value):
    value = jnp.clip(value, -4.0, 4.0)
    square = value * value
    top = jnp.full_like(square, -2.72614225801306e-10)
    for coefficient in (
        2.77068142495902e-08,
        -2.10102402082508e-06,
        -5.69250639462346e-05,
        -7.34990630326855e-04,
        -2.95459980854025e-03,
        -1.60960333262415e-02,
    ):
        top = top * square + coefficient
    bottom = jnp.full_like(square, -1.45660718464996e-05)
    for coefficient in (
        -2.13374055278905e-04,
        -1.68282697438203e-03,
        -7.37332916720468e-03,
        -1.42647390514189e-02,
    ):
        bottom = bottom * square + coefficient
    return value * top / bottom


def full(shape):
    return pl.BlockSpec(shape, lambda *_: (0,) * len(shape))


def sds(shape, dtype):
    return jax.ShapeDtypeStruct(shape, dtype)


def call(body, name, grid, in_specs, out_specs, out_shape, scratch, flops, moved):
    return pl.pallas_call(
        body,
        name=name,
        out_shape=out_shape,
        grid_spec=pltpu.PrefetchScalarGridSpec(
            num_scalar_prefetch=1,
            grid=grid,
            in_specs=in_specs,
            out_specs=out_specs,
            scratch_shapes=scratch,
        ),
        cost_estimate=pl.CostEstimate(flops=flops, bytes_accessed=moved, transcendentals=0),
    )


def joint_body(
    block, packed, head, meta, x_ref, gain_ref, shift_ref, pattern_ref, w_ref, b_ref,
    own_ref, other_ref, pre_ref, out_ref, normed_ref, *stage
):
    step = pl.program_id(0)
    rows, width = normed_ref.shape
    per_part = width // CHUNK
    half = rows // 2

    @pl.when(step == 0)
    def _():
        hat, _ = center_norm(x_ref[...].astype(f32), norm_eps)
        normed = (hat * row(gain_ref, block) + row(shift_ref, block)).astype(bf16)
        normed_ref[...] = normed

        @pl.when(meta[0] == 0)
        def _():
            own_ref[...] = normed[:, : width // 2]
            other_ref[...] = normed[:, width // 2 :]

        @pl.when(meta[0] != 0)
        def _():
            own_ref[...] = normed[:, width // 2 :]
            other_ref[...] = normed[:, : width // 2]

        if packed:
            count = jnp.full((8, LANES), meta[3], jnp.int32).astype(f32)
            for place in range(stage[0].shape[0]):
                stage[0][place, 3 * half : 3 * half + 8, :] = count

    joined = nn(normed_ref[...], w_ref[0]) + row(b_ref, block)
    pattern = pattern_ref[...]

    def emit(part, values):
        if packed:
            base = (step - part * per_part) * (CHUNK // head)
            for slab in range(CHUNK // LANES):
                even, odd = pack_pair(values[:, slab * LANES : (slab + 1) * LANES])
                stage[0][base + 2 * slab, part * half : (part + 1) * half, :] = even
                stage[0][base + 2 * slab + 1, part * half : (part + 1) * half, :] = odd
        else:
            out_ref[...] = values.astype(bf16)

    def normed_heads(gain, shift):
        mean_matrix = seg_matrix(SLAB, head, 1.0 / head)
        pieces = []
        for slab in range(CHUNK // SLAB):
            hat, _ = seg_norm(joined[:, slab * SLAB : (slab + 1) * SLAB], mean_matrix)
            pieces.append(hat * gain if shift is None else hat * gain + shift)
        return jnp.concatenate(pieces, axis=1)

    scale = head ** (-0.5)

    @pl.when(step < per_part)
    def _():
        pre_ref[...] = joined
        emit(0, normed_heads(
            pattern[3 * block : 3 * block + 1] * scale,
            pattern[3 * block + 1 : 3 * block + 2] * scale,
        ))

    @pl.when((step >= per_part) & (step < 2 * per_part))
    def _():
        pre_ref[...] = joined
        emit(1, normed_heads(pattern[3 * block + 2 : 3 * block + 3], None))

    @pl.when(step >= 2 * per_part)
    def _():
        emit(2, joined)

    if packed:

        @pl.when(step == 3 * per_part - 1)
        def _():
            out_ref[...] = stage[0][...].astype(bf16)


def joint_forward(block, packed, head, meta, x, gain, shift, pattern, weight, bias):
    rows, width = x.shape
    per_part = width // CHUNK
    heads = width // head
    packed_rows = 3 * (rows // 2) + 8
    if packed:
        out_spec, out = full((heads, packed_rows, LANES)), sds((heads, packed_rows, LANES), bf16)
        extra = [pltpu.VMEM((heads, packed_rows, LANES), f32)]
    else:
        out_spec = pl.BlockSpec((rows, CHUNK), lambda j, m: (0, j))
        out = sds((rows, 3 * width), bf16)
        extra = []
    return call(
        partial(joint_body, block, packed, head),
        f"joint_forward_{block}",
        (3 * per_part,),
        [
            full((rows, width)),
            full(gain.shape),
            full(shift.shape),
            full(pattern.shape),
            pl.BlockSpec((1, width, CHUNK), lambda j, m: (block, 0, j)),
            pl.BlockSpec((2, CHUNK), lambda j, m: (0, j)),
        ],
        [
            full((rows, width // 2)),
            full((rows, width // 2)),
            pl.BlockSpec((rows, CHUNK), lambda j, m: (0, jnp.minimum(j, 2 * per_part - 1))),
            out_spec,
        ],
        [
            sds((rows, width // 2), bf16),
            sds((rows, width // 2), bf16),
            sds((rows, 2 * width), f32),
            out,
        ],
        [pltpu.VMEM((rows, width), bf16)] + extra,
        2 * rows * width * 3 * width,
        6 * width * width + 16 * rows * width,
    )(meta, x, gain, shift, pattern, weight, bias)


def lane_picks():
    lane = lax.broadcasted_iota(jnp.int32, (1, LANES), 1)
    low = jnp.where(lane < LANES // 2, 1.0, 0.0)
    return low.astype(bf16), (1.0 - low).astype(bf16)


def open_row(meta, rows):
    place = lax.broadcasted_iota(jnp.int32, (1, rows), 1)
    return jnp.where(place < meta[3] + SPECIAL, 0.0, closed_score)


def frame_body(meta, qkv_ref, out_ref):
    rows, width = out_ref.shape
    bias = open_row(meta, rows)
    picks = lane_picks()
    low = first_lanes(rows)
    for slab in range(width // LANES):
        at = slab * LANES
        queries = qkv_ref[:, at : at + LANES]
        keys = qkv_ref[:, width + at : width + at + LANES]
        values = qkv_ref[:, 2 * width + at : 2 * width + at + LANES]
        results = []
        for pick in picks:
            power = jnp.exp(nt(queries * pick, keys) + bias)
            probs = power / jnp.sum(power, axis=-1, keepdims=True)
            results.append(nn(probs.astype(bf16), values))
        out_ref[:, at : at + LANES] = jnp.where(low, results[0], results[1]).astype(bf16)


def frame_forward(meta, qkv):
    rows = qkv.shape[0]
    width = qkv.shape[1] // 3
    return call(
        frame_body,
        "frame_forward",
        (1,),
        [full(qkv.shape)],
        full((rows, width)),
        sds((rows, width), bf16),
        [],
        4 * rows * rows * width,
        8 * rows * width,
    )(meta, qkv)


def frame_back_body(meta, qkv_ref, grad_ref, out_ref):
    rows, width = grad_ref.shape
    bias = open_row(meta, rows)
    picks = lane_picks()
    low = first_lanes(rows)
    scale = (LANES // 2) ** (-0.5)
    for slab in range(width // LANES):
        at = slab * LANES
        queries = qkv_ref[:, at : at + LANES]
        keys = qkv_ref[:, width + at : width + at + LANES]
        values = qkv_ref[:, 2 * width + at : 2 * width + at + LANES]
        grads = grad_ref[:, at : at + LANES]
        found = []
        for pick in picks:
            power = jnp.exp(nt(queries * pick, keys) + bias)
            probs = power / jnp.sum(power, axis=-1, keepdims=True)
            grad_probs = nt(grads * pick, values)
            delta = jnp.sum(probs * grad_probs, axis=-1, keepdims=True)
            grad_scores = (probs * (grad_probs - delta)).astype(bf16)
            found.append((
                nn(grad_scores, keys) * scale,
                tn(grad_scores, queries),
                tn(probs.astype(bf16), grads),
            ))
        for part in range(3):
            out_ref[:, part * width + at : part * width + at + LANES] = jnp.where(
                low, found[0][part], found[1][part]
            )


def frame_backward(meta, qkv, grad):
    rows, width = grad.shape
    return call(
        frame_back_body,
        "frame_backward",
        (1,),
        [full(qkv.shape), full(grad.shape)],
        full((rows, 3 * width)),
        sds((rows, 3 * width), f32),
        [],
        10 * rows * rows * width,
        20 * rows * width,
    )(meta, qkv, grad)


def packed_part(value, part, half):
    whole = value.astype(f32)
    return whole[:, part * half : (part + 1) * half, :].reshape(-1, LANES)


def open_slots(value, half):
    count = value.astype(f32)[:, 3 * half : 3 * half + 8, :]
    count = jnp.concatenate([count] * (half // 8), axis=1)
    place = lax.broadcasted_iota(jnp.int32, count.shape, 1).astype(f32)
    return (
        (place < count + SPECIAL).reshape(-1, LANES),
        (place + half < count + SPECIAL).reshape(-1, LANES),
    )


MESH = pl.DeviceIdType.MESH


def peers_of(frames):
    scene = lax.axis_index("scene")
    frame = lax.axis_index("frame")
    bits = []
    bit = 1
    while bit < frames:
        value = lax.rem(frame // bit, 2)
        bits.append((value, (scene, frame + bit * (1 - 2 * value))))
        bit *= 2
    core, core_peer = bits[0]
    scene_peer = (1 - scene, frame)
    cross_peer = (1 - scene, core_peer[1])
    return core, core_peer, scene_peer, cross_peer, bits[1:]


def enter(targets):
    barrier = pltpu.get_barrier_semaphore()
    for target in targets:
        pl.semaphore_signal(barrier, inc=1, device_id=target, device_id_type=MESH)
    pl.semaphore_wait(barrier, len(targets))


def enter_scene(frames):
    barrier = pltpu.get_barrier_semaphore()
    _, _, scene_peer, cross_peer, _ = peers_of(frames)
    scene = lax.axis_index("scene")
    frame = lax.axis_index("frame")
    for target in (scene_peer, cross_peer):
        pl.semaphore_signal(barrier, inc=1, device_id=target, device_id_type=MESH)

    @pl.loop(1, frames)
    def _(offset):
        pl.semaphore_signal(
            barrier, inc=1, device_id=(scene, lax.rem(frame + offset, frames)), device_id_type=MESH
        )

    pl.semaphore_wait(barrier, frames + 1)


def remote(source, target, send, recv, device):
    return pltpu.make_async_remote_copy(
        src_ref=source, dst_ref=target, send_sem=send, recv_sem=recv, device_id=device, device_id_type=MESH
    )


class Share:
    def __init__(self, frames, pairs, outs, send, recv):
        _, core_peer, scene_peer, _, _ = peers_of(frames)
        self.first, self.second = [], []
        for index, ((own, other), out) in enumerate(zip(pairs, outs)):
            self.first.append(remote(other, out.at[0], send.at[3 * index], recv.at[3 * index], scene_peer))
            self.first.append(remote(own, out.at[1], send.at[3 * index + 1], recv.at[3 * index + 1], core_peer))
            self.second.append(
                remote(out.at[0], out.at[2], send.at[3 * index + 2], recv.at[3 * index + 2], core_peer)
            )

    def start(self):
        for copy in self.first:
            copy.start()

    def relay(self):
        for index, copy in enumerate(self.second):
            self.first[2 * index].wait_recv()
            copy.start()

    def close(self):
        for index, copy in enumerate(self.second):
            self.first[2 * index].wait_send()
            self.first[2 * index + 1].wait()
            copy.wait()


def scene_body(
    frames, half, span, n_share, meta, pack_ref, *refs
):
    heads = pack_ref.shape[0]
    pairs = [(refs[2 * index], refs[2 * index + 1]) for index in range(n_share)]
    refs = refs[2 * n_share :]
    att_ref, kept_ref, out_ref, log_ref = refs[:4]
    outs, refs = refs[4 : 4 + n_share], refs[4 + n_share :]
    queries, keys, values, sent, a_send, a_recv, b_send, b_recv, s_send, s_recv, own_sem = refs
    n = queries.shape[0] // 2
    m = keys.shape[0] // 2
    scene = lax.axis_index("scene")
    frame = lax.axis_index("frame")
    part = frame // heads
    own = pltpu.make_async_copy(pack_ref.at[lax.rem(frame, heads)], kept_ref.at[frame], own_sem)
    own.start()
    share = Share(frames, pairs, outs, s_send, s_recv)
    enter_scene(frames)

    def to_head(offset):
        target = lax.rem(frame + offset, frames)
        return remote(
            pack_ref.at[lax.rem(target, heads)], kept_ref.at[frame], a_send.at[offset], a_recv.at[offset], (scene, target)
        )

    @pl.loop(1, frames)
    def _(offset):
        to_head(offset).start()

    share.start()
    own.wait()

    @pl.loop(1, frames)
    def _(offset):
        to_head(offset).wait_recv()

    first = pl.multiple_of(part * heads, heads)
    q = packed_part(kept_ref[pl.ds(first, heads)], 0, half)
    low_n, low_m = first_lanes(n), first_lanes(m)
    queries[:n, :] = jnp.where(low_n, q, 0.0).astype(bf16)
    queries[n:, :] = jnp.where(low_n, turn(q), 0.0).astype(bf16)
    k = packed_part(kept_ref[...], 1, half)
    keys[:m, :] = k.astype(bf16)
    keys[m:, :] = turn(k).astype(bf16)
    v = packed_part(kept_ref[...], 2, half)
    open_low, open_high = open_slots(kept_ref[...], half)
    values[:m, :] = jnp.where(open_low, jnp.where(low_m, v, 1.0), 0.0).astype(bf16)
    values[m:, :] = jnp.where(open_high, jnp.where(low_m, turn(v), 1.0), 0.0).astype(bf16)
    low = first_lanes(LANES)

    @pl.loop(0, n // LANES)
    def _(piece):
        at = pl.multiple_of(piece * LANES, LANES)
        some = jnp.concatenate([queries[pl.ds(at, LANES), :], queries[pl.ds(n + at, LANES), :]], axis=0)
        total = jnp.zeros((2 * LANES, LANES), f32)
        for start in range(0, 2 * m, span):
            power = jnp.exp(nt(some, keys[start : start + span, :])).astype(bf16)
            total = total + nn(power, values[start : start + span, :])
        first, second = total[:LANES], total[LANES:]
        bottom = jnp.where(low, turn(first), second)
        result = jnp.where(low, first, turn(second)) / bottom
        out_ref[pl.ds(at, LANES), :] = result
        log_ref[pl.ds(at, LANES), :] = jnp.log(bottom)

    share.relay()
    sent[...] = out_ref[...].reshape(heads, half, LANES).astype(bf16)
    place = lax.rem(frame, heads)

    def from_head(offset):
        target = lax.rem(place + offset, heads)
        return remote(
            sent.at[target], att_ref.at[place], b_send.at[offset], b_recv.at[offset], (scene, part * heads + target)
        )

    @pl.loop(1, heads)
    def _(offset):
        from_head(offset).start()

    att_ref[place] = sent[place]

    @pl.loop(1, frames)
    def _(offset):
        to_head(offset).wait_send()

    @pl.loop(1, heads)
    def _(offset):
        from_head(offset).wait()

    share.close()


any_space = pl.BlockSpec(memory_space=pl.ANY)
vmem_space = pl.BlockSpec(memory_space=pltpu.VMEM)
dma = pltpu.SemaphoreType.DMA


def scene_forward(frames, meta, pack, half, pairs):
    heads = pack.shape[0]
    n = heads * half
    m = frames * half
    span = m // 2
    while span > 640:
        span = span // 2
    flat = [value for pair in pairs for value in pair]
    results = pl.pallas_call(
        partial(scene_body, frames, half, span, len(pairs)),
        name="scene_forward",
        out_shape=[
            sds((heads, half, LANES), bf16),
            sds((frames,) + pack.shape[1:], bf16),
            sds((n, LANES), f32),
            sds((n, LANES), f32),
        ]
        + [sds((3,) + own.shape, bf16) for own, _ in pairs],
        grid_spec=pltpu.PrefetchScalarGridSpec(
            num_scalar_prefetch=1,
            grid=(1,),
            in_specs=[vmem_space] + [any_space] * len(flat),
            out_specs=[vmem_space] * 4 + [any_space] * len(pairs),
            scratch_shapes=[
                pltpu.VMEM((2 * n, LANES), bf16),
                pltpu.VMEM((2 * m, LANES), bf16),
                pltpu.VMEM((2 * m, LANES), bf16),
                pltpu.VMEM((heads, half, LANES), bf16),
                dma((frames,)),
                dma((frames,)),
                dma((heads,)),
                dma((heads,)),
                dma((3 * len(pairs),)),
                dma((3 * len(pairs),)),
                dma(()),
            ],
        ),
        compiler_params=pltpu.CompilerParams(collective_id=1, has_side_effects=True),
        cost_estimate=pl.CostEstimate(flops=16 * n * m * LANES, bytes_accessed=20 * n * LANES, transcendentals=0),
    )(meta, pack, *flat)
    return results[0], results[1], results[2], results[3], results[4:]


def three_lanes(value, closed):
    lane = lax.broadcasted_iota(jnp.int32, value.shape, 1)
    base = LANES // 2
    high = value.astype(bf16).astype(f32)
    rest = value - high
    middle = rest.astype(bf16).astype(f32)
    last = rest - middle
    result = jnp.where(lane == base, high, jnp.where(lane == base + 1, middle, last))
    return jnp.where(lane < base + 3, result, jnp.where(lane == base + 3, closed, 0.0))


def scene_back_body(frames, half, span, n_share, meta, kept_ref, grad_ref, out_ref, log_ref, *refs):
    heads = grad_ref.shape[0]
    pairs = [(refs[2 * index], refs[2 * index + 1]) for index in range(n_share)]
    refs = refs[2 * n_share :]
    back_ref, outs, refs = refs[0], refs[1 : 1 + n_share], refs[1 + n_share :]
    queries, keys, values, grads, turned, came, dk_ref, dv_ref, sent_q, sent_kv = refs[:10]
    a_send, a_recv, b_send, b_recv, c_send, c_recv, s_send, s_recv = refs[10:]
    n = queries.shape[0] // 2
    m = keys.shape[0] // 2
    scene = lax.axis_index("scene")
    frame = lax.axis_index("frame")
    part = frame // heads
    place = lax.rem(frame, heads)
    share = Share(frames, pairs, outs, s_send, s_recv)
    enter_scene(frames)

    def to_head(offset):
        target = lax.rem(place + offset, heads)
        return remote(
            grad_ref.at[target], came.at[place], a_send.at[offset], a_recv.at[offset], (scene, part * heads + target)
        )

    @pl.loop(1, heads)
    def _(offset):
        to_head(offset).start()

    share.start()
    came[place] = grad_ref[place]
    first = pl.multiple_of(part * heads, heads)
    low_n, low_m = first_lanes(n), first_lanes(m)
    base = LANES // 2
    q = packed_part(kept_ref[pl.ds(first, heads)], 0, half)
    log = -log_ref[...]
    queries[:n, :] = jnp.where(low_n, q, three_lanes(turn(log), closed_score)).astype(bf16)
    queries[n:, :] = jnp.where(low_n, turn(q), three_lanes(log, closed_score)).astype(bf16)
    lane = lax.broadcasted_iota(jnp.int32, (m, LANES), 1)
    ones = jnp.where(lane < base + 3, 1.0, 0.0)
    open_low, open_high = open_slots(kept_ref[...], half)
    k = packed_part(kept_ref[...], 1, half)
    for place_at, k_now, is_open in ((0, k, open_low), (m, turn(k), open_high)):
        tail = jnp.where((lane == base + 3) & jnp.logical_not(is_open), 1.0, ones)
        keys[place_at : place_at + m, :] = jnp.where(low_m, k_now, tail).astype(bf16)
    v = packed_part(kept_ref[...], 2, half)
    values[:m, :] = jnp.where(low_m, v, ones).astype(bf16)
    values[m:, :] = jnp.where(low_m, turn(v), ones).astype(bf16)
    turned[...] = jnp.zeros_like(turned)
    low = first_lanes(LANES)

    @pl.loop(1, heads)
    def _(offset):
        to_head(offset).wait_recv()

    g = came[...].astype(f32).reshape(n, LANES)
    delta = -seg_dot(g * out_ref[...], seg_matrix(LANES, base, 1.0))
    grads[:n, :] = jnp.where(low_n, g, three_lanes(turn(delta), 0.0)).astype(bf16)
    grads[n:, :] = jnp.where(low_n, turn(g), three_lanes(delta, 0.0)).astype(bf16)

    @pl.loop(0, m // LANES)
    def _(piece):
        at = pl.multiple_of(piece * LANES, LANES)
        key_part = jnp.concatenate([keys[pl.ds(at, LANES), :], keys[pl.ds(m + at, LANES), :]], axis=0)
        value_part = jnp.concatenate(
            [values[pl.ds(at, LANES), :], values[pl.ds(m + at, LANES), :]], axis=0
        )
        key_turned = jnp.transpose(key_part.astype(f32)).astype(bf16)
        dk = jnp.zeros((2 * LANES, LANES), f32)
        dv = jnp.zeros((2 * LANES, LANES), f32)
        for start in range(0, 2 * n, span):
            some = queries[start : start + span, :]
            some_grads = grads[start : start + span, :]
            probs = jnp.exp(nt(key_part, some))
            grad_scores = (probs * nt(value_part, some_grads)).astype(bf16)
            dv = dv + nn(probs.astype(bf16), some_grads)
            dk = dk + nn(grad_scores, some)
            turned[:, start : start + span] += nn(key_turned, grad_scores)
        dk_ref[pl.ds(at, LANES), :] = jnp.where(low, dk[:LANES], turn(dk[LANES:]))
        dv_ref[pl.ds(at, LANES), :] = jnp.where(low, dv[:LANES], turn(dv[LANES:]))

    share.relay()
    sent_kv[:, 0] = dk_ref[...].reshape(frames, half, LANES).astype(bf16)
    sent_kv[:, 1] = dv_ref[...].reshape(frames, half, LANES).astype(bf16)

    def back_kv(offset):
        target = lax.rem(frame + offset, frames)
        return remote(
            sent_kv.at[target], back_ref.at[frame, pl.ds(1, 2)], b_send.at[offset], b_recv.at[offset], (scene, target)
        )

    @pl.loop(1, frames)
    def _(offset):
        back_kv(offset).start()

    scale = base ** (-0.5)
    rows = []
    for at in range(0, n, LANES):
        first = jnp.transpose(turned[:, at : at + LANES])
        second = jnp.transpose(turned[:, n + at : n + at + LANES])
        rows.append(jnp.where(low, first, turn(second)) * scale)
    sent_q[...] = jnp.concatenate(rows, axis=0).reshape(heads, half, LANES).astype(bf16)

    def back_q(offset):
        target = lax.rem(place + offset, heads)
        return remote(
            sent_q.at[target], back_ref.at[frame, 0], c_send.at[offset], c_recv.at[offset], (scene, part * heads + target)
        )

    back_ref[frame, 1] = sent_kv[frame, 0]
    back_ref[frame, 2] = sent_kv[frame, 1]

    @pl.loop(1, heads)
    def _(offset):
        back_q(offset).start()

    back_ref[frame, 0] = sent_q[place]

    @pl.loop(1, heads)
    def _(offset):
        to_head(offset).wait_send()

    @pl.loop(1, frames)
    def _(offset):
        back_kv(offset).wait()

    @pl.loop(1, heads)
    def _(offset):
        back_q(offset).wait()

    share.close()


def scene_backward(frames, meta, kept, grad, out, log, half, pairs):
    heads = grad.shape[0]
    n = heads * half
    m = frames * half
    span = n // 2
    while span > 640:
        span = span // 2
    flat = [value for pair in pairs for value in pair]
    results = pl.pallas_call(
        partial(scene_back_body, frames, half, span, len(pairs)),
        name="scene_backward",
        out_shape=[sds((frames, 3, half, LANES), bf16)] + [sds((3,) + own.shape, bf16) for own, _ in pairs],
        grid_spec=pltpu.PrefetchScalarGridSpec(
            num_scalar_prefetch=1,
            grid=(1,),
            in_specs=[vmem_space] * 4 + [any_space] * len(flat),
            out_specs=[vmem_space] + [any_space] * len(pairs),
            scratch_shapes=[
                pltpu.VMEM((2 * n, LANES), bf16),
                pltpu.VMEM((2 * m, LANES), bf16),
                pltpu.VMEM((2 * m, LANES), bf16),
                pltpu.VMEM((2 * n, LANES), bf16),
                pltpu.VMEM((LANES, 2 * n), f32),
                pltpu.VMEM((heads, half, LANES), bf16),
                pltpu.VMEM((m, LANES), f32),
                pltpu.VMEM((m, LANES), f32),
                pltpu.VMEM((heads, half, LANES), bf16),
                pltpu.VMEM((frames, 2, half, LANES), bf16),
                dma((heads,)),
                dma((heads,)),
                dma((frames,)),
                dma((frames,)),
                dma((heads,)),
                dma((heads,)),
                dma((3 * len(pairs),)),
                dma((3 * len(pairs),)),
            ],
        ),
        compiler_params=pltpu.CompilerParams(collective_id=2, has_side_effects=True),
        cost_estimate=pl.CostEstimate(flops=40 * n * m * LANES, bytes_accessed=30 * n * LANES, transcendentals=0),
    )(meta, kept, grad, out, log, *flat)
    back = results[0]
    if frames > heads:
        place = lax.axis_index("frame") // heads * heads
        dq = lax.dynamic_slice(back, (place, 0, 0, 0), (heads, 1, half, LANES))
        both = back.reshape(frames // heads, heads, 3, half, LANES)[:, :, 1:].astype(f32).sum(0)
        back = jnp.concatenate([dq, both.astype(bf16)], axis=1)
    return back, results[1:]


def feed_body(
    block, packed, meta, att_ref, x_ref, mixer_ref, mixer_bias, mixer_scale, gain_ref, shift_ref,
    inner_ref, inner_bias, outer_ref, outer_bias, outer_scale,
    own_ref, other_ref, middle_ref, branch_ref, feed_ref, slope_ref, out_ref, normed_ref, total_ref
):
    step = pl.program_id(0)
    steps = pl.num_programs(0)
    rows, width = middle_ref.shape
    hidden_half = own_ref.shape[1] - width
    half_steps = hidden_half // CHUNK
    mine = meta[0]

    def split(value, at):
        first, second = value[:, : width // 2], value[:, width // 2 :]

        @pl.when(mine == 0)
        def _():
            own_ref[:, at : at + width // 2] = first
            other_ref[:, at : at + width // 2] = second

        @pl.when(mine != 0)
        def _():
            own_ref[:, at : at + width // 2] = second
            other_ref[:, at : at + width // 2] = first

    @pl.when(step == 0)
    def _():
        if packed:
            pieces = []
            for pair in range(width // LANES):
                pieces.append(
                    unpack_pair(att_ref[2 * pair].astype(f32), att_ref[2 * pair + 1].astype(f32))
                )
            attended = jnp.concatenate(pieces, axis=1).astype(bf16)
        else:
            attended = att_ref[...]
        branch = nn(attended, mixer_ref[0]) + row(mixer_bias, block)
        middle = x_ref[...].astype(f32) + row(mixer_scale, block) * branch
        hat, _ = center_norm(middle, norm_eps)
        normed = (hat * row(gain_ref, block) + row(shift_ref, block)).astype(bf16)
        branch_ref[...] = branch
        middle_ref[...] = middle
        normed_ref[...] = normed
        split(normed, hidden_half)
        split(attended, hidden_half + width // 2)
        total_ref[...] = jnp.zeros_like(total_ref)

    pre = nn(normed_ref[...], inner_ref[0]) + row(inner_bias, block)
    share = 0.5 * (1.0 + erf(pre * (2.0 ** (-0.5))))
    slope_ref[...] = share + pre * jnp.exp(-0.5 * pre * pre) * 0.3989422804014327
    hidden = (pre * share).astype(bf16)
    place = pl.multiple_of(lax.rem(step, half_steps) * CHUNK, CHUNK)

    @pl.when(step // half_steps == mine)
    def _():
        own_ref[:, pl.ds(place, CHUNK)] = hidden

    @pl.when(step // half_steps != mine)
    def _():
        other_ref[:, pl.ds(place, CHUNK)] = hidden

    total_ref[...] += nn(hidden, outer_ref[0])

    @pl.when(step == steps - 1)
    def _():
        feed = total_ref[...] + row(outer_bias, block)
        feed_ref[...] = feed
        result = middle_ref[...] + row(outer_scale, block) * feed
        if packed:
            place = lax.broadcasted_iota(jnp.int32, result.shape, 0)
            result = jnp.where(place < meta[3] + SPECIAL, result, 0.0)
        out_ref[...] = result.astype(out_ref.dtype)


def feed_forward(block, packed, meta, att, x, mixer, mixer_bias, mixer_scale, gain, shift, inner, inner_bias, outer, outer_bias, outer_scale):
    rows, width = x.shape
    hidden = inner.shape[2]
    kept = hidden // 2 + width
    steps = hidden // CHUNK
    vector = full(gain.shape)
    return call(
        partial(feed_body, block, packed),
        f"feed_forward_{block}",
        (steps,),
        [
            full(att.shape),
            full((rows, width)),
            pl.BlockSpec((1, width, width), lambda j, m: (block, 0, 0)),
            vector, vector, vector, vector,
            pl.BlockSpec((1, width, CHUNK), lambda j, m: (block, 0, j)),
            pl.BlockSpec((2, CHUNK), lambda j, m: (0, j)),
            pl.BlockSpec((1, CHUNK, width), lambda j, m: (block, j, 0)),
            vector, vector,
        ],
        [full((rows, kept))] * 2
        + [full((rows, width))] * 3
        + [pl.BlockSpec((rows, CHUNK), lambda j, m: (0, j)), full((rows, width))],
        [sds((rows, kept), bf16)] * 2
        + [sds((rows, width), f32)] * 3
        + [sds((rows, hidden), f32), sds((rows, width), bf16 if packed else f32)],
        [pltpu.VMEM((rows, width), bf16), pltpu.VMEM((rows, width), f32)],
        2 * rows * width * (2 * hidden + width),
        4 * width * hidden + 4 * rows * hidden + 30 * rows * width,
    )(meta, att, x, mixer, mixer_bias, mixer_scale, gain, shift, inner, inner_bias, outer, outer_bias, outer_scale)


def feed_back_body(
    block, packed, meta, g_ref, feed_ref, slope_ref, middle_ref, branch_ref,
    outer_scale, gain_ref, mixer_scale, outer_ref, inner_ref, mixer_ref,
    grads_ref, g_middle_ref, g_att_ref, vector_ref, g_feed_ref, total_ref, *kept
):
    step = pl.program_id(0)
    steps = pl.num_programs(0)
    rows, width = middle_ref.shape
    half_steps = steps // 2

    def incoming():
        g = g_ref[...].astype(f32)
        if packed:
            place = lax.broadcasted_iota(jnp.int32, g.shape, 0)
            g = jnp.where(place < meta[3] + SPECIAL, g, 0.0)
        return g

    @pl.when(step == 0)
    def _():
        g = incoming()
        g_feed = (g * row(outer_scale, block)).astype(bf16)
        g_feed_ref[...] = g_feed
        grads_ref[0, :, : width // 2] = g_feed[:, : width // 2]
        grads_ref[1, :, : width // 2] = g_feed[:, width // 2 :]
        vector_ref[0:1, :] = col_sum(g * feed_ref[...])
        vector_ref[1:2, :] = col_sum(g_feed.astype(f32))
        total_ref[...] = jnp.zeros_like(total_ref)

    g_pre = (nt(g_feed_ref[...], outer_ref[0]) * slope_ref[...]).astype(bf16)
    grads_ref[step // half_steps, :, pl.ds(pl.multiple_of(width + lax.rem(step, half_steps) * CHUNK, CHUNK), CHUNK)] = g_pre
    per_row = width // CHUNK
    vector_ref[pl.ds(6 + step // per_row, 1), pl.ds(pl.multiple_of(lax.rem(step, per_row) * CHUNK, CHUNK), CHUNK)] = col_sum(g_pre.astype(f32))
    total_ref[...] += nt(g_pre, inner_ref[0])

    @pl.when(step == steps - 1)
    def _():
        hat, spread = center_norm(middle_ref[...], norm_eps)
        g_nm = total_ref[...]
        vector_ref[2:3, :] = col_sum(g_nm * hat)
        vector_ref[3:4, :] = col_sum(g_nm)
        g_middle = incoming() + norm_back(g_nm * row(gain_ref, block), hat, spread)
        g_middle_ref[...] = g_middle
        vector_ref[4:5, :] = col_sum(g_middle * branch_ref[...])
        g_branch = (g_middle * row(mixer_scale, block)).astype(bf16)
        vector_ref[5:6, :] = col_sum(g_branch.astype(f32))
        grads_ref[0, :, width // 2 : width] = g_branch[:, : width // 2]
        grads_ref[1, :, width // 2 : width] = g_branch[:, width // 2 :]
        g_att = nt(g_branch, mixer_ref[0])
        if packed:
            for pair in range(width // LANES):
                even, odd = pack_pair(g_att[:, pair * LANES : (pair + 1) * LANES])
                g_att_ref[2 * pair] = even.astype(bf16)
                g_att_ref[2 * pair + 1] = odd.astype(bf16)
        else:
            g_att_ref[...] = g_att.astype(bf16)


def feed_backward(block, packed, heads, meta, g, feed, slope, middle, branch, outer_scale, gain, mixer_scale, outer, inner, mixer):
    rows, width = middle.shape
    hidden = inner.shape[2]
    steps = hidden // CHUNK
    vector = full(gain.shape)
    vector_rows = 6 + hidden // width
    att_shape = (heads, rows // 2, LANES) if packed else (rows, width)
    return call(
        partial(feed_back_body, block, packed),
        f"feed_backward_{block}",
        (steps,),
        [
            full((rows, width)),
            full((rows, width)),
            pl.BlockSpec((rows, CHUNK), lambda j, m: (0, j)),
            full((rows, width)),
            full((rows, width)),
            vector, vector, vector,
            pl.BlockSpec((1, CHUNK, width), lambda j, m: (block, j, 0)),
            pl.BlockSpec((1, width, CHUNK), lambda j, m: (block, 0, j)),
            pl.BlockSpec((1, width, width), lambda j, m: (block, 0, 0)),
        ],
        [
            full((2, rows, width + hidden // 2)),
            full((rows, width)),
            full(att_shape),
            full((vector_rows, width)),
        ],
        [
            sds((2, rows, width + hidden // 2), bf16),
            sds((rows, width), f32),
            sds(att_shape, bf16),
            sds((vector_rows, width), f32),
        ],
        [pltpu.VMEM((rows, width), bf16), pltpu.VMEM((rows, width), f32)],
        2 * rows * width * (2 * hidden + width),
        4 * width * hidden + 8 * rows * hidden + 20 * rows * width,
    )(meta, g, feed, slope, middle, branch, outer_scale, gain, mixer_scale, outer, inner, mixer)


def joint_back_body(
    block, packed, head, meta, g_ref, pre_ref, x_ref, g_middle_ref, gain_ref, pattern_ref, w_ref,
    grads_ref, out_ref, vector_ref, total_ref
):
    step = pl.program_id(0)
    steps = pl.num_programs(0)
    rows, width = total_ref.shape
    per_part = width // CHUNK
    half_steps = steps // 2

    @pl.when(step == 0)
    def _():
        total_ref[...] = jnp.zeros_like(total_ref)
        vector_ref[...] = jnp.zeros_like(vector_ref)

    if packed:
        pieces = []
        for pair in range(CHUNK // LANES):
            pieces.append(
                unpack_pair(g_ref[2 * pair, 0].astype(f32), g_ref[2 * pair + 1, 0].astype(f32))
            )
        g = jnp.concatenate(pieces, axis=1)
    else:
        g = g_ref[...]
    pattern = pattern_ref[...]

    def finish(g_joined):
        rounded = g_joined.astype(bf16)
        grads_ref[step // half_steps, :, pl.ds(pl.multiple_of(lax.rem(step, half_steps) * CHUNK, CHUNK), CHUNK)] = rounded
        vector_ref[pl.ds(2 + step // per_part, 1), pl.ds(pl.multiple_of(lax.rem(step, per_part) * CHUNK, CHUNK), CHUNK)] = col_sum(rounded.astype(f32))
        total_ref[...] += nt(rounded, w_ref[0])

    def head_back(gain, gain_row, shift_row):
        mean_matrix = seg_matrix(SLAB, head, 1.0 / head)
        pieces = []
        for slab in range(CHUNK // SLAB):
            at = slab * SLAB
            g_now = g[:, at : at + SLAB]
            hat, spread = seg_norm(pre_ref[:, at : at + SLAB], mean_matrix)
            vector_ref[gain_row : gain_row + 1, at : at + SLAB] += col_sum(g_now * hat)
            if shift_row is not None:
                vector_ref[shift_row : shift_row + 1, at : at + SLAB] += col_sum(g_now)
            grad_hat = g_now * gain
            pieces.append(
                spread
                * (
                    grad_hat
                    - seg_dot(grad_hat, mean_matrix)
                    - hat * seg_dot(grad_hat * hat, mean_matrix)
                )
            )
        finish(jnp.concatenate(pieces, axis=1))

    @pl.when(step < per_part)
    def _():
        head_back(pattern[3 * block : 3 * block + 1], 5, 6)

    @pl.when((step >= per_part) & (step < 2 * per_part))
    def _():
        head_back(pattern[3 * block + 2 : 3 * block + 3], 7, None)

    @pl.when(step >= 2 * per_part)
    def _():
        finish(g)

    @pl.when(step == steps - 1)
    def _():
        hat, spread = center_norm(x_ref[...].astype(f32), norm_eps)
        g_normed = total_ref[...]
        vector_ref[0:1, :] = col_sum(g_normed * hat)
        vector_ref[1:2, :] = col_sum(g_normed)
        result = g_middle_ref[...] + norm_back(g_normed * row(gain_ref, block), hat, spread)
        out_ref[...] = result.astype(out_ref.dtype)


def joint_backward(block, packed, head, meta, g, pre, x, g_middle, gain, pattern, weight):
    rows, width = x.shape
    per_part = width // CHUNK
    if packed:
        g_spec = pl.BlockSpec(
            (CHUNK // head, 1, rows // 2, LANES),
            lambda j, m: (lax.rem(j, per_part), j // per_part, 0, 0),
        )
    else:
        g_spec = pl.BlockSpec((rows, CHUNK), lambda j, m: (0, j))
    return call(
        partial(joint_back_body, block, packed, head),
        f"joint_backward_{block}",
        (3 * per_part,),
        [
            g_spec,
            pl.BlockSpec((rows, CHUNK), lambda j, m: (0, jnp.minimum(j, 2 * per_part - 1))),
            full((rows, width)),
            full((rows, width)),
            full(gain.shape),
            full(pattern.shape),
            pl.BlockSpec((1, width, CHUNK), lambda j, m: (block, 0, j)),
        ],
        [full((2, rows, 3 * width // 2)), full((rows, width)), full((8, width))],
        [
            sds((2, rows, 3 * width // 2), bf16),
            sds((rows, width), f32 if packed else bf16),
            sds((8, width), f32),
        ],
        [pltpu.VMEM((rows, width), f32)],
        2 * rows * width * 3 * width,
        6 * width * width + 30 * rows * width,
    )(meta, g, pre, x, g_middle, gain, pattern, weight)


def collect_body(frames, blocks, hidden_half, width, meta, *refs):
    count = 2 + 4
    inputs, refs = refs[: blocks * count], refs[blocks * count :]
    vector_in, refs = refs[0], refs[1:]
    out_ref, vector_out, refs = refs[0], refs[1], refs[2:]
    own, came, acts, hids, parts, last, sums, refs = (
        refs[0], refs[1], refs[2], refs[3], refs[4], refs[5], refs[6], refs[7:]
    )
    stages = len(refs) - 9
    steps, refs = refs[:stages], refs[stages:]
    load_sem, g_send, g_recv, p_send, p_recv, f_send, f_recv, v_send, v_recv = refs
    rows = own.shape[2]
    chips = frames // 2
    n_outer = 4
    n_inner = hidden_half // CHUNK
    n_joint = 3 * (width // 2) // CHUNK
    per_block = n_outer + n_inner + 1 + n_joint
    n_pieces = 1 + n_inner + 1 + n_joint
    total = blocks * per_block
    half = width // 2
    core, core_peer, scene_peer, cross_peer, bits = peers_of(frames)

    loads = []

    def load(source, target):
        copy = pltpu.make_async_copy(source, target, load_sem.at[len(loads)])
        copy.start()
        loads.append(copy)

    for block in range(blocks):
        feed_g, joint_g = inputs[block * count], inputs[block * count + 1]
        pre_lanes = hidden_half
        load(feed_g.at[:, :, pl.ds(0, half)], own.at[block, :, :, pl.ds(0, half)])
        load(feed_g.at[:, :, pl.ds(width, pre_lanes)], own.at[block, :, :, pl.ds(half, pre_lanes)])
        load(feed_g.at[:, :, pl.ds(half, half)], own.at[block, :, :, pl.ds(half + pre_lanes, half)])
        load(joint_g, own.at[block, :, :, pl.ds(width + pre_lanes, 3 * half)])
    first_loads = len(loads)
    for block in range(blocks):
        for place in range(4):
            feed_x, joint_x = inputs[block * count + 2], inputs[block * count + 4]
            if place:
                feed_x = inputs[block * count + 3].at[place - 1]
                joint_x = inputs[block * count + 5].at[place - 1]
            load(feed_x.at[:, pl.ds(0, hidden_half)], hids.at[block, place])
            load(feed_x.at[:, pl.ds(hidden_half, width)], acts.at[block, place, :, pl.ds(0, width)])
            load(joint_x, acts.at[block, place, :, pl.ds(width, half)])

    enter([core_peer, scene_peer, cross_peer] + [peer for _, peer in bits])
    for copy in loads[:first_loads]:
        copy.wait()

    def piece_copy(block, piece, which):
        lanes = pl.ds(pl.multiple_of(piece * CHUNK, CHUNK), CHUNK)
        target = (scene_peer, core_peer, cross_peer)[which]
        side = core if which == 0 else 1 - core
        return pltpu.make_async_remote_copy(
            src_ref=own.at[block, side, :, lanes],
            dst_ref=came.at[block, which, :, lanes],
            send_sem=g_send.at[block, which, piece],
            recv_sem=g_recv.at[block, which, piece],
            device_id=target,
            device_id_type=MESH,
        )

    ahead = 3

    def start_pieces(index):
        block = index // per_block
        unit = lax.rem(index, per_block)

        @pl.when((index < total) & ((unit == 0) | (unit >= n_outer)))
        def _():
            piece = jnp.where(unit == 0, 0, unit - (n_outer - 1))
            for which in range(3):
                piece_copy(block, piece, which).start()

    @pl.loop(0, ahead)
    def _(index):
        start_pieces(index)

    for copy in loads[first_loads:]:
        copy.wait()

    vector_peers = [core_peer, scene_peer] + [peer for _, peer in bits]
    sums[0] = vector_in[...]

    def vector_copy(stage):
        return pltpu.make_async_remote_copy(
            src_ref=sums.at[2 * stage],
            dst_ref=sums.at[2 * stage + 1],
            send_sem=v_send.at[stage],
            recv_sem=v_recv.at[stage],
            device_id=vector_peers[stage],
            device_id_type=MESH,
        )

    def vector_step(stage):
        vector_copy(stage).wait()
        result = sums[2 * stage] + sums[2 * stage + 1]
        if stage + 1 < len(vector_peers):
            sums[2 * stage + 2] = result
        else:
            vector_out[...] = result

    def stage_pieces(stage, index):
        value, peer = bits[stage]
        source = parts if stage == 0 else steps[stage - 1]
        for pair in range(chips >> (stage + 1)):
            yield pltpu.make_async_remote_copy(
                src_ref=source.at[index, 2 * pair + 1 - value],
                dst_ref=steps[stage].at[index, pair],
                send_sem=p_send.at[stage, index],
                recv_sem=p_recv.at[stage, index],
                device_id=peer,
                device_id_type=MESH,
            )

    def stage_start(stage, index):
        for copy in stage_pieces(stage, index):
            copy.start()

    def stage_whole(stage, index):
        return pltpu.make_async_remote_copy(
            src_ref=steps[stage].at[index],
            dst_ref=steps[stage].at[index],
            send_sem=p_send.at[stage, index],
            recv_sem=p_recv.at[stage, index],
            device_id=bits[stage][1],
            device_id_type=MESH,
        )

    def last_copy(index):
        return pltpu.make_async_remote_copy(
            src_ref=steps[stages - 1].at[index, 0, 1 - core],
            dst_ref=last.at[index],
            send_sem=f_send.at[index],
            recv_sem=f_recv.at[index],
            device_id=core_peer,
            device_id_type=MESH,
        )

    def multiply(index):
        block = index // per_block
        unit = lax.rem(index, per_block)

        def wait_piece(piece):
            for which in range(3):
                piece_copy(block, piece, which).wait_recv()

        def gathered(lanes):
            return jnp.concatenate(
                [own[block, core, :, lanes]] + [came[block, which, :, lanes] for which in range(3)], axis=0
            )

        @pl.when(unit < n_outer)
        def _():
            @pl.when(unit == 0)
            def _():
                wait_piece(0)

            left = jnp.concatenate([hids[block, place] for place in range(4)], axis=0)
            right = gathered(pl.ds(pl.multiple_of(unit * LANES, LANES), LANES))
            value = tn(left, right)
            deep = hidden_half // chips // 8
            value = value.reshape(chips, 2, 4, deep, LANES)
            value = jnp.concatenate([value[:, :, turn] for turn in range(4)], axis=-1)
            parts[index] = value.astype(bf16)

        @pl.when(unit >= n_outer)
        def _():
            piece = unit - (n_outer - 1)
            wait_piece(piece)
            place = jnp.where(unit >= n_outer + n_inner, 1, 0) + jnp.where(unit >= n_outer + n_inner + 1, 1, 0)
            lanes = pl.ds(pl.multiple_of(place * half, half), half)
            left = jnp.concatenate([acts[block, source, :, lanes] for source in range(4)], axis=0)
            value = tn(left, gathered(pl.ds(pl.multiple_of(piece * CHUNK, CHUNK), CHUNK)))
            parts[index] = value.reshape(chips, 2, half // chips // 2, CHUNK).astype(bf16)

    def add(stage, index):
        stage_whole(stage, index).wait_recv()
        value = bits[stage][0]
        source = parts if stage == 0 else steps[stage - 1]
        for pair in range(chips >> (stage + 1)):
            held = source[index, 2 * pair + value].astype(f32) + steps[stage][index, pair].astype(f32)
            if stage + 1 == stages:
                out_ref[index, core] = jnp.where(core == 0, held[0], held[1])
            steps[stage][index, pair] = held.astype(bf16)

    def close(index):
        last_copy(index).wait_recv()
        out_ref[index, 1 - core] = last[index].astype(f32)

    n_vector = len(vector_peers)
    vector_copy(0).start()
    lags = [2 + 2 * stage for stage in range(stages)]
    ends = lags[-1] + 2

    @pl.loop(0, total + ends)
    def _(turn_at):
        @pl.when(turn_at < total)
        def _():
            multiply(turn_at)

        for stage in range(stages):
            index = turn_at - lags[stage]

            @pl.when((index >= 0) & (index < total))
            def _():
                add(stage, index)

        for stage in range(n_vector):

            @pl.when(turn_at == 2 * stage + 1)
            def _():
                vector_step(stage)

        index_last = turn_at - ends

        @pl.when((index_last >= 0) & (index_last < total))
        def _():
            close(index_last)

        for stage in range(stages):
            index = turn_at - lags[stage]

            @pl.when((index >= 0) & (index < total))
            def _():
                if stage + 1 < stages:
                    stage_start(stage + 1, index)
                else:
                    last_copy(index).start()

        for stage in range(1, n_vector):

            @pl.when(turn_at == 2 * stage - 1)
            def _():
                vector_copy(stage).start()

        @pl.when(turn_at < total)
        def _():
            stage_start(0, turn_at)

        start_pieces(turn_at + ahead)

    @pl.loop(0, total)
    def _(index):
        for stage in range(stages):
            stage_whole(stage, index).wait_send()
        last_copy(index).wait_send()

    for block in range(blocks):

        @pl.loop(0, n_pieces)
        def _(piece):
            for which in range(3):
                piece_copy(block, piece, which).wait_send()


def collect(frames, meta, groups, vector):
    blocks = len(groups)
    flat = []
    for group in groups:
        flat += group
    rows = flat[0].shape[1]
    half = flat[1].shape[2] // 3
    width = 2 * half
    hidden_half = flat[0].shape[2] - width
    chips = frames // 2
    stages = chips.bit_length() - 1
    n_inner = hidden_half // CHUNK
    n_joint = 3 * half // CHUNK
    per_block = 4 + n_inner + 1 + n_joint
    n_pieces = 2 + n_inner + n_joint
    total = blocks * per_block
    deep = half // chips // 2
    n_vector = 2 + stages
    moved = 12 * total * chips * deep * CHUNK
    return pl.pallas_call(
        partial(collect_body, frames, blocks, hidden_half, width),
        name="collect",
        out_shape=[sds((total, 2, deep, CHUNK), f32), sds(vector.shape, f32)],
        grid_spec=pltpu.PrefetchScalarGridSpec(
            num_scalar_prefetch=1,
            grid=(1,),
            in_specs=[any_space] * len(flat) + [full(vector.shape)],
            out_specs=[full((total, 2, deep, CHUNK)), full(vector.shape)],
            scratch_shapes=[
                pltpu.VMEM((blocks, 2, rows, n_pieces * CHUNK), bf16),
                pltpu.VMEM((blocks, 3, rows, n_pieces * CHUNK), bf16),
                pltpu.VMEM((blocks, 4, rows, 3 * half), bf16),
                pltpu.VMEM((blocks, 4, rows, hidden_half), bf16),
                pltpu.VMEM((total, chips, 2, deep, CHUNK), bf16),
                pltpu.VMEM((total, deep, CHUNK), bf16),
                pltpu.VMEM((2 * n_vector,) + vector.shape, f32),
            ]
            + [pltpu.VMEM((total, chips >> (stage + 1), 2, deep, CHUNK), bf16) for stage in range(stages)]
            + [
                dma((blocks * 16,)),
                dma((blocks, 3, n_pieces)),
                dma((blocks, 3, n_pieces)),
                dma((stages, total)),
                dma((stages, total)),
                dma((total,)),
                dma((total,)),
                dma((n_vector,)),
                dma((n_vector,)),
            ],
        ),
        compiler_params=pltpu.CompilerParams(
            collective_id=0, has_side_effects=True, vmem_limit_bytes=64 * 1024 * 1024 - 65536
        ),
        cost_estimate=pl.CostEstimate(flops=2 * 4 * rows * total * chips * 2 * deep * CHUNK, bytes_accessed=moved, transcendentals=0),
    )(meta, *flat, vector)


def local(scenes, frames, tokens, patch_counts, first_gain, first_shift, joint_weight, joint_bias, query_gain, query_shift, key_gain, mixer_weight, mixer_bias, mixer_scale, second_gain, second_shift, inner_weight, inner_bias, outer_weight, outer_bias, outer_scale, cotangent):
    rows, width = tokens.shape[1:]
    half = rows // 2
    head = query_gain.shape[1]
    heads = width // head
    hidden = inner_weight.shape[2]
    chips = frames // 2
    scene = lax.axis_index("scene")
    frame = lax.axis_index("frame")
    core = lax.rem(frame, 2)
    meta = jnp.stack([scene, core, lax.rem(frame // 2, 2), patch_counts[0, 0]]).astype(jnp.int32)
    pattern = jnp.tile(
        jnp.stack([vector[block] for block in range(2) for vector in (query_gain, query_shift, key_gain)]).astype(f32),
        (1, SLAB // head),
    )

    x0 = tokens[0]
    feed_params = (mixer_weight, mixer_bias, mixer_scale, second_gain, second_shift, inner_weight, inner_bias, outer_weight, outer_bias, outer_scale)
    back_params = (outer_scale, second_gain, mixer_scale, outer_weight, inner_weight, mixer_weight)

    own0, other0, pre0, qkv0 = joint_forward(0, False, head, meta, x0, first_gain, first_shift, pattern, joint_weight, joint_bias)
    att0 = frame_forward(meta, qkv0)
    own_feed0, other_feed0, middle0, branch0, feed0, slope0, x1 = feed_forward(0, False, meta, att0, x0, *feed_params)
    own1, other1, pre1, pack1 = joint_forward(1, True, head, meta, x1, first_gain, first_shift, pattern, joint_weight, joint_bias)
    att1, kept1, att_full, att_log, (left_joint0, left_feed0, left_joint1) = scene_forward(
        frames, meta, pack1, half, [(own0, other0), (own_feed0, other_feed0), (own1, other1)]
    )
    own_feed1, other_feed1, middle1, branch1, feed1, slope1, layer_out = feed_forward(1, True, meta, att1, x1, *feed_params)

    g_feed1, g_middle1, g_att1, vector_feed1 = feed_backward(1, True, heads, meta, cotangent[0], feed1, slope1, middle1, branch1, *back_params)
    g_qkv1, (left_feed1,) = scene_backward(frames, meta, kept1, g_att1, att_full, att_log, half, [(own_feed1, other_feed1)])
    g_joint1, g1, vector_joint1 = joint_backward(1, True, head, meta, g_qkv1, pre1, x1, g_middle1, first_gain, pattern, joint_weight)

    g_feed0, g_middle0, g_att0, vector_feed0 = feed_backward(0, False, heads, meta, g1, feed0, slope0, middle0, branch0, *back_params)
    g_qkv0 = frame_backward(meta, qkv0, g_att0)
    g_joint0, g0, vector_joint0 = joint_backward(0, False, head, meta, g_qkv0, pre0, x0, g_middle0, first_gain, pattern, joint_weight)

    vectors = jnp.concatenate([vector_feed0, vector_joint0, vector_feed1, vector_joint1], axis=0)
    pieces, vectors = collect(
        frames,
        meta,
        [
            (g_feed1, g_joint1, own_feed1, left_feed1, own1, left_joint1),
            (g_feed0, g_joint0, own_feed0, left_feed0, own0, left_joint0),
        ],
        vectors,
    )
    pieces = pieces[:].reshape((2, -1) + pieces.shape[1:])[::-1]
    n_inner = hidden // 2 // CHUNK
    deep = pieces.shape[3]

    def laid_out(first, last):
        some = jnp.transpose(pieces[:, first:last], (0, 3, 2, 1, 4))
        return some.reshape(2, deep, -1)

    outer = pieces[:, :4].reshape(2, 4, 2, deep, 4, LANES)
    outer = jnp.transpose(outer, (0, 4, 3, 2, 1, 5)).reshape(2, 4 * deep, width)
    inner = laid_out(4, 4 + n_inner)
    mixer = laid_out(4 + n_inner, 5 + n_inner)
    joint = laid_out(5 + n_inner, pieces.shape[1])
    vectors = vectors.reshape(2, -1, width)
    at_joint = vector_feed0.shape[0]

    def folded(index):
        return vectors[:, at_joint + index].reshape(2, heads, head).sum(1)

    return (
        layer_out[None],
        g0[None],
        vectors[:, at_joint],
        vectors[:, at_joint + 1],
        joint,
        vectors[:, at_joint + 2 : at_joint + 5].reshape(2, 3 * width),
        folded(5),
        folded(6),
        folded(7),
        mixer,
        vectors[:, 5],
        vectors[:, 4],
        vectors[:, 2],
        vectors[:, 3],
        inner,
        vectors[:, 6:at_joint].reshape(2, hidden),
        outer,
        vectors[:, 1],
        vectors[:, 0],
    )


def solution(mesh):
    tokens_spec = P("scene", "frame", None)
    shard = P(None, ("scene", "frame"), None)
    in_specs = (tokens_spec, P("scene", "frame")) + (P(),) * 17 + (tokens_spec,)
    out_specs = (
        tokens_spec, tokens_spec, P(), P(), shard, P(), P(), P(), P(), shard,
        P(), P(), P(), P(), shard, P(), shard, P(), P(),
    )
    body = partial(local, mesh.shape["scene"], mesh.shape["frame"])
    return jax.shard_map(body, mesh=mesh, in_specs=in_specs, out_specs=out_specs, check_vma=False)
```

profile of v0, /device:TPU:0, one launch (start us, length us, event | category | flops | bytes accessed | tf_op | source)
XLA Modules:
  0.0 424.6 jit_solution(3016517283777684496)
XLA Ops:
  1.3 0.6 pad_add_fusion.meta
  1.9 0.7 fusion.4
  2.6 0.7 fusion.2
  3.4 0.7 tile.10.pattern_ref
  4.1 8.9 %joint_forward_0.1 = (bf16[144,512]{1,0:T(8,128)(2,1)}, bf16[144,512]{1,0:T(8,128)(2,1)}, f32[144,2048]{1,0:T(8,128)}, bf16[144,3072]{1,0:T(8,128)(2,1)}) custom-call(s32[4]{0:T(128)} %pad_add_fusion.meta, bf16[144,1024]{1,0:T(8,128)(2,1)} %bitcast.57, bf16[2,1024]{1,0:T(2,128)(2,1)} %gain_ref.15, bf16[2,1024]{1,0:T(2,128)(2,1)} %shift_ref.6, ...), custom_call_target="tpu_custom_call" | custom-call | flops 905969664 | bytes 8650752 | tf_op jit(solution)/shard_map/joint_forward_0/pallas_call | solution.py:231
  13.0 3.7 frame_forward.1.att_ref
  16.8 16.7 %feed_forward_0.1 = (bf16[144,3072]{1,0:T(8,128)(2,1)}, bf16[144,3072]{1,0:T(8,128)(2,1)}, f32[144,1024]{1,0:T(8,128)}, f32[144,1024]{1,0:T(8,128)}, f32[144,102...) custom-call(s32[4]{0:T(128)} %pad_add_fusion.meta, bf16[144,1024]{1,0:T(8,128)(2,1)} %frame_forward.1.att_ref, ...), custom_call_target="tpu_custom_call" | custom-call | flops 2717908992 | bytes 23560192 | tf_op jit(solution)/shard_map/feed_forward_0/pallas_call | solution.py:851
  33.5 9.6 %joint_forward_1.1 = (bf16[144,512]{1,0:T(8,128)(2,1)}, bf16[144,512]{1,0:T(8,128)(2,1)}, f32[144,2048]{1,0:T(8,128)}, bf16[16,224,128]{2,1,0:T(8,128)(2,1)}) custom-call(s32[4]{0:T(128)} %pad_add_fusion.meta, f32[144,1024]{1,0:T(8,128)} %get-tuple-element.67.x_ref, bf16[2,1024]{1,0:T(2,128)(2,1)} %gain_ref.15, bf16[2,1024]{1,0:T(2,128)(2,1)} %shift_ref.6, ...), custom_call_target="tpu_custom_call" | custom-call | flops 905969664 | bytes 8650752 | tf_op jit(solution)/shard_map/joint_forward_1/pallas_call | solution.py:231
  43.1 46.5 %scene_forward.1 = (bf16[16,72,128]{2,1,0:T(8,128)(2,1)}, bf16[16,224,128]{2,1,0:T(8,128)(2,1)}, f32[1152,128]{1,0:T(8,128)}, f32[1152,128]{1,0:T(8,128)}, bf16[...) custom-call(s32[4]{0:T(128)} %pad_add_fusion.meta, ...), custom_call_target="tpu_custom_call" | custom-call | flops 2717908992 | bytes 2949120 | tf_op jit(solution)/shard_map/scene_forward/pallas_call | solution.py:545
  89.6 16.7 %feed_forward_1.1 = (bf16[144,3072]{1,0:T(8,128)(2,1)}, bf16[144,3072]{1,0:T(8,128)(2,1)}, f32[144,1024]{1,0:T(8,128)}, f32[144,1024]{1,0:T(8,128)}, f32[144,102...) custom-call(s32[4]{0:T(128)} %pad_add_fusion.meta, bf16[16,72,128]{2,1,0:T(8,128)(2,1)} %get-tuple-element.75.att_ref, ...), custom_call_target="tpu_custom_call" | custom-call | flops 2717908992 | bytes 23560192 | tf_op jit(solution)/shard_map/feed_forward_1/pallas_call | solution.py:851
  106.3 16.9 %feed_backward_1.1 = (bf16[2,144,3072]{2,1,0:T(8,128)(2,1)}, f32[144,1024]{1,0:T(8,128)}, bf16[16,72,128]{2,1,0:T(8,128)(2,1)}, f32[10,1024]{1,0:T(8,128)}) custom-call(s32[4]{0:T(128)} %pad_add_fusion.meta, bf16[144,1024]{1,0:T(8,128)(2,1)} %bitcast.60, f32[144,1024]{1,0:T(8,128)} %get-tuple-element.78.feed_ref, f32[144,4096]{1,0:T(8,128)} %get-tuple-element.79.slope_ref, ...), custom_call_target="tpu_custom_call" | custom-call | flops 2717908992 | bytes 24444928 | tf_op jit(solution)/shard_map/feed_backward_1/pallas_call | solution.py:941
  123.2 53.4 %scene_backward.1 = (bf16[16,3,72,128]{3,2,1,0:T(8,128)(2,1)}, bf16[3,144,3072]{2,1,0:T(8,128)(2,1)}) custom-call(s32[4]{0:T(128)} %pad_add_fusion.meta, bf16[16,224,128]{2,1,0:T(8,128)(2,1)} %get-tuple-element.77.kept_ref, bf16[16,72,128]{2,1,0:T(8,128)(2,1)} %get-tuple-element.82.grad_ref, f32[1152,128]{1,0:T(8,128)} %get-tuple-element.83.out_ref, ...), custom_call_target="tpu_custom_call" | custom-call | flops 6794772480 | bytes 4423680 | tf_op jit(solution)/shard_map/scene_backward/pallas_call | solution.py:729
  176.7 11.4 %joint_backward_1.1 = (bf16[2,144,1536]{2,1,0:T(8,128)(2,1)}, f32[144,1024]{1,0:T(8,128)}, f32[8,1024]{1,0:T(8,128)}) custom-call(s32[4]{0:T(128)} %pad_add_fusion.meta, bf16[16,3,72,128]{3,2,1,0:T(8,128)(2,1)} %get-tuple-element.87.g_ref, f32[144,2048]{1,0:T(8,128)} %get-tuple-element.88.pre_ref, f32[144,1024]{1,0:T(8,128)} %get-tuple-element.67.x_ref, ...), custom_call_target="tpu_custom_call" | custom-call | flops 905969664 | bytes 10715136 | tf_op jit(solution)/shard_map/joint_backward_1/pallas_call | solution.py:1059
  188.0 16.8 %feed_backward_0.1 = (bf16[2,144,3072]{2,1,0:T(8,128)(2,1)}, f32[144,1024]{1,0:T(8,128)}, bf16[144,1024]{1,0:T(8,128)(2,1)}, f32[10,1024]{1,0:T(8,128)}) custom-call(s32[4]{0:T(128)} %pad_add_fusion.meta, f32[144,1024]{1,0:T(8,128)} %get-tuple-element.90.g_ref, f32[144,1024]{1,0:T(8,128)} %get-tuple-element.91.feed_ref, ...), custom_call_target="tpu_custom_call" | custom-call | flops 2717908992 | bytes 24444928 | tf_op jit(solution)/shard_map/feed_backward_0/pallas_call | solution.py:941
  204.8 10.2 %frame_backward.1.g_ref = f32[144,3072]{1,0:T(8,128)} custom-call(s32[4]{0:T(128)} %pad_add_fusion.meta, bf16[144,3072]{1,0:T(8,128)(2,1)} %get-tuple-element.66.qkv_ref, bf16[144,1024]{1,0:T(8,128)(2,1)} %get-tuple-element.95.grad_ref), custom_call_target="tpu_custom_call" | custom-call | flops 212336640 | bytes 2949120 | tf_op jit(solution)/shard_map/frame_backward/pallas_call | solution.py:338
  215.0 11.2 %joint_backward_0.1 = (bf16[2,144,1536]{2,1,0:T(8,128)(2,1)}, bf16[144,1024]{1,0:T(8,128)(2,1)}, f32[8,1024]{1,0:T(8,128)}) custom-call(s32[4]{0:T(128)} %pad_add_fusion.meta, f32[144,3072]{1,0:T(8,128)} %frame_backward.1.g_ref, f32[144,2048]{1,0:T(8,128)} %get-tuple-element.96.pre_ref, bf16[144,1024]{1,0:T(8,128)(2,1)} %bitcast.59, ...), custom_call_target="tpu_custom_call" | custom-call | flops 905969664 | bytes 10715136 | tf_op jit(solution)/shard_map/joint_backward_0/pallas_call | solution.py:1059
  226.2 1.5 pad_maximum_fusion.refs_12_
  227.6 173.4 %collect.1 = (f32[24,2,32,512]{3,2,1,0:T(8,128)}, f32[36,1024]{1,0:T(8,128)}) custom-call(s32[4]{0:T(128)} %pad_add_fusion.meta, bf16[2,144,3072]{2,1,0:T(8,128)(2,1)} %get-tuple-element.99.refs_0_, bf16[2,144,1536]{2,1,0:T(8,128)(2,1)} %get-tuple-element.100.refs_1_, bf16[144,3072]{1,0:T(8,128)(2,1)} %get-tuple-element.85.refs_0_.refs_2_, ...), custom_call_target="tpu_custom_call" | custom-call | flops 7247757312 | bytes 37748736 | tf_op jit(solution)/shard_map/collect/pallas_call | solution.py:1361
  401.1 0.9 reshape.111
  402.0 0.6 copy.64
  402.7 0.1 fusion.1
  402.8 0.6 copy.76
  403.4 0.6 copy.65
  404.0 0.6 copy.78
  404.6 0.6 copy.79
  405.2 0.6 copy.80
  405.8 0.6 copy.81
  406.4 0.6 copy.77
  407.0 0.6 copy.82
  407.6 0.6 copy.83
  408.3 0.6 reduce_sum.27
  409.0 0.6 reduce_sum.28
  409.7 0.6 reduce_sum.29
  410.3 1.0 slice.115
  411.3 0.2 copy.52
  411.5 0.9 reshape.115
  412.4 2.1 slice.110
  414.5 1.8 fusion
  416.2 0.1 slice.105
  416.3 0.4 reshape.118
  416.7 0.7 copy.75
  417.4 1.4 reshape.119
  418.8 1.7 copy.63
  420.4 0.2 reverse_bitcast_fusion.1
  420.6 1.5 reshape.113
  422.1 0.1 reverse_bitcast_fusion
  422.2 0.7 copy.53
  422.9 1.7 reshape.116
  (14 shorter events, 0.3 us)
Async XLA Ops:
  215.0 11.2 %copy-start = (f32[10,1024]{1,0:T(8,128)S(1)}, f32[10,1024]{1,0:T(8,128)}, u32[]{:S(2)}) copy-start(f32[10,1024]{1,0:T(8,128)} %get-tuple-element.109) | copy-start | bytes 122884
  215.0 11.2 %copy-start.1 = (f32[10,1024]{1,0:T(8,128)S(1)}, f32[10,1024]{1,0:T(8,128)}, u32[]{:S(2)}) copy-start(f32[10,1024]{1,0:T(8,128)} %get-tuple-element.107) | copy-start | bytes 122884
  215.0 11.2 %copy-start.2 = (f32[8,1024]{1,0:T(8,128)S(1)}, f32[8,1024]{1,0:T(8,128)}, u32[]{:S(2)}) copy-start(f32[8,1024]{1,0:T(8,128)} %get-tuple-element.110) | copy-start | bytes 98308
where the time goes:
time: 426 us; the launch traced here: 425 us
  Pallas kernels  395 us (93%)
  local copies, waits for them, and re-layouts  23.8 us (6%)
    pallas_call x1, Pallas kernels, collect(): pl.pallas_call(partial(collect_body, frames, blocks, hidden_half, width),...  173 us
    pallas_call x1, Pallas kernels, scene_backward(): pl.pallas_call(partial(scene_back_body, frames, half, span, len(pairs)),...  53.4 us
    pallas_call x1, Pallas kernels, scene_forward(): pl.pallas_call(partial(scene_body, frames, half, span, len(pairs)), name=...  46.5 us
    pallas_call x2, Pallas kernels, feed_backward(): call(partial(feed_back_body, block, packed), f'feed_backward_{block}', (s...  33.7 us
    pallas_call x2, Pallas kernels, feed_forward(): call(partial(feed_body, block, packed), f'feed_forward_{block}', (steps,)...  33.4 us
    pallas_call x2, Pallas kernels, joint_backward(): call(partial(joint_back_body, block, packed, head), f'joint_backward_{blo...  22.5 us
    pallas_call x2, Pallas kernels, joint_forward(): call(partial(joint_body, block, packed, head), f'joint_forward_{block}',...  18.6 us
    pallas_call x1, Pallas kernels, frame_backward(): call(frame_back_body, 'frame_backward', (1,), [full(qkv.shape), full(grad...  10.2 us

commit v1 on v0

--- a/solution.py
+++ b/solution.py
@@ -11,6 +11,11 @@
 CHUNK = 512
 LANES = 128
 SLAB = 256
+SHARED_PIECES = 4
+SWAP_EVERY = 4
+AHEAD = 3
+LAG = 3
+VECTOR_LAG = 3
 norm_eps = 1e-06
 head_eps = 1e-05
 closed_score = -10000.0
@@ -303,49 +308,33 @@
     )(meta, qkv)
 
 
-def frame_back_body(meta, qkv_ref, grad_ref, out_ref):
+def frame_back_slab(at, meta, qkv_ref, grad_ref, out_ref):
     rows, width = grad_ref.shape
     bias = open_row(meta, rows)
-    picks = lane_picks()
+    scale = (LANES // 2) ** (-0.5)
+
+    def lanes(part):
+        return pl.ds(pl.multiple_of(part * width + at, LANES), LANES)
+
+    queries = qkv_ref[:, lanes(0)]
+    keys = qkv_ref[:, lanes(1)]
+    values = qkv_ref[:, lanes(2)]
+    grads = grad_ref[:, lanes(0)]
+    found = []
+    for pick in lane_picks():
+        power = jnp.exp(nt(queries * pick, keys) + bias)
+        probs = power / jnp.sum(power, axis=-1, keepdims=True)
+        grad_probs = nt(grads * pick, values)
+        delta = jnp.sum(probs * grad_probs, axis=-1, keepdims=True)
+        grad_scores = (probs * (grad_probs - delta)).astype(bf16)
+        found.append((
+            nn(grad_scores, keys) * scale,
+            tn(grad_scores, queries),
+            tn(probs.astype(bf16), grads),
+        ))
     low = first_lanes(rows)
-    scale = (LANES // 2) ** (-0.5)
-    for slab in range(width // LANES):
-        at = slab * LANES
-        queries = qkv_ref[:, at : at + LANES]
-        keys = qkv_ref[:, width + at : width + at + LANES]
-        values = qkv_ref[:, 2 * width + at : 2 * width + at + LANES]
-        grads = grad_ref[:, at : at + LANES]
-        found = []
-        for pick in picks:
-            power = jnp.exp(nt(queries * pick, keys) + bias)
-            probs = power / jnp.sum(power, axis=-1, keepdims=True)
-            grad_probs = nt(grads * pick, values)
-            delta = jnp.sum(probs * grad_probs, axis=-1, keepdims=True)
-            grad_scores = (probs * (grad_probs - delta)).astype(bf16)
-            found.append((
-                nn(grad_scores, keys) * scale,
-                tn(grad_scores, queries),
-                tn(probs.astype(bf16), grads),
-            ))
-        for part in range(3):
-            out_ref[:, part * width + at : part * width + at + LANES] = jnp.where(
-                low, found[0][part], found[1][part]
-            )
-
-
-def frame_backward(meta, qkv, grad):
-    rows, width = grad.shape
-    return call(
-        frame_back_body,
-        "frame_backward",
-        (1,),
-        [full(qkv.shape), full(grad.shape)],
-        full((rows, 3 * width)),
-        sds((rows, 3 * width), f32),
-        [],
-        10 * rows * rows * width,
-        20 * rows * width,
-    )(meta, qkv, grad)
+    for part in range(3):
+        out_ref[:, lanes(part)] = jnp.where(low, found[0][part], found[1][part])
 
 
 def packed_part(value, part, half):
@@ -588,13 +577,22 @@
     return jnp.where(lane < base + 3, result, jnp.where(lane == base + 3, closed, 0.0))
 
 
-def scene_back_body(frames, half, span, n_share, meta, kept_ref, grad_ref, out_ref, log_ref, *refs):
+def gradient_copies(frames, own, came, send, recv, lanes):
+    core, core_peer, scene_peer, cross_peer, _ = peers_of(frames)
+    targets = ((core, scene_peer), (1 - core, core_peer), (1 - core, cross_peer))
+    return [
+        remote(own.at[side, :, lanes], came.at[which, :, lanes], send.at[which], recv.at[which], peer)
+        for which, (side, peer) in enumerate(targets)
+    ]
+
+
+def scene_back_body(frames, half, span, n_share, shared, meta, kept_ref, grad_ref, out_ref, log_ref, feed_ref, *refs):
     heads = grad_ref.shape[0]
     pairs = [(refs[2 * index], refs[2 * index + 1]) for index in range(n_share)]
     refs = refs[2 * n_share :]
-    back_ref, outs, refs = refs[0], refs[1 : 1 + n_share], refs[1 + n_share :]
+    back_ref, feed_came, outs, refs = refs[0], refs[1], refs[2 : 2 + n_share], refs[2 + n_share :]
     queries, keys, values, grads, turned, came, dk_ref, dv_ref, sent_q, sent_kv = refs[:10]
-    a_send, a_recv, b_send, b_recv, c_send, c_recv, s_send, s_recv = refs[10:]
+    a_send, a_recv, b_send, b_recv, c_send, c_recv, s_send, s_recv, g_send, g_recv = refs[10:]
     n = queries.shape[0] // 2
     m = keys.shape[0] // 2
     scene = lax.axis_index("scene")
@@ -602,6 +600,7 @@
     part = frame // heads
     place = lax.rem(frame, heads)
     share = Share(frames, pairs, outs, s_send, s_recv)
+    feed_copies = gradient_copies(frames, feed_ref, feed_came, g_send, g_recv, pl.ds(0, shared))
     enter_scene(frames)
 
     def to_head(offset):
@@ -615,6 +614,8 @@
         to_head(offset).start()
 
     share.start()
+    for copy in feed_copies:
+        copy.start()
     came[place] = grad_ref[place]
     first = pl.multiple_of(part * heads, heads)
     low_n, low_m = first_lanes(n), first_lanes(m)
@@ -716,9 +717,11 @@
         back_q(offset).wait()
 
     share.close()
-
-
-def scene_backward(frames, meta, kept, grad, out, log, half, pairs):
+    for copy in feed_copies:
+        copy.wait()
+
+
+def scene_backward(frames, meta, kept, grad, out, log, half, pairs, feed_grads, shared):
     heads = grad.shape[0]
     n = heads * half
     m = frames * half
@@ -727,14 +730,15 @@
         span = span // 2
     flat = [value for pair in pairs for value in pair]
     results = pl.pallas_call(
-        partial(scene_back_body, frames, half, span, len(pairs)),
+        partial(scene_back_body, frames, half, span, len(pairs), shared),
         name="scene_backward",
-        out_shape=[sds((frames, 3, half, LANES), bf16)] + [sds((3,) + own.shape, bf16) for own, _ in pairs],
+        out_shape=[sds((frames, 3, half, LANES), bf16), sds((3,) + feed_grads.shape[1:], bf16)]
+        + [sds((3,) + own.shape, bf16) for own, _ in pairs],
         grid_spec=pltpu.PrefetchScalarGridSpec(
             num_scalar_prefetch=1,
             grid=(1,),
-            in_specs=[vmem_space] * 4 + [any_space] * len(flat),
-            out_specs=[vmem_space] + [any_space] * len(pairs),
+            in_specs=[vmem_space] * 4 + [any_space] * (1 + len(flat)),
+            out_specs=[vmem_space] + [any_space] * (1 + len(pairs)),
             scratch_shapes=[
                 pltpu.VMEM((2 * n, LANES), bf16),
                 pltpu.VMEM((2 * m, LANES), bf16),
@@ -754,18 +758,20 @@
                 dma((heads,)),
                 dma((3 * len(pairs),)),
                 dma((3 * len(pairs),)),
+                dma((3,)),
+                dma((3,)),
             ],
         ),
         compiler_params=pltpu.CompilerParams(collective_id=2, has_side_effects=True),
         cost_estimate=pl.CostEstimate(flops=40 * n * m * LANES, bytes_accessed=30 * n * LANES, transcendentals=0),
-    )(meta, kept, grad, out, log, *flat)
+    )(meta, kept, grad, out, log, feed_grads, *flat)
     back = results[0]
     if frames > heads:
         place = lax.axis_index("frame") // heads * heads
         dq = lax.dynamic_slice(back, (place, 0, 0, 0), (heads, 1, half, LANES))
         both = back.reshape(frames // heads, heads, 3, half, LANES)[:, :, 1:].astype(f32).sum(0)
         back = jnp.concatenate([dq, both.astype(bf16)], axis=1)
-    return back, results[1:]
+    return back, results[1], results[2:]
 
 
 def feed_body(
@@ -874,15 +880,14 @@
     )(meta, att, x, mixer, mixer_bias, mixer_scale, gain, shift, inner, inner_bias, outer, outer_bias, outer_scale)
 
 
-def feed_back_body(
-    block, packed, meta, g_ref, feed_ref, slope_ref, middle_ref, branch_ref,
+def feed_back_core(
+    block, packed, step, steps, chunk, meta, g_ref, feed_ref, slope_ref, middle_ref, branch_ref,
     outer_scale, gain_ref, mixer_scale, outer_ref, inner_ref, mixer_ref,
-    grads_ref, g_middle_ref, g_att_ref, vector_ref, g_feed_ref, total_ref, *kept
+    grads_ref, g_middle_ref, g_att_ref, vector_ref, g_feed_ref, total_ref
 ):
-    step = pl.program_id(0)
-    steps = pl.num_programs(0)
-    rows, width = middle_ref.shape
+    rows, width = total_ref.shape
     half_steps = steps // 2
+    at_branch = width // 2 + half_steps * CHUNK
 
     def incoming():
         g = g_ref[...].astype(f32)
@@ -903,9 +908,11 @@
         total_ref[...] = jnp.zeros_like(total_ref)
 
     g_pre = (nt(g_feed_ref[...], outer_ref[0]) * slope_ref[...]).astype(bf16)
-    grads_ref[step // half_steps, :, pl.ds(pl.multiple_of(width + lax.rem(step, half_steps) * CHUNK, CHUNK), CHUNK)] = g_pre
+    place = pl.multiple_of(width // 2 + lax.rem(chunk, half_steps) * CHUNK, CHUNK)
+    grads_ref[chunk // half_steps, :, pl.ds(place, CHUNK)] = g_pre
     per_row = width // CHUNK
-    vector_ref[pl.ds(6 + step // per_row, 1), pl.ds(pl.multiple_of(lax.rem(step, per_row) * CHUNK, CHUNK), CHUNK)] = col_sum(g_pre.astype(f32))
+    lanes = pl.ds(pl.multiple_of(lax.rem(chunk, per_row) * CHUNK, CHUNK), CHUNK)
+    vector_ref[pl.ds(6 + chunk // per_row, 1), lanes] = col_sum(g_pre.astype(f32))
     total_ref[...] += nt(g_pre, inner_ref[0])
 
     @pl.when(step == steps - 1)
@@ -919,8 +926,8 @@
         vector_ref[4:5, :] = col_sum(g_middle * branch_ref[...])
         g_branch = (g_middle * row(mixer_scale, block)).astype(bf16)
         vector_ref[5:6, :] = col_sum(g_branch.astype(f32))
-        grads_ref[0, :, width // 2 : width] = g_branch[:, : width // 2]
-        grads_ref[1, :, width // 2 : width] = g_branch[:, width // 2 :]
+        grads_ref[0, :, at_branch : at_branch + width // 2] = g_branch[:, : width // 2]
+        grads_ref[1, :, at_branch : at_branch + width // 2] = g_branch[:, width // 2 :]
         g_att = nt(g_branch, mixer_ref[0])
         if packed:
             for pair in range(width // LANES):
@@ -929,6 +936,11 @@
                 g_att_ref[2 * pair + 1] = odd.astype(bf16)
         else:
             g_att_ref[...] = g_att.astype(bf16)
+
+
+def feed_back_body(block, packed, meta, *refs):
+    step = pl.program_id(0)
+    feed_back_core(block, packed, step, pl.num_programs(0), step, meta, *refs)
 
 
 def feed_backward(block, packed, heads, meta, g, feed, slope, middle, branch, outer_scale, gain, mixer_scale, outer, inner, mixer):
@@ -971,12 +983,10 @@
     )(meta, g, feed, slope, middle, branch, outer_scale, gain, mixer_scale, outer, inner, mixer)
 
 
-def joint_back_body(
-    block, packed, head, meta, g_ref, pre_ref, x_ref, g_middle_ref, gain_ref, pattern_ref, w_ref,
-    grads_ref, out_ref, vector_ref, total_ref
+def joint_back_core(
+    block, head, step, steps, chunk, g, pre_ref, x_ref, g_middle_ref, gain_ref, pattern_ref, w_ref,
+    grads_ref, at_joined, out_ref, vector_ref, total_ref
 ):
-    step = pl.program_id(0)
-    steps = pl.num_programs(0)
     rows, width = total_ref.shape
     per_part = width // CHUNK
     half_steps = steps // 2
@@ -984,23 +994,15 @@
     @pl.when(step == 0)
     def _():
         total_ref[...] = jnp.zeros_like(total_ref)
-        vector_ref[...] = jnp.zeros_like(vector_ref)
-
-    if packed:
-        pieces = []
-        for pair in range(CHUNK // LANES):
-            pieces.append(
-                unpack_pair(g_ref[2 * pair, 0].astype(f32), g_ref[2 * pair + 1, 0].astype(f32))
-            )
-        g = jnp.concatenate(pieces, axis=1)
-    else:
-        g = g_ref[...]
+
     pattern = pattern_ref[...]
+    in_row = pl.ds(pl.multiple_of(lax.rem(chunk, per_part) * CHUNK, CHUNK), CHUNK)
 
     def finish(g_joined):
         rounded = g_joined.astype(bf16)
-        grads_ref[step // half_steps, :, pl.ds(pl.multiple_of(lax.rem(step, half_steps) * CHUNK, CHUNK), CHUNK)] = rounded
-        vector_ref[pl.ds(2 + step // per_part, 1), pl.ds(pl.multiple_of(lax.rem(step, per_part) * CHUNK, CHUNK), CHUNK)] = col_sum(rounded.astype(f32))
+        place = pl.multiple_of(at_joined + lax.rem(chunk, half_steps) * CHUNK, CHUNK)
+        grads_ref[chunk // half_steps, :, pl.ds(place, CHUNK)] = rounded
+        vector_ref[pl.ds(2 + chunk // per_part, 1), in_row] = col_sum(rounded.astype(f32))
         total_ref[...] += nt(rounded, w_ref[0])
 
     def head_back(gain, gain_row, shift_row):
@@ -1024,15 +1026,15 @@
             )
         finish(jnp.concatenate(pieces, axis=1))
 
-    @pl.when(step < per_part)
+    @pl.when(chunk < per_part)
     def _():
         head_back(pattern[3 * block : 3 * block + 1], 5, 6)
 
-    @pl.when((step >= per_part) & (step < 2 * per_part))
+    @pl.when((chunk >= per_part) & (chunk < 2 * per_part))
     def _():
         head_back(pattern[3 * block + 2 : 3 * block + 3], 7, None)
 
-    @pl.when(step >= 2 * per_part)
+    @pl.when(chunk >= 2 * per_part)
     def _():
         finish(g)
 
@@ -1046,189 +1048,279 @@
         out_ref[...] = result.astype(out_ref.dtype)
 
 
-def joint_backward(block, packed, head, meta, g, pre, x, g_middle, gain, pattern, weight):
-    rows, width = x.shape
-    per_part = width // CHUNK
-    if packed:
-        g_spec = pl.BlockSpec(
-            (CHUNK // head, 1, rows // 2, LANES),
-            lambda j, m: (lax.rem(j, per_part), j // per_part, 0, 0),
+class Rows:
+    def __init__(self, ref, lead, base):
+        self.ref, self.lead, self.base = ref, lead, base
+
+    def at(self, key):
+        rows, lanes = key
+        if isinstance(rows, slice):
+            rows = slice(rows.start + self.base, rows.stop + self.base)
+        else:
+            rows = pl.ds(rows.start + self.base, rows.size)
+        return self.lead, rows, lanes
+
+    def __getitem__(self, key):
+        return self.ref[self.at(key)]
+
+    def __setitem__(self, key, value):
+        self.ref[self.at(key)] = value
+
+
+class Plan:
+    def __init__(self, frames, rows, width, hidden):
+        self.half = width // 2
+        self.hidden_half = hidden // 2
+        self.chips = frames // 2
+        self.stages = self.chips.bit_length() - 1
+        self.deep = self.half // self.chips // 2
+        self.n_outer = CHUNK // LANES
+        self.n_inner = self.hidden_half // CHUNK
+        self.n_joint = 3 * self.half // CHUNK
+        self.per_block = self.n_outer + self.n_inner + 1 + self.n_joint
+        self.n_pieces = self.n_inner + self.n_joint + 2
+        self.total = 2 * self.per_block
+        self.joint_steps = 2 * self.n_joint
+        self.feed_steps = 2 * self.n_inner
+        self.slabs = 4
+        self.frame_steps = width // LANES // self.slabs
+        self.feed_at = self.joint_steps
+        self.frame_at = self.feed_at + self.feed_steps
+        self.joint_at = self.frame_at + self.frame_steps
+        self.compute_end = self.joint_at + self.joint_steps
+        self.leave = []
+        for piece in range(SHARED_PIECES, 1 + self.n_inner + 1):
+            self.leave.append((1 + piece - SHARED_PIECES, 0, piece))
+        at_joined = 2 + self.n_inner
+        for piece in range(self.n_joint):
+            self.leave.append((2 + 2 * piece, 0, at_joined + piece))
+        self.leave.append((self.feed_at + 1, 1, 0))
+        for piece in range(self.n_inner):
+            self.leave.append((self.feed_at + 2 + 2 * piece, 1, 1 + piece))
+        self.leave.append((self.frame_at + 1, 1, 1 + self.n_inner))
+        for piece in range(self.n_joint):
+            self.leave.append((self.joint_at + 2 + 2 * piece, 1, at_joined + piece))
+        first = 1
+        for slot, block, piece in self.leave:
+            unit = 0 if piece == 0 else piece + self.n_outer - 1
+            first = max(first, slot + AHEAD - block * self.per_block - unit)
+        self.first = first
+        self.ring = 12
+        self.lags = [LAG * (stage + 1) for stage in range(self.stages)]
+        self.end_lag = self.lags[-1] + 2
+        self.n_vector = 2 + self.stages
+        self.slots = max(
+            self.first + self.total + self.end_lag, self.compute_end + VECTOR_LAG * self.n_vector + 1
         )
-    else:
-        g_spec = pl.BlockSpec((rows, CHUNK), lambda j, m: (0, j))
-    return call(
-        partial(joint_back_body, block, packed, head),
-        f"joint_backward_{block}",
-        (3 * per_part,),
-        [
-            g_spec,
-            pl.BlockSpec((rows, CHUNK), lambda j, m: (0, jnp.minimum(j, 2 * per_part - 1))),
-            full((rows, width)),
-            full((rows, width)),
-            full(gain.shape),
-            full(pattern.shape),
-            pl.BlockSpec((1, width, CHUNK), lambda j, m: (block, 0, j)),
-        ],
-        [full((2, rows, 3 * width // 2)), full((rows, width)), full((8, width))],
-        [
-            sds((2, rows, 3 * width // 2), bf16),
-            sds((rows, width), f32 if packed else bf16),
-            sds((8, width), f32),
-        ],
-        [pltpu.VMEM((rows, width), f32)],
-        2 * rows * width * 3 * width,
-        6 * width * width + 30 * rows * width,
-    )(meta, g, pre, x, g_middle, gain, pattern, weight)
-
-
-def collect_body(frames, blocks, hidden_half, width, meta, *refs):
-    count = 2 + 4
-    inputs, refs = refs[: blocks * count], refs[blocks * count :]
-    vector_in, refs = refs[0], refs[1:]
-    out_ref, vector_out, refs = refs[0], refs[1], refs[2:]
-    own, came, acts, hids, parts, last, sums, refs = (
-        refs[0], refs[1], refs[2], refs[3], refs[4], refs[5], refs[6], refs[7:]
-    )
-    stages = len(refs) - 9
-    steps, refs = refs[:stages], refs[stages:]
-    load_sem, g_send, g_recv, p_send, p_recv, f_send, f_recv, v_send, v_recv = refs
+
+
+def rear_body(plan, frames, head, meta, *refs):
+    (
+        back_ref, pre1_ref, x1_ref, g_middle1_ref, gain_ref, pattern_ref, joint_ref,
+        outer_scale, second_gain, mixer_scale, outer_ref, inner_ref, slope_ref, pre0_ref,
+        mixer_in, feed_in, middle_in, branch_in, qkv_in, x0_in,
+        feed_g, came_in, feed_x1, feed_three1, joint_x1, joint_three1, feed_x0, feed_three0, joint_x0, joint_three0,
+        vector_in,
+    ) = refs[:31]
+    tokens_ref, outer_out, inner_out, mixer_out, joint_out, vector_out = refs[31:37]
+    (
+        own, came, acts, hids, act_turned, hid_turned, parts, last, sums,
+        mixer, feed0, middle0, branch0, qkv0, x0,
+        g1, g_middle0, g_att0, g_feed, g_qkv, total_sum,
+    ) = refs[37:58]
+    steps = refs[58 : 58 + plan.stages]
+    load_sem, act_sem, hid_sem, g_send, g_recv, p_send, p_recv, f_send, f_recv, v_send, v_recv = refs[58 + plan.stages :]
+    slot = pl.program_id(0)
     rows = own.shape[2]
-    chips = frames // 2
-    n_outer = 4
-    n_inner = hidden_half // CHUNK
-    n_joint = 3 * (width // 2) // CHUNK
-    per_block = n_outer + n_inner + 1 + n_joint
-    n_pieces = 1 + n_inner + 1 + n_joint
-    total = blocks * per_block
-    half = width // 2
+    half, hidden_half, chips, total = plan.half, plan.hidden_half, plan.chips, plan.total
+    width = 2 * half
+    per_block, n_outer, n_inner = plan.per_block, plan.n_outer, plan.n_inner
+    at_joined = (2 + n_inner) * CHUNK
     core, core_peer, scene_peer, cross_peer, bits = peers_of(frames)
-
-    loads = []
-
-    def load(source, target):
-        copy = pltpu.make_async_copy(source, target, load_sem.at[len(loads)])
-        copy.start()
-        loads.append(copy)
-
-    for block in range(blocks):
-        feed_g, joint_g = inputs[block * count], inputs[block * count + 1]
-        pre_lanes = hidden_half
-        load(feed_g.at[:, :, pl.ds(0, half)], own.at[block, :, :, pl.ds(0, half)])
-        load(feed_g.at[:, :, pl.ds(width, pre_lanes)], own.at[block, :, :, pl.ds(half, pre_lanes)])
-        load(feed_g.at[:, :, pl.ds(half, half)], own.at[block, :, :, pl.ds(half + pre_lanes, half)])
-        load(joint_g, own.at[block, :, :, pl.ds(width + pre_lanes, 3 * half)])
-    first_loads = len(loads)
-    for block in range(blocks):
+    vector_rows = 6 + hidden_half * 2 // width
+    section = vector_rows + 8
+
+    sources = [
+        (feed_g, own.at[0, :, :, pl.ds(0, at_joined)]),
+        (came_in.at[:, :, pl.ds(0, SHARED_PIECES * CHUNK)], came.at[0, :, :, pl.ds(0, SHARED_PIECES * CHUNK)]),
+        (feed_in, feed0),
+        (mixer_in.at[pl.ds(0, 1)], mixer),
+        (middle_in, middle0),
+        (branch_in, branch0),
+        (qkv_in, qkv0),
+        (x0_in, x0),
+    ]
+
+    def load(index):
+        return pltpu.make_async_copy(sources[index][0], sources[index][1], load_sem.at[index])
+
+    def act_loads(block):
+        feed_x, feed_three, joint_x, joint_three = (
+            (feed_x1, feed_three1, joint_x1, joint_three1),
+            (feed_x0, feed_three0, joint_x0, joint_three0),
+        )[block]
+        copies = []
         for place in range(4):
-            feed_x, joint_x = inputs[block * count + 2], inputs[block * count + 4]
-            if place:
-                feed_x = inputs[block * count + 3].at[place - 1]
-                joint_x = inputs[block * count + 5].at[place - 1]
-            load(feed_x.at[:, pl.ds(0, hidden_half)], hids.at[block, place])
-            load(feed_x.at[:, pl.ds(hidden_half, width)], acts.at[block, place, :, pl.ds(0, width)])
-            load(joint_x, acts.at[block, place, :, pl.ds(width, half)])
-
-    enter([core_peer, scene_peer, cross_peer] + [peer for _, peer in bits])
-    for copy in loads[:first_loads]:
-        copy.wait()
+            feed_from = feed_x if place == 0 else feed_three.at[place - 1]
+            joint_from = joint_x if place == 0 else joint_three.at[place - 1]
+            copies.append(pltpu.make_async_copy(
+                feed_from.at[:, pl.ds(hidden_half, width)], acts.at[place, :, pl.ds(0, width)], act_sem.at[2 * place]
+            ))
+            copies.append(pltpu.make_async_copy(
+                joint_from, acts.at[place, :, pl.ds(width, half)], act_sem.at[2 * place + 1]
+            ))
+        return copies
+
+    def hid_loads(block):
+        feed_x, feed_three = ((feed_x1, feed_three1), (feed_x0, feed_three0))[block]
+        return [
+            pltpu.make_async_copy(
+                (feed_x if place == 0 else feed_three.at[place - 1]).at[:, pl.ds(0, hidden_half)],
+                hids.at[place],
+                hid_sem.at[place],
+            )
+            for place in range(4)
+        ]
 
     def piece_copy(block, piece, which):
         lanes = pl.ds(pl.multiple_of(piece * CHUNK, CHUNK), CHUNK)
-        target = (scene_peer, core_peer, cross_peer)[which]
         side = core if which == 0 else 1 - core
-        return pltpu.make_async_remote_copy(
-            src_ref=own.at[block, side, :, lanes],
-            dst_ref=came.at[block, which, :, lanes],
-            send_sem=g_send.at[block, which, piece],
-            recv_sem=g_recv.at[block, which, piece],
-            device_id=target,
-            device_id_type=MESH,
+        return remote(
+            own.at[block, side, :, lanes],
+            came.at[block, which, :, lanes],
+            g_send.at[block, which, piece],
+            g_recv.at[block, which, piece],
+            (scene_peer, core_peer, cross_peer)[which],
         )
 
-    ahead = 3
-
-    def start_pieces(index):
-        block = index // per_block
-        unit = lax.rem(index, per_block)
-
-        @pl.when((index < total) & ((unit == 0) | (unit >= n_outer)))
+    @pl.when(slot == 0)
+    def _():
+        load(0).start()
+        for copy in hid_loads(0):
+            copy.start()
+        load(1).start()
+        for copy in act_loads(0):
+            copy.start()
+        for index in range(2, len(sources)):
+            load(index).start()
+        sums[0] = jnp.zeros(sums.shape[1:], f32)
+        for index in range(vector_rows):
+            sums[0, section + index : section + index + 1, :] = vector_in[index : index + 1, :]
+        enter([core_peer, scene_peer, cross_peer] + [peer for _, peer in bits])
+        load(0).wait()
+        for copy in hid_loads(0):
+            copy.wait()
+        load(1).wait()
+        for copy in act_loads(0):
+            copy.wait()
+
+    def spread(step, steps_of):
+        return lax.rem(step, 2) * (steps_of // 2) + step // 2
+
+    @pl.when(slot < plan.joint_steps)
+    def _():
+        pieces = []
+        for pair in range(CHUNK // LANES):
+            pieces.append(
+                unpack_pair(back_ref[2 * pair, 0].astype(f32), back_ref[2 * pair + 1, 0].astype(f32))
+            )
+        joint_back_core(
+            1, head, slot, plan.joint_steps, spread(slot, plan.joint_steps), jnp.concatenate(pieces, axis=1),
+            pre1_ref, x1_ref, g_middle1_ref, gain_ref, pattern_ref, joint_ref,
+            own.at[0], at_joined, g1, Rows(sums, 0, section + vector_rows), total_sum,
+        )
+
+    @pl.when(slot == plan.feed_at)
+    def _():
+        for index in range(2, len(sources)):
+            load(index).wait()
+
+    @pl.when((slot >= plan.feed_at) & (slot < plan.frame_at))
+    def _():
+        step = slot - plan.feed_at
+        feed_back_core(
+            0, False, step, plan.feed_steps, spread(step, plan.feed_steps), meta, g1, feed0, slope_ref, middle0, branch0,
+            outer_scale, second_gain, mixer_scale, outer_ref, inner_ref, mixer,
+            own.at[1], g_middle0, g_att0, Rows(sums, 0, 0), g_feed, total_sum,
+        )
+
+    @pl.when((slot >= plan.frame_at) & (slot < plan.joint_at))
+    def _():
+        @pl.loop(0, plan.slabs)
+        def _(slab):
+            at = ((slot - plan.frame_at) * plan.slabs + slab) * LANES
+            frame_back_slab(at, meta, qkv0, g_att0, g_qkv)
+
+    @pl.when((slot >= plan.joint_at) & (slot < plan.compute_end))
+    def _():
+        step = slot - plan.joint_at
+        chunk = spread(step, plan.joint_steps)
+        joint_back_core(
+            0, head, step, plan.joint_steps, chunk,
+            g_qkv[:, pl.ds(pl.multiple_of(chunk * CHUNK, CHUNK), CHUNK)],
+            pre0_ref, x0, g_middle0, gain_ref, pattern_ref, joint_ref,
+            own.at[1], at_joined, tokens_ref, Rows(sums, 0, vector_rows), total_sum,
+        )
+
+    def swapped(index):
+        return lax.rem(index, SWAP_EVERY) == 1
+
+    def way(stage, index):
+        value, peer = bits[stage]
+        if stage > 1:
+            return value, peer
+        other_value, other_peer = bits[1 - stage]
+        changed = swapped(index)
+        return jnp.where(changed, other_value, value), (peer[0], jnp.where(changed, other_peer[1], peer[1]))
+
+    def stage_start(stage, index):
+        value, peer = way(stage, index)
+        source = parts if stage == 0 else steps[stage - 1]
+        held = lax.rem(index, plan.ring)
+        for pair in range(chips >> (stage + 1)):
+            remote(
+                source.at[held, 2 * pair + 1 - value],
+                steps[stage].at[held, pair],
+                p_send.at[stage, held],
+                p_recv.at[stage, held],
+                peer,
+            ).start()
+
+    def stage_whole(stage, index):
+        held = lax.rem(index, plan.ring)
+        return remote(
+            steps[stage].at[held], steps[stage].at[held], p_send.at[stage, held], p_recv.at[stage, held], way(stage, index)[1]
+        )
+
+    def last_copy(index):
+        held = lax.rem(index, plan.ring)
+        return remote(
+            steps[-1].at[held, 0, 1 - core], last.at[held], f_send.at[held], f_recv.at[held], core_peer
+        )
+
+    def store(index, value):
+        changed = swapped(index)
+        held = lax.rem(index, plan.ring)
+
+        @pl.when(jnp.logical_not(changed))
         def _():
-            piece = jnp.where(unit == 0, 0, unit - (n_outer - 1))
-            for which in range(3):
-                piece_copy(block, piece, which).start()
-
-    @pl.loop(0, ahead)
-    def _(index):
-        start_pieces(index)
-
-    for copy in loads[first_loads:]:
-        copy.wait()
-
-    vector_peers = [core_peer, scene_peer] + [peer for _, peer in bits]
-    sums[0] = vector_in[...]
-
-    def vector_copy(stage):
-        return pltpu.make_async_remote_copy(
-            src_ref=sums.at[2 * stage],
-            dst_ref=sums.at[2 * stage + 1],
-            send_sem=v_send.at[stage],
-            recv_sem=v_recv.at[stage],
-            device_id=vector_peers[stage],
-            device_id_type=MESH,
-        )
-
-    def vector_step(stage):
-        vector_copy(stage).wait()
-        result = sums[2 * stage] + sums[2 * stage + 1]
-        if stage + 1 < len(vector_peers):
-            sums[2 * stage + 2] = result
-        else:
-            vector_out[...] = result
-
-    def stage_pieces(stage, index):
-        value, peer = bits[stage]
-        source = parts if stage == 0 else steps[stage - 1]
-        for pair in range(chips >> (stage + 1)):
-            yield pltpu.make_async_remote_copy(
-                src_ref=source.at[index, 2 * pair + 1 - value],
-                dst_ref=steps[stage].at[index, pair],
-                send_sem=p_send.at[stage, index],
-                recv_sem=p_recv.at[stage, index],
-                device_id=peer,
-                device_id_type=MESH,
-            )
-
-    def stage_start(stage, index):
-        for copy in stage_pieces(stage, index):
-            copy.start()
-
-    def stage_whole(stage, index):
-        return pltpu.make_async_remote_copy(
-            src_ref=steps[stage].at[index],
-            dst_ref=steps[stage].at[index],
-            send_sem=p_send.at[stage, index],
-            recv_sem=p_recv.at[stage, index],
-            device_id=bits[stage][1],
-            device_id_type=MESH,
-        )
-
-    def last_copy(index):
-        return pltpu.make_async_remote_copy(
-            src_ref=steps[stages - 1].at[index, 0, 1 - core],
-            dst_ref=last.at[index],
-            send_sem=f_send.at[index],
-            recv_sem=f_recv.at[index],
-            device_id=core_peer,
-            device_id_type=MESH,
-        )
+            parts[held] = value.astype(bf16)
+
+        @pl.when(changed)
+        def _():
+            pairs = value.reshape((chips // 4, 2, 2) + value.shape[1:])
+            pairs = jnp.stack([pairs[:, :, place] for place in range(2)], axis=1)
+            parts[held] = pairs.reshape(value.shape).astype(bf16)
 
     def multiply(index):
         block = index // per_block
         unit = lax.rem(index, per_block)
 
         def wait_piece(piece):
-            for which in range(3):
-                piece_copy(block, piece, which).wait_recv()
+            @pl.when((block > 0) | (piece >= SHARED_PIECES))
+            def _():
+                for which in range(3):
+                    piece_copy(block, piece, which).wait_recv()
 
         def gathered(lanes):
             return jnp.concatenate(
@@ -1240,160 +1332,255 @@
             @pl.when(unit == 0)
             def _():
                 wait_piece(0)
-
-            left = jnp.concatenate([hids[block, place] for place in range(4)], axis=0)
+                hid_turned[...] = jnp.transpose(jnp.concatenate([hids[place] for place in range(4)], axis=0))
+
             right = gathered(pl.ds(pl.multiple_of(unit * LANES, LANES), LANES))
-            value = tn(left, right)
-            deep = hidden_half // chips // 8
-            value = value.reshape(chips, 2, 4, deep, LANES)
-            value = jnp.concatenate([value[:, :, turn] for turn in range(4)], axis=-1)
-            parts[index] = value.astype(bf16)
+            value = nn(hid_turned[...], right)
+            value = value.reshape(chips, 2, 4, plan.deep, LANES)
+            store(index, jnp.concatenate([value[:, :, place] for place in range(4)], axis=-1))
 
         @pl.when(unit >= n_outer)
         def _():
             piece = unit - (n_outer - 1)
             wait_piece(piece)
-            place = jnp.where(unit >= n_outer + n_inner, 1, 0) + jnp.where(unit >= n_outer + n_inner + 1, 1, 0)
-            lanes = pl.ds(pl.multiple_of(place * half, half), half)
-            left = jnp.concatenate([acts[block, source, :, lanes] for source in range(4)], axis=0)
-            value = tn(left, gathered(pl.ds(pl.multiple_of(piece * CHUNK, CHUNK), CHUNK)))
-            parts[index] = value.reshape(chips, 2, half // chips // 2, CHUNK).astype(bf16)
+
+            for place, at in enumerate((n_outer, n_outer + n_inner, n_outer + n_inner + 1)):
+
+                @pl.when(unit == at)
+                def _():
+                    left = [acts[source, :, place * half : (place + 1) * half] for source in range(4)]
+                    act_turned[...] = jnp.transpose(jnp.concatenate(left, axis=0))
+
+            value = nn(act_turned[...], gathered(pl.ds(pl.multiple_of(piece * CHUNK, CHUNK), CHUNK)))
+            store(index, value.reshape(chips, 2, plan.deep, CHUNK))
+
+    def put(index, side, value):
+        block = 1 - index // per_block
+        unit = lax.rem(index, per_block)
+
+        @pl.when(unit < n_outer)
+        def _():
+            lanes = pl.ds(pl.multiple_of(side * half + unit * LANES, LANES), LANES)
+            for place in range(4):
+                outer_out[block, place * plan.deep : (place + 1) * plan.deep, lanes] = (
+                    value[:, place * LANES : (place + 1) * LANES]
+                )
+
+        def wide(first, count, target):
+            @pl.when((unit >= first) & (unit < first + count))
+            def _():
+                lanes = pl.ds(pl.multiple_of((side * count + unit - first) * CHUNK, CHUNK), CHUNK)
+                target[block, :, lanes] = value
+
+        wide(n_outer, n_inner, inner_out)
+        wide(n_outer + n_inner, 1, mixer_out)
+        wide(n_outer + n_inner + 1, plan.n_joint, joint_out)
 
     def add(stage, index):
-        stage_whole(stage, index).wait_recv()
-        value = bits[stage][0]
+        stage_whole(stage, index).wait()
+        value = way(stage, index)[0]
+        held = lax.rem(index, plan.ring)
         source = parts if stage == 0 else steps[stage - 1]
         for pair in range(chips >> (stage + 1)):
-            held = source[index, 2 * pair + value].astype(f32) + steps[stage][index, pair].astype(f32)
-            if stage + 1 == stages:
-                out_ref[index, core] = jnp.where(core == 0, held[0], held[1])
-            steps[stage][index, pair] = held.astype(bf16)
+            result = source[held, 2 * pair + value].astype(f32) + steps[stage][held, pair].astype(f32)
+            if stage + 1 == plan.stages:
+                put(index, core, jnp.where(core == 0, result[0], result[1]))
+            steps[stage][held, pair] = result.astype(bf16)
 
     def close(index):
-        last_copy(index).wait_recv()
-        out_ref[index, 1 - core] = last[index].astype(f32)
-
-    n_vector = len(vector_peers)
-    vector_copy(0).start()
-    lags = [2 + 2 * stage for stage in range(stages)]
-    ends = lags[-1] + 2
-
-    @pl.loop(0, total + ends)
-    def _(turn_at):
-        @pl.when(turn_at < total)
+        last_copy(index).wait()
+        put(index, 1 - core, last[lax.rem(index, plan.ring)].astype(f32))
+
+    def when_due(lag, action):
+        index = slot - plan.first - lag
+
+        @pl.when((index >= 0) & (index < total))
         def _():
-            multiply(turn_at)
-
-        for stage in range(stages):
-            index = turn_at - lags[stage]
-
-            @pl.when((index >= 0) & (index < total))
-            def _():
-                add(stage, index)
-
-        for stage in range(n_vector):
-
-            @pl.when(turn_at == 2 * stage + 1)
-            def _():
-                vector_step(stage)
-
-        index_last = turn_at - ends
-
-        @pl.when((index_last >= 0) & (index_last < total))
+            action(index)
+
+    vector_peers = [core_peer, scene_peer] + [peer for _, peer in bits]
+
+    def vector_copy(stage):
+        return remote(
+            sums.at[2 * stage], sums.at[2 * stage + 1], v_send.at[stage], v_recv.at[stage], vector_peers[stage]
+        )
+
+    when_due(0, multiply)
+    for stage in range(plan.stages):
+        when_due(plan.lags[stage], partial(add, stage))
+    when_due(plan.end_lag, close)
+
+    for stage in range(plan.n_vector):
+
+        @pl.when(slot == plan.compute_end + VECTOR_LAG * (stage + 1))
         def _():
-            close(index_last)
-
-        for stage in range(stages):
-            index = turn_at - lags[stage]
-
-            @pl.when((index >= 0) & (index < total))
-            def _():
-                if stage + 1 < stages:
-                    stage_start(stage + 1, index)
-                else:
-                    last_copy(index).start()
-
-        for stage in range(1, n_vector):
-
-            @pl.when(turn_at == 2 * stage - 1)
-            def _():
-                vector_copy(stage).start()
-
-        @pl.when(turn_at < total)
+            vector_copy(stage).wait()
+            result = sums[2 * stage] + sums[2 * stage + 1]
+            if stage + 1 < plan.n_vector:
+                sums[2 * stage + 2] = result
+            else:
+                vector_out[...] = result
+
+    for stage in range(plan.stages - 1):
+        when_due(plan.lags[stage], partial(stage_start, stage + 1))
+    when_due(plan.lags[-1], lambda index: last_copy(index).start())
+    when_due(0, partial(stage_start, 0))
+
+    for at, block, piece in plan.leave:
+
+        @pl.when(slot == at)
         def _():
-            stage_start(0, turn_at)
-
-        start_pieces(turn_at + ahead)
-
-    @pl.loop(0, total)
-    def _(index):
-        for stage in range(stages):
-            stage_whole(stage, index).wait_send()
-        last_copy(index).wait_send()
-
-    for block in range(blocks):
-
-        @pl.loop(0, n_pieces)
-        def _(piece):
+            for which in range(3):
+                piece_copy(block, piece, which).start()
+
+    for stage in range(plan.n_vector):
+
+        @pl.when(slot == plan.compute_end + VECTOR_LAG * stage)
+        def _():
+            vector_copy(stage).start()
+
+    @pl.when(slot == plan.first + 1)
+    def _():
+        for copy in hid_loads(1):
+            copy.start()
+
+    @pl.when(slot == plan.first + per_block - 1)
+    def _():
+        for copy in hid_loads(1):
+            copy.wait()
+
+    @pl.when(slot == plan.first + n_outer + n_inner + 1)
+    def _():
+        for copy in act_loads(1):
+            copy.start()
+
+    @pl.when(slot == plan.first + per_block + n_outer - 1)
+    def _():
+        for copy in act_loads(1):
+            copy.wait()
+
+    @pl.when(slot == plan.slots - 1)
+    def _():
+        for at, block, piece in plan.leave:
             for which in range(3):
                 piece_copy(block, piece, which).wait_send()
 
 
-def collect(frames, meta, groups, vector):
-    blocks = len(groups)
-    flat = []
-    for group in groups:
-        flat += group
-    rows = flat[0].shape[1]
-    half = flat[1].shape[2] // 3
-    width = 2 * half
-    hidden_half = flat[0].shape[2] - width
-    chips = frames // 2
-    stages = chips.bit_length() - 1
-    n_inner = hidden_half // CHUNK
-    n_joint = 3 * half // CHUNK
-    per_block = 4 + n_inner + 1 + n_joint
-    n_pieces = 2 + n_inner + n_joint
-    total = blocks * per_block
-    deep = half // chips // 2
-    n_vector = 2 + stages
-    moved = 12 * total * chips * deep * CHUNK
+def rear(frames, head, meta, back, pre1, x1, g_middle1, gain, pattern, joint, outer_scale, second_gain, mixer_scale, outer, inner, slope0, pre0, mixer, feed0, middle0, branch0, qkv0, x0, feed_g1, came1, shares, vector1):
+    rows, width = x1.shape
+    hidden = inner.shape[2]
+    half = width // 2
+    plan = Plan(frames, rows, width, hidden)
+    per_part = width // CHUNK
+    vector_rows = vector1.shape[0]
+    n_vector_rows = 2 * (vector_rows + 8)
+
+    def clip(value, size):
+        return jnp.minimum(jnp.maximum(value, 0), size - 1)
+
+    def spread(step, steps):
+        return lax.rem(step, 2) * (steps // 2) + step // 2
+
+    def chunk1(slot):
+        return spread(clip(slot, plan.joint_steps), plan.joint_steps)
+
+    def chunk0(slot):
+        return spread(clip(slot - plan.joint_at, plan.joint_steps), plan.joint_steps)
+
+    def chunk_feed(slot):
+        return spread(clip(slot - plan.feed_at, plan.feed_steps), plan.feed_steps)
+
+    def back_map(slot, m):
+        chunk = chunk1(slot)
+        return (lax.rem(chunk, per_part), chunk // per_part, 0, 0)
+
+    def joint_map(slot, m):
+        late = slot >= plan.feed_at
+        return (jnp.where(late, 0, 1), 0, jnp.where(late, chunk0(slot), chunk1(slot)))
+
+    once = dict(pipeline_mode=pl.Buffered(1))
+    single = lambda shape: pl.BlockSpec(shape, lambda *_: (0,) * len(shape), **once)
+    out_shape = [
+        sds((rows, width), bf16),
+        sds((2, 4 * plan.deep, width), f32),
+        sds((2, plan.deep, hidden), f32),
+        sds((2, plan.deep, width), f32),
+        sds((2, plan.deep, 3 * width), f32),
+        sds((n_vector_rows, width), f32),
+    ]
+    container = (plan.ring, plan.chips, 2, plan.deep, CHUNK)
     return pl.pallas_call(
-        partial(collect_body, frames, blocks, hidden_half, width),
-        name="collect",
-        out_shape=[sds((total, 2, deep, CHUNK), f32), sds(vector.shape, f32)],
+        partial(rear_body, plan, frames, head),
+        name="rear",
+        out_shape=out_shape,
         grid_spec=pltpu.PrefetchScalarGridSpec(
             num_scalar_prefetch=1,
-            grid=(1,),
-            in_specs=[any_space] * len(flat) + [full(vector.shape)],
-            out_specs=[full((total, 2, deep, CHUNK)), full(vector.shape)],
+            grid=(plan.slots,),
+            in_specs=[
+                pl.BlockSpec((CHUNK // head, 1, rows // 2, LANES), back_map),
+                pl.BlockSpec((rows, CHUNK), lambda j, m: (0, jnp.minimum(chunk1(j), 2 * per_part - 1))),
+                single(x1.shape),
+                single(g_middle1.shape),
+                single(gain.shape),
+                single(pattern.shape),
+                pl.BlockSpec((1, width, CHUNK), joint_map),
+                single(outer_scale.shape),
+                single(second_gain.shape),
+                single(mixer_scale.shape),
+                pl.BlockSpec((1, CHUNK, width), lambda j, m: (0, chunk_feed(j), 0)),
+                pl.BlockSpec((1, width, CHUNK), lambda j, m: (0, 0, chunk_feed(j))),
+                pl.BlockSpec((rows, CHUNK), lambda j, m: (0, chunk_feed(j))),
+                pl.BlockSpec((rows, CHUNK), lambda j, m: (0, jnp.minimum(chunk0(j), 2 * per_part - 1))),
+            ]
+            + [any_space] * 16
+            + [single(vector1.shape)],
+            out_specs=[vmem_space] * len(out_shape),
             scratch_shapes=[
-                pltpu.VMEM((blocks, 2, rows, n_pieces * CHUNK), bf16),
-                pltpu.VMEM((blocks, 3, rows, n_pieces * CHUNK), bf16),
-                pltpu.VMEM((blocks, 4, rows, 3 * half), bf16),
-                pltpu.VMEM((blocks, 4, rows, hidden_half), bf16),
-                pltpu.VMEM((total, chips, 2, deep, CHUNK), bf16),
-                pltpu.VMEM((total, deep, CHUNK), bf16),
-                pltpu.VMEM((2 * n_vector,) + vector.shape, f32),
+                pltpu.VMEM((2, 2, rows, plan.n_pieces * CHUNK), bf16),
+                pltpu.VMEM((2, 3, rows, plan.n_pieces * CHUNK), bf16),
+                pltpu.VMEM((4, rows, 3 * half), bf16),
+                pltpu.VMEM((4, rows, plan.hidden_half), bf16),
+                pltpu.VMEM((half, 4 * rows), bf16),
+                pltpu.VMEM((plan.hidden_half, 4 * rows), bf16),
+                pltpu.VMEM(container, bf16),
+                pltpu.VMEM((plan.ring, plan.deep, CHUNK), bf16),
+                pltpu.VMEM((2 * plan.n_vector, n_vector_rows, width), f32),
+                pltpu.VMEM((1, width, width), bf16),
+                pltpu.VMEM((rows, width), f32),
+                pltpu.VMEM((rows, width), f32),
+                pltpu.VMEM((rows, width), f32),
+                pltpu.VMEM((rows, 3 * width), bf16),
+                pltpu.VMEM((rows, width), bf16),
+                pltpu.VMEM((rows, width), f32),
+                pltpu.VMEM((rows, width), f32),
+                pltpu.VMEM((rows, width), bf16),
+                pltpu.VMEM((rows, width), bf16),
+                pltpu.VMEM((rows, 3 * width), f32),
+                pltpu.VMEM((rows, width), f32),
             ]
-            + [pltpu.VMEM((total, chips >> (stage + 1), 2, deep, CHUNK), bf16) for stage in range(stages)]
+            + [pltpu.VMEM((plan.ring, plan.chips >> (stage + 1)) + container[2:], bf16) for stage in range(plan.stages)]
             + [
-                dma((blocks * 16,)),
-                dma((blocks, 3, n_pieces)),
-                dma((blocks, 3, n_pieces)),
-                dma((stages, total)),
-                dma((stages, total)),
-                dma((total,)),
-                dma((total,)),
-                dma((n_vector,)),
-                dma((n_vector,)),
+                dma((8,)),
+                dma((8,)),
+                dma((4,)),
+                dma((2, 3, plan.n_pieces)),
+                dma((2, 3, plan.n_pieces)),
+                dma((plan.stages, plan.ring)),
+                dma((plan.stages, plan.ring)),
+                dma((plan.ring,)),
+                dma((plan.ring,)),
+                dma((plan.n_vector,)),
+                dma((plan.n_vector,)),
             ],
         ),
         compiler_params=pltpu.CompilerParams(
             collective_id=0, has_side_effects=True, vmem_limit_bytes=64 * 1024 * 1024 - 65536
         ),
-        cost_estimate=pl.CostEstimate(flops=2 * 4 * rows * total * chips * 2 * deep * CHUNK, bytes_accessed=moved, transcendentals=0),
-    )(meta, *flat, vector)
+        cost_estimate=pl.CostEstimate(flops=2 * rows * width * hidden * 20, bytes_accessed=60 * width * hidden, transcendentals=0),
+    )(
+        meta, back, pre1, x1, g_middle1, gain, pattern, joint, outer_scale, second_gain, mixer_scale, outer, inner, slope0, pre0,
+        mixer, feed0, middle0, branch0, qkv0, x0, feed_g1, came1, *shares, vector1,
+    )
 
 
 def local(scenes, frames, tokens, patch_counts, first_gain, first_shift, joint_weight, joint_bias, query_gain, query_shift, key_gain, mixer_weight, mixer_bias, mixer_scale, second_gain, second_shift, inner_weight, inner_bias, outer_weight, outer_bias, outer_scale, cotangent):
@@ -1426,38 +1613,18 @@
     own_feed1, other_feed1, middle1, branch1, feed1, slope1, layer_out = feed_forward(1, True, meta, att1, x1, *feed_params)
 
     g_feed1, g_middle1, g_att1, vector_feed1 = feed_backward(1, True, heads, meta, cotangent[0], feed1, slope1, middle1, branch1, *back_params)
-    g_qkv1, (left_feed1,) = scene_backward(frames, meta, kept1, g_att1, att_full, att_log, half, [(own_feed1, other_feed1)])
-    g_joint1, g1, vector_joint1 = joint_backward(1, True, head, meta, g_qkv1, pre1, x1, g_middle1, first_gain, pattern, joint_weight)
-
-    g_feed0, g_middle0, g_att0, vector_feed0 = feed_backward(0, False, heads, meta, g1, feed0, slope0, middle0, branch0, *back_params)
-    g_qkv0 = frame_backward(meta, qkv0, g_att0)
-    g_joint0, g0, vector_joint0 = joint_backward(0, False, head, meta, g_qkv0, pre0, x0, g_middle0, first_gain, pattern, joint_weight)
-
-    vectors = jnp.concatenate([vector_feed0, vector_joint0, vector_feed1, vector_joint1], axis=0)
-    pieces, vectors = collect(
-        frames,
-        meta,
-        [
-            (g_feed1, g_joint1, own_feed1, left_feed1, own1, left_joint1),
-            (g_feed0, g_joint0, own_feed0, left_feed0, own0, left_joint0),
-        ],
-        vectors,
+    shared = SHARED_PIECES * CHUNK
+    g_qkv1, came_feed1, (left_feed1,) = scene_backward(
+        frames, meta, kept1, g_att1, att_full, att_log, half, [(own_feed1, other_feed1)], g_feed1, shared
     )
-    pieces = pieces[:].reshape((2, -1) + pieces.shape[1:])[::-1]
-    n_inner = hidden // 2 // CHUNK
-    deep = pieces.shape[3]
-
-    def laid_out(first, last):
-        some = jnp.transpose(pieces[:, first:last], (0, 3, 2, 1, 4))
-        return some.reshape(2, deep, -1)
-
-    outer = pieces[:, :4].reshape(2, 4, 2, deep, 4, LANES)
-    outer = jnp.transpose(outer, (0, 4, 3, 2, 1, 5)).reshape(2, 4 * deep, width)
-    inner = laid_out(4, 4 + n_inner)
-    mixer = laid_out(4 + n_inner, 5 + n_inner)
-    joint = laid_out(5 + n_inner, pieces.shape[1])
+    g0, outer, inner, mixer, joint, vectors = rear(
+        frames, head, meta, g_qkv1, pre1, x1, g_middle1, first_gain, pattern, joint_weight,
+        outer_scale, second_gain, mixer_scale, outer_weight, inner_weight, slope0, pre0,
+        mixer_weight, feed0, middle0, branch0, qkv0, x0, g_feed1, came_feed1,
+        [own_feed1, left_feed1, own1, left_joint1, own_feed0, left_feed0, own0, left_joint0], vector_feed1,
+    )
     vectors = vectors.reshape(2, -1, width)
-    at_joint = vector_feed0.shape[0]
+    at_joint = vector_feed1.shape[0]
 
     def folded(index):
         return vectors[:, at_joint + index].reshape(2, heads, head).sum(1)

time: 426 us -> 362 us (0.85)
  Pallas kernels: 395 us -> 341 us
  local copies, waits for them, and re-layouts: 23.8 us -> 16.1 us
    pallas_call x5 -> x2, Pallas kernels: 260 us -> 222 us  [the longest x1 166 us: rear(): pl.pallas_call(partial(rear_body, plan, frames, head), name='rear', out_s...]
    pallas_call x2 -> x1, Pallas kernels: 33.7 us -> 16.9 us  [feed_backward(): call(partial(feed_back_body, block, packed), f'feed_backward_{block}', (s...]
    reshape x6 -> x0, local copies, waits for them, and re-layouts: 6.51 us -> none  [the longest x3 4.08 us: laid_out(): return some.reshape(2, deep, -1)]
    slice x4 -> x0, local copies, waits for them, and re-layouts: 4.87 us -> none  [the longest x2 3.03 us: laid_out(): some = jnp.transpose(pieces[:, first:last], (0, 3, 2, 1, 4))]
    unnamed x19 -> x23, local copies, waits for them, and re-layouts: 7.8 us -> 12.5 us
where the time goes in v1:
time: 362 us; the launch traced here: 361 us
  Pallas kernels  341 us (94%)
  local copies, waits for them, and re-layouts  16.1 us (4%)
    pallas_call x1, Pallas kernels, rear(): pl.pallas_call(partial(rear_body, plan, frames, head), name='rear', out_s...  166 us
    pallas_call x1, Pallas kernels, scene_backward(): pl.pallas_call(partial(scene_back_body, frames, half, span, len(pairs), s...  55.3 us
    pallas_call x1, Pallas kernels, scene_forward(): pl.pallas_call(partial(scene_body, frames, half, span, len(pairs)), name=...  46.5 us
    pallas_call x2, Pallas kernels, feed_forward(): call(partial(feed_body, block, packed), f'feed_forward_{block}', (steps,)...  33.4 us
    pallas_call x2, Pallas kernels, joint_forward(): call(partial(joint_body, block, packed, head), f'joint_forward_{block}',...  18.6 us
    pallas_call x1, Pallas kernels, feed_backward(): call(partial(feed_back_body, block, packed), f'feed_backward_{block}', (s...  16.9 us
    unnamed x23, local copies, waits for them, and re-layouts  12.5 us

profile of v1, /device:TPU:0, one launch (start us, length us, event | category | flops | bytes accessed | tf_op | source)
XLA Modules:
  0.0 360.6 jit_solution(1782984341683070487)
XLA Ops:
  1.3 0.6 pad_add_fusion.meta
  1.9 0.7 fusion.3
  2.6 0.7 fusion.1
  3.4 0.7 tile.10.pattern_ref.refs_5_
  4.1 8.9 %joint_forward_0.1 = (bf16[144,512]{1,0:T(8,128)(2,1)}, bf16[144,512]{1,0:T(8,128)(2,1)}, f32[144,2048]{1,0:T(8,128)}, bf16[144,3072]{1,0:T(8,128)(2,1)}) custom-call(s32[4]{0:T(128)} %pad_add_fusion.meta, bf16[144,1024]{1,0:T(8,128)(2,1)} %bitcast.39, bf16[2,1024]{1,0:T(2,128)(2,1)} %refs_4_.1, bf16[2,1024]{1,0:T(2,128)(2,1)} %shift_ref.6, ...), custom_call_target="tpu_custom_call" | custom-call | flops 905969664 | bytes 8650752 | tf_op jit(solution)/shard_map/joint_forward_0/pallas_call | solution.py:236
  13.0 3.7 %frame_forward.1.att_ref = bf16[144,1024]{1,0:T(8,128)(2,1)} custom-call(s32[4]{0:T(128)} %pad_add_fusion.meta, bf16[144,3072]{1,0:T(8,128)(2,1)} %get-tuple-element.61.qkv_ref.refs_18_), custom_call_target="tpu_custom_call" | custom-call | flops 84934656 | bytes 1179648 | tf_op jit(solution)/shard_map/frame_forward/pallas_call | solution.py:298
  16.8 16.7 %feed_forward_0.1 = (bf16[144,3072]{1,0:T(8,128)(2,1)}, bf16[144,3072]{1,0:T(8,128)(2,1)}, f32[144,1024]{1,0:T(8,128)}, f32[144,1024]{1,0:T(8,128)}, f32[144,102...) custom-call(s32[4]{0:T(128)} %pad_add_fusion.meta, bf16[144,1024]{1,0:T(8,128)(2,1)} %frame_forward.1.att_ref, ...), custom_call_target="tpu_custom_call" | custom-call | flops 2717908992 | bytes 23560192 | tf_op jit(solution)/shard_map/feed_forward_0/pallas_call | solution.py:857
  33.5 9.6 %joint_forward_1.1 = (bf16[144,512]{1,0:T(8,128)(2,1)}, bf16[144,512]{1,0:T(8,128)(2,1)}, f32[144,2048]{1,0:T(8,128)}, bf16[16,224,128]{2,1,0:T(8,128)(2,1)}) custom-call(s32[4]{0:T(128)} %pad_add_fusion.meta, f32[144,1024]{1,0:T(8,128)} %get-tuple-element.62.x_ref.refs_2_, bf16[2,1024]{1,0:T(2,128)(2,1)} %refs_4_.1, bf16[2,1024]{1,0:T(2,128)(2,1)} %shift_ref.6, ...), custom_call_target="tpu_custom_call" | custom-call | flops 905969664 | bytes 8650752 | tf_op jit(solution)/shard_map/joint_forward_1/pallas_call | solution.py:236
  43.1 46.5 %scene_forward.1 = (bf16[16,72,128]{2,1,0:T(8,128)(2,1)}, bf16[16,224,128]{2,1,0:T(8,128)(2,1)}, f32[1152,128]{1,0:T(8,128)}, f32[1152,128]{1,0:T(8,128)}, bf16[...) custom-call(s32[4]{0:T(128)} %pad_add_fusion.meta, ...), custom_call_target="tpu_custom_call" | custom-call | flops 2717908992 | bytes 2949120 | tf_op jit(solution)/shard_map/scene_forward/pallas_call | solution.py:534
  89.6 16.7 %feed_forward_1.1 = (bf16[144,3072]{1,0:T(8,128)(2,1)}, bf16[144,3072]{1,0:T(8,128)(2,1)}, f32[144,1024]{1,0:T(8,128)}, f32[144,1024]{1,0:T(8,128)}, f32[144,102...) custom-call(s32[4]{0:T(128)} %pad_add_fusion.meta, bf16[16,72,128]{2,1,0:T(8,128)(2,1)} %get-tuple-element.70.att_ref, ...), custom_call_target="tpu_custom_call" | custom-call | flops 2717908992 | bytes 23560192 | tf_op jit(solution)/shard_map/feed_forward_1/pallas_call | solution.py:857
  106.4 16.9 %feed_backward_1.1 = (bf16[2,144,3072]{2,1,0:T(8,128)(2,1)}, f32[144,1024]{1,0:T(8,128)}, bf16[16,72,128]{2,1,0:T(8,128)(2,1)}, f32[10,1024]{1,0:T(8,128)}) custom-call(s32[4]{0:T(128)} %pad_add_fusion.meta, bf16[144,1024]{1,0:T(8,128)(2,1)} %bitcast.43, f32[144,1024]{1,0:T(8,128)} %get-tuple-element.73.refs_1_, f32[144,4096]{1,0:T(8,128)} %get-tuple-element.74.refs_2_, ...), custom_call_target="tpu_custom_call" | custom-call | flops 2717908992 | bytes 24444928 | tf_op jit(solution)/shard_map/feed_backward_1/pallas_call | solution.py:953
  123.3 55.3 %scene_backward.1 = (bf16[16,3,72,128]{3,2,1,0:T(8,128)(2,1)}, bf16[3,144,3072]{2,1,0:T(8,128)(2,1)}, bf16[3,144,3072]{2,1,0:T(8,128)(2,1)}) custom-call(s32[4]{0:T(128)} %pad_add_fusion.meta, bf16[16,224,128]{2,1,0:T(8,128)(2,1)} %get-tuple-element.72.kept_ref, bf16[16,72,128]{2,1,0:T(8,128)(2,1)} %get-tuple-element.77.grad_ref, ...), custom_call_target="tpu_custom_call" | custom-call | flops 6794772480 | bytes 4423680 | tf_op jit(solution)/shard_map/scene_backward/pallas_call | solution.py:732
  178.5 166.3 %rear.1 = (bf16[144,1024]{1,0:T(8,128)(2,1)}, f32[2,128,1024]{2,1,0:T(8,128)}, f32[2,32,4096]{2,1,0:T(8,128)}, f32[2,32,1024]{2,1,0:T(8,128)}, f32[2,32,3072]{2,1,0:T(8,128)}, /*index=5*/f32[36,1024]{1,0:T(8,128)}) custom-call(s32[4]{0:T(128)} %pad_add_fusion.meta, bf16[16,3,72,128]{3,2,1,0:T(8,128)(2,1)} %get-tuple-element.83.refs_0_, ...), custom_call_target="tpu_custom_call" | custom-call | flops 24159191040 | bytes 251658240 | tf_op jit(solution)/shard_map/rear/pallas_call | solution.py:1512
  344.8 0.0 copy-start.2
  344.9 0.0 copy-start.1
  344.9 1.0 reshape.93
  345.9 0.6 copy.55
  346.6 0.0 copy-start
  346.6 0.1 fusion
  346.7 0.6 copy.65
  347.3 0.6 copy.56
  347.9 0.6 copy.67
  348.5 0.6 copy.68
  349.1 0.6 copy.69
  349.7 0.6 copy.70
  350.4 0.6 copy.66
  351.0 0.6 copy.71
  351.6 0.6 copy.72
  352.2 0.1 reshape_squeeze.9
  352.2 0.6 reduce_sum.27
  352.8 0.1 reshape_squeeze.10
  352.9 0.6 reduce_sum.28
  353.5 0.1 reshape_squeeze.11
  353.6 0.6 reduce_sum.29
  354.2 1.7 copy.79
  355.9 2.1 copy.80
  357.9 0.0 copy-done.2
  357.9 0.7 copy.81
  358.6 0.0 copy-done.1
  358.6 1.0 copy.82
  359.6 0.0 copy-done
  359.6 1.0 copy.83
  (4 shorter events, 0.1 us)
Async XLA Ops:
  344.8 13.1 %copy-start.2 = (f32[2,32,1024]{2,1,0:T(8,128)S(1)}, f32[2,32,1024]{2,1,0:T(8,128)}, u32[]{:S(2)}) copy-start(f32[2,32,1024]{2,1,0:T(8,128)} %get-tuple-element.153) | copy-start | bytes 786436
  344.9 13.8 %copy-start.1 = (f32[2,32,4096]{2,1,0:T(8,128)S(1)}, f32[2,32,4096]{2,1,0:T(8,128)}, u32[]{:S(2)}) copy-start(f32[2,32,4096]{2,1,0:T(8,128)} %get-tuple-element.158) | copy-start | bytes 3145732
  346.6 13.0 %copy-start = (f32[2,128,1024]{2,1,0:T(8,128)S(1)}, f32[2,128,1024]{2,1,0:T(8,128)}, u32[]{:S(2)}) copy-start(f32[2,128,1024]{2,1,0:T(8,128)} %get-tuple-element.160) | copy-start | bytes 3145732

commit v2 on v1

--- a/solution.py
+++ b/solution.py
@@ -11,9 +11,9 @@
 CHUNK = 512
 LANES = 128
 SLAB = 256
-SHARED_PIECES = 4
-SWAP_EVERY = 4
-AHEAD = 3
+SHARED_PIECES = 3
+SWAP_EVERY = 3
+AHEAD = 2
 LAG = 3
 VECTOR_LAG = 3
 norm_eps = 1e-06
@@ -477,34 +477,48 @@
     values[m:, :] = jnp.where(open_high, jnp.where(low_m, turn(v), 1.0), 0.0).astype(bf16)
     low = first_lanes(LANES)
 
-    @pl.loop(0, n // LANES)
+    pair = 2 * half
+    place = lax.rem(frame, heads)
+    low = first_lanes(pair)
+    pieces = heads // 2
+
+    def from_head(target):
+        return remote(
+            sent.at[target], att_ref.at[place], b_send.at[target], b_recv.at[place], (scene, part * heads + target)
+        )
+
+    def turned(piece):
+        return lax.rem(piece + place // 2 + 1, pieces)
+
+    def send(piece):
+        for index in range(2):
+            target = 2 * turned(piece) + index
+
+            @pl.when(target != place)
+            def _():
+                from_head(target).start()
+
+    @pl.loop(0, pieces)
     def _(piece):
-        at = pl.multiple_of(piece * LANES, LANES)
-        some = jnp.concatenate([queries[pl.ds(at, LANES), :], queries[pl.ds(n + at, LANES), :]], axis=0)
-        total = jnp.zeros((2 * LANES, LANES), f32)
+        @pl.when(piece > 0)
+        def _():
+            send(piece - 1)
+
+        at = pl.multiple_of(turned(piece) * pair, pair)
+        some = jnp.concatenate([queries[pl.ds(at, pair), :], queries[pl.ds(n + at, pair), :]], axis=0)
+        total = jnp.zeros((2 * pair, LANES), f32)
         for start in range(0, 2 * m, span):
             power = jnp.exp(nt(some, keys[start : start + span, :])).astype(bf16)
             total = total + nn(power, values[start : start + span, :])
-        first, second = total[:LANES], total[LANES:]
+        first, second = total[:pair], total[pair:]
         bottom = jnp.where(low, turn(first), second)
         result = jnp.where(low, first, turn(second)) / bottom
-        out_ref[pl.ds(at, LANES), :] = result
-        log_ref[pl.ds(at, LANES), :] = jnp.log(bottom)
+        sent[pl.ds(2 * turned(piece), 2)] = result.reshape(2, half, LANES).astype(bf16)
+        out_ref[pl.ds(at, pair), :] = result
+        log_ref[pl.ds(at, pair), :] = jnp.log(bottom)
 
     share.relay()
-    sent[...] = out_ref[...].reshape(heads, half, LANES).astype(bf16)
-    place = lax.rem(frame, heads)
-
-    def from_head(offset):
-        target = lax.rem(place + offset, heads)
-        return remote(
-            sent.at[target], att_ref.at[place], b_send.at[offset], b_recv.at[offset], (scene, part * heads + target)
-        )
-
-    @pl.loop(1, heads)
-    def _(offset):
-        from_head(offset).start()
-
+    send(pieces - 1)
     att_ref[place] = sent[place]
 
     @pl.loop(1, frames)
@@ -513,7 +527,11 @@
 
     @pl.loop(1, heads)
     def _(offset):
-        from_head(offset).wait()
+        other = lax.rem(place + offset, heads)
+        from_head(other).wait_send()
+        remote(
+            sent.at[other], att_ref.at[other], b_send.at[other], b_recv.at[other], (scene, part * heads + other)
+        ).wait_recv()
 
     share.close()
 
@@ -591,8 +609,8 @@
     pairs = [(refs[2 * index], refs[2 * index + 1]) for index in range(n_share)]
     refs = refs[2 * n_share :]
     back_ref, feed_came, outs, refs = refs[0], refs[1], refs[2 : 2 + n_share], refs[2 + n_share :]
-    queries, keys, values, grads, turned, came, dk_ref, dv_ref, sent_q, sent_kv = refs[:10]
-    a_send, a_recv, b_send, b_recv, c_send, c_recv, s_send, s_recv, g_send, g_recv = refs[10:]
+    queries, keys, values, grads, turned, came, sent_q, sent_kv = refs[:8]
+    a_send, a_recv, b_send, b_recv, c_send, c_recv, s_send, s_recv, g_send, g_recv = refs[8:]
     n = queries.shape[0] // 2
     m = keys.shape[0] // 2
     scene = lax.axis_index("scene")
@@ -646,16 +664,38 @@
     grads[:n, :] = jnp.where(low_n, g, three_lanes(turn(delta), 0.0)).astype(bf16)
     grads[n:, :] = jnp.where(low_n, turn(g), three_lanes(delta, 0.0)).astype(bf16)
 
-    @pl.loop(0, m // LANES)
+    pair = 2 * half
+    low_pair = first_lanes(pair)
+    pieces = frames // 2
+
+    def back_kv(target):
+        return remote(
+            sent_kv.at[target], back_ref.at[frame, pl.ds(1, 2)], b_send.at[target], b_recv.at[frame], (scene, target)
+        )
+
+    def turned_to(piece):
+        return lax.rem(piece + frame // 2 + 1, pieces)
+
+    def send(piece):
+        for index in range(2):
+            target = 2 * turned_to(piece) + index
+
+            @pl.when(target != frame)
+            def _():
+                back_kv(target).start()
+
+    @pl.loop(0, pieces)
     def _(piece):
-        at = pl.multiple_of(piece * LANES, LANES)
-        key_part = jnp.concatenate([keys[pl.ds(at, LANES), :], keys[pl.ds(m + at, LANES), :]], axis=0)
-        value_part = jnp.concatenate(
-            [values[pl.ds(at, LANES), :], values[pl.ds(m + at, LANES), :]], axis=0
-        )
+        @pl.when(piece > 0)
+        def _():
+            send(piece - 1)
+
+        at = pl.multiple_of(turned_to(piece) * pair, pair)
+        key_part = jnp.concatenate([keys[pl.ds(at, pair), :], keys[pl.ds(m + at, pair), :]], axis=0)
+        value_part = jnp.concatenate([values[pl.ds(at, pair), :], values[pl.ds(m + at, pair), :]], axis=0)
         key_turned = jnp.transpose(key_part.astype(f32)).astype(bf16)
-        dk = jnp.zeros((2 * LANES, LANES), f32)
-        dv = jnp.zeros((2 * LANES, LANES), f32)
+        dk = jnp.zeros((2 * pair, LANES), f32)
+        dv = jnp.zeros((2 * pair, LANES), f32)
         for start in range(0, 2 * n, span):
             some = queries[start : start + span, :]
             some_grads = grads[start : start + span, :]
@@ -664,22 +704,13 @@
             dv = dv + nn(probs.astype(bf16), some_grads)
             dk = dk + nn(grad_scores, some)
             turned[:, start : start + span] += nn(key_turned, grad_scores)
-        dk_ref[pl.ds(at, LANES), :] = jnp.where(low, dk[:LANES], turn(dk[LANES:]))
-        dv_ref[pl.ds(at, LANES), :] = jnp.where(low, dv[:LANES], turn(dv[LANES:]))
+        dk = jnp.where(low_pair, dk[:pair], turn(dk[pair:])).reshape(2, half, LANES)
+        dv = jnp.where(low_pair, dv[:pair], turn(dv[pair:])).reshape(2, half, LANES)
+        sent_kv[pl.ds(2 * turned_to(piece), 2), 0] = dk.astype(bf16)
+        sent_kv[pl.ds(2 * turned_to(piece), 2), 1] = dv.astype(bf16)
 
     share.relay()
-    sent_kv[:, 0] = dk_ref[...].reshape(frames, half, LANES).astype(bf16)
-    sent_kv[:, 1] = dv_ref[...].reshape(frames, half, LANES).astype(bf16)
-
-    def back_kv(offset):
-        target = lax.rem(frame + offset, frames)
-        return remote(
-            sent_kv.at[target], back_ref.at[frame, pl.ds(1, 2)], b_send.at[offset], b_recv.at[offset], (scene, target)
-        )
-
-    @pl.loop(1, frames)
-    def _(offset):
-        back_kv(offset).start()
+    send(pieces - 1)
 
     scale = base ** (-0.5)
     rows = []
@@ -710,7 +741,11 @@
 
     @pl.loop(1, frames)
     def _(offset):
-        back_kv(offset).wait()
+        other = lax.rem(frame + offset, frames)
+        back_kv(other).wait_send()
+        remote(
+            sent_kv.at[other], back_ref.at[other, pl.ds(1, 2)], b_send.at[other], b_recv.at[other], (scene, other)
+        ).wait_recv()
 
     @pl.loop(1, heads)
     def _(offset):
@@ -746,8 +781,6 @@
                 pltpu.VMEM((2 * n, LANES), bf16),
                 pltpu.VMEM((LANES, 2 * n), f32),
                 pltpu.VMEM((heads, half, LANES), bf16),
-                pltpu.VMEM((m, LANES), f32),
-                pltpu.VMEM((m, LANES), f32),
                 pltpu.VMEM((heads, half, LANES), bf16),
                 pltpu.VMEM((frames, 2, half, LANES), bf16),
                 dma((heads,)),
@@ -1583,6 +1616,76 @@
     )
 
 
+def finish_body(heads, meta, vectors_ref, *refs):
+    count = 5
+    large_in, large_out = refs[:count], refs[count : 2 * count]
+    (
+        first_gain, first_shift, joint_bias, query_gain, query_shift, key_gain, mixer_bias, mixer_scale,
+        second_gain, second_shift, inner_bias, outer_bias, outer_scale,
+    ) = refs[2 * count : -1]
+    sem = refs[-1]
+    copies = [
+        pltpu.make_async_copy(source, target, sem.at[index])
+        for index, (source, target) in enumerate(zip(large_in, large_out))
+    ]
+    for copy in copies:
+        copy.start()
+    width = first_gain.shape[1]
+    head = query_gain.shape[1]
+    feed_rows = 6 + inner_bias.shape[1] // width
+    for block in range(2):
+        base = block * (feed_rows + 8)
+        rows = vectors_ref[base : base + feed_rows + 8, :]
+
+        def pick(index):
+            return rows[index : index + 1, :]
+
+        def at(index):
+            return pick(feed_rows + index)
+
+        def fold(value):
+            total = value[:, :LANES]
+            for place in range(1, width // LANES):
+                total = total + value[:, place * LANES : (place + 1) * LANES]
+            return (total + turn(total))[:, :head]
+
+        here = slice(block, block + 1)
+        for target, index in (
+            (outer_scale, 0), (outer_bias, 1), (second_gain, 2), (second_shift, 3), (mixer_scale, 4), (mixer_bias, 5),
+        ):
+            target[here, :] = pick(index)
+        for index in range(inner_bias.shape[1] // width):
+            inner_bias[here, index * width : (index + 1) * width] = pick(6 + index)
+        first_gain[here, :] = at(0)
+        first_shift[here, :] = at(1)
+        for index in range(3):
+            joint_bias[here, index * width : (index + 1) * width] = at(2 + index)
+        query_gain[here, :] = fold(at(5))
+        query_shift[here, :] = fold(at(6))
+        key_gain[here, :] = fold(at(7))
+    for copy in copies:
+        copy.wait()
+
+
+def finish(heads, meta, vectors, large):
+    width = vectors.shape[1]
+    head = width // heads
+    hidden = large[2].shape[2]
+    sizes = [width, width, 3 * width, head, head, head, width, width, width, width, hidden, width, width]
+    return pl.pallas_call(
+        partial(finish_body, heads),
+        name="finish",
+        out_shape=[sds(value.shape, value.dtype) for value in large] + [sds((2, size), f32) for size in sizes],
+        grid_spec=pltpu.PrefetchScalarGridSpec(
+            num_scalar_prefetch=1,
+            grid=(1,),
+            in_specs=[vmem_space] * 6,
+            out_specs=[any_space] * 5 + [full((2, size)) for size in sizes],
+            scratch_shapes=[dma((5,))],
+        ),
+    )(meta, vectors, *large)
+
+
 def local(scenes, frames, tokens, patch_counts, first_gain, first_shift, joint_weight, joint_bias, query_gain, query_shift, key_gain, mixer_weight, mixer_bias, mixer_scale, second_gain, second_shift, inner_weight, inner_bias, outer_weight, outer_bias, outer_scale, cotangent):
     rows, width = tokens.shape[1:]
     half = rows // 2
@@ -1623,32 +1726,16 @@
         mixer_weight, feed0, middle0, branch0, qkv0, x0, g_feed1, came_feed1,
         [own_feed1, left_feed1, own1, left_joint1, own_feed0, left_feed0, own0, left_joint0], vector_feed1,
     )
-    vectors = vectors.reshape(2, -1, width)
-    at_joint = vector_feed1.shape[0]
-
-    def folded(index):
-        return vectors[:, at_joint + index].reshape(2, heads, head).sum(1)
-
+    (
+        g0, outer, inner, mixer, joint,
+        grad_first_gain, grad_first_shift, grad_joint_bias, grad_query_gain, grad_query_shift, grad_key_gain,
+        grad_mixer_bias, grad_mixer_scale, grad_second_gain, grad_second_shift, grad_inner_bias, grad_outer_bias, grad_outer_scale,
+    ) = finish(heads, meta, vectors, (g0, outer, inner, mixer, joint))
     return (
-        layer_out[None],
-        g0[None],
-        vectors[:, at_joint],
-        vectors[:, at_joint + 1],
-        joint,
-        vectors[:, at_joint + 2 : at_joint + 5].reshape(2, 3 * width),
-        folded(5),
-        folded(6),
-        folded(7),
-        mixer,
-        vectors[:, 5],
-        vectors[:, 4],
-        vectors[:, 2],
-        vectors[:, 3],
-        inner,
-        vectors[:, 6:at_joint].reshape(2, hidden),
-        outer,
-        vectors[:, 1],
-        vectors[:, 0],
+        layer_out[None], g0[None],
+        grad_first_gain, grad_first_shift, joint, grad_joint_bias, grad_query_gain, grad_query_shift, grad_key_gain,
+        mixer, grad_mixer_bias, grad_mixer_scale, grad_second_gain, grad_second_shift,
+        inner, grad_inner_bias, outer, grad_outer_bias, grad_outer_scale,
     )
 
 

time: 362 us -> 336 us (0.928)
  local copies, waits for them, and re-layouts: 16.1 us -> 2.19 us
  Pallas kernels: 341 us -> 330 us
    unnamed x23 -> x0, local copies, waits for them, and re-layouts: 12.5 us -> none
    pallas_call x1, Pallas kernels: 166 us -> 160 us  [rear(): pl.pallas_call(partial(rear_body, plan, frames, head), name='rear', out_s...]
    pallas_call x1, Pallas kernels: 46.5 us -> 41.2 us  [scene_forward(): pl.pallas_call(partial(scene_body, frames, half, span, len(pairs)), name=...]
    pallas_call x0 -> x1, Pallas kernels: none -> 5.13 us  [finish(): pl.pallas_call(partial(finish_body, heads), name='finish', out_shape=[sds...]
    pallas_call x1, Pallas kernels: 55.3 us -> 51.4 us  [scene_backward(): pl.pallas_call(partial(scene_back_body, frames, half, span, len(pairs), s...]
where the time goes in v2:
time: 336 us; the launch traced here: 335 us
  Pallas kernels  330 us (98%)
    pallas_call x1, Pallas kernels, rear(): pl.pallas_call(partial(rear_body, plan, frames, head), name='rear', out_s...  160 us
    pallas_call x1, Pallas kernels, scene_backward(): pl.pallas_call(partial(scene_back_body, frames, half, span, len(pairs), s...  51.4 us
    pallas_call x1, Pallas kernels, scene_forward(): pl.pallas_call(partial(scene_body, frames, half, span, len(pairs)), name=...  41.2 us
    pallas_call x2, Pallas kernels, feed_forward(): call(partial(feed_body, block, packed), f'feed_forward_{block}', (steps,)...  33.4 us
    pallas_call x2, Pallas kernels, joint_forward(): call(partial(joint_body, block, packed, head), f'joint_forward_{block}',...  18.6 us
    pallas_call x1, Pallas kernels, feed_backward(): call(partial(feed_back_body, block, packed), f'feed_backward_{block}', (s...  16.9 us

profile of v2, /device:TPU:0, one launch (start us, length us, event | category | flops | bytes accessed | tf_op | source)
XLA Modules:
  0.0 334.6 jit_solution(7176308255508048700)
XLA Ops:
  1.3 0.6 pad_add_fusion.meta
  1.9 0.7 fusion.2
  2.7 0.7 fusion
  3.4 0.7 tile.10.pattern_ref.refs_5_
  4.1 8.9 %joint_forward_0.1 = (bf16[144,512]{1,0:T(8,128)(2,1)}, bf16[144,512]{1,0:T(8,128)(2,1)}, f32[144,2048]{1,0:T(8,128)}, bf16[144,3072]{1,0:T(8,128)(2,1)}) custom-call(s32[4]{0:T(128)} %pad_add_fusion.meta, bf16[144,1024]{1,0:T(8,128)(2,1)} %bitcast.9, bf16[2,1024]{1,0:T(2,128)(2,1)} %refs_4_.1, bf16[2,1024]{1,0:T(2,128)(2,1)} %shift_ref.6, ...), custom_call_target="tpu_custom_call" | custom-call | flops 905969664 | bytes 8650752 | tf_op jit(solution)/shard_map/joint_forward_0/pallas_call | solution.py:236
  13.1 3.7 %frame_forward.1.att_ref = bf16[144,1024]{1,0:T(8,128)(2,1)} custom-call(s32[4]{0:T(128)} %pad_add_fusion.meta, bf16[144,3072]{1,0:T(8,128)(2,1)} %get-tuple-element.79.qkv_ref.refs_18_), custom_call_target="tpu_custom_call" | custom-call | flops 84934656 | bytes 1179648 | tf_op jit(solution)/shard_map/frame_forward/pallas_call | solution.py:298
  16.8 16.7 %feed_forward_0.1 = (bf16[144,3072]{1,0:T(8,128)(2,1)}, bf16[144,3072]{1,0:T(8,128)(2,1)}, f32[144,1024]{1,0:T(8,128)}, f32[144,1024]{1,0:T(8,128)}, f32[144,102...) custom-call(s32[4]{0:T(128)} %pad_add_fusion.meta, bf16[144,1024]{1,0:T(8,128)(2,1)} %frame_forward.1.att_ref, ...), custom_call_target="tpu_custom_call" | custom-call | flops 2717908992 | bytes 23560192 | tf_op jit(solution)/shard_map/feed_forward_0/pallas_call | solution.py:890
  33.5 9.6 %joint_forward_1.1 = (bf16[144,512]{1,0:T(8,128)(2,1)}, bf16[144,512]{1,0:T(8,128)(2,1)}, f32[144,2048]{1,0:T(8,128)}, bf16[16,224,128]{2,1,0:T(8,128)(2,1)}) custom-call(s32[4]{0:T(128)} %pad_add_fusion.meta, f32[144,1024]{1,0:T(8,128)} %get-tuple-element.80.x_ref.refs_2_, bf16[2,1024]{1,0:T(2,128)(2,1)} %refs_4_.1, bf16[2,1024]{1,0:T(2,128)(2,1)} %shift_ref.6, ...), custom_call_target="tpu_custom_call" | custom-call | flops 905969664 | bytes 8650752 | tf_op jit(solution)/shard_map/joint_forward_1/pallas_call | solution.py:236
  43.1 41.2 %scene_forward.1 = (bf16[16,72,128]{2,1,0:T(8,128)(2,1)}, bf16[16,224,128]{2,1,0:T(8,128)(2,1)}, f32[1152,128]{1,0:T(8,128)}, f32[1152,128]{1,0:T(8,128)}, bf16[...) custom-call(s32[4]{0:T(128)} %pad_add_fusion.meta, ...), custom_call_target="tpu_custom_call" | custom-call | flops 2717908992 | bytes 2949120 | tf_op jit(solution)/shard_map/scene_forward/pallas_call | solution.py:552
  84.3 16.7 %feed_forward_1.1 = (bf16[144,3072]{1,0:T(8,128)(2,1)}, bf16[144,3072]{1,0:T(8,128)(2,1)}, f32[144,1024]{1,0:T(8,128)}, f32[144,1024]{1,0:T(8,128)}, f32[144,102...) custom-call(s32[4]{0:T(128)} %pad_add_fusion.meta, bf16[16,72,128]{2,1,0:T(8,128)(2,1)} %get-tuple-element.88.att_ref, ...), custom_call_target="tpu_custom_call" | custom-call | flops 2717908992 | bytes 23560192 | tf_op jit(solution)/shard_map/feed_forward_1/pallas_call | solution.py:890
  101.0 16.9 %feed_backward_1.1 = (bf16[2,144,3072]{2,1,0:T(8,128)(2,1)}, f32[144,1024]{1,0:T(8,128)}, bf16[16,72,128]{2,1,0:T(8,128)(2,1)}, f32[10,1024]{1,0:T(8,128)}) custom-call(s32[4]{0:T(128)} %pad_add_fusion.meta, bf16[144,1024]{1,0:T(8,128)(2,1)} %bitcast.12, f32[144,1024]{1,0:T(8,128)} %get-tuple-element.91.refs_1_, f32[144,4096]{1,0:T(8,128)} %get-tuple-element.92.refs_2_, ...), custom_call_target="tpu_custom_call" | custom-call | flops 2717908992 | bytes 24444928 | tf_op jit(solution)/shard_map/feed_backward_1/pallas_call | solution.py:986
  117.9 51.4 %scene_backward.1 = (bf16[16,3,72,128]{3,2,1,0:T(8,128)(2,1)}, bf16[3,144,3072]{2,1,0:T(8,128)(2,1)}, bf16[3,144,3072]{2,1,0:T(8,128)(2,1)}) custom-call(s32[4]{0:T(128)} %pad_add_fusion.meta, bf16[16,224,128]{2,1,0:T(8,128)(2,1)} %get-tuple-element.90.kept_ref, bf16[16,72,128]{2,1,0:T(8,128)(2,1)} %get-tuple-element.95.grad_ref, ...), custom_call_target="tpu_custom_call" | custom-call | flops 6794772480 | bytes 4423680 | tf_op jit(solution)/shard_map/scene_backward/pallas_call | solution.py:767
  169.4 159.9 %rear.1 = (bf16[144,1024]{1,0:T(8,128)(2,1)}, f32[2,128,1024]{2,1,0:T(8,128)}, f32[2,32,4096]{2,1,0:T(8,128)}, f32[2,32,1024]{2,1,0:T(8,128)}, f32[2,32,3072]{2,1,0:T(8,128)}, /*index=5*/f32[36,1024]{1,0:T(8,128)}) custom-call(s32[4]{0:T(128)} %pad_add_fusion.meta, bf16[16,3,72,128]{3,2,1,0:T(8,128)(2,1)} %get-tuple-element.101.refs_0_, ...), custom_call_target="tpu_custom_call" | custom-call | flops 24159191040 | bytes 251658240 | tf_op jit(solution)/shard_map/rear/pallas_call | solution.py:1545
  329.3 5.1 %finish.1 = (bf16[144,1024]{1,0:T(8,128)(2,1)}, f32[2,128,1024]{2,1,0:T(8,128)}, f32[2,32,4096]{2,1,0:T(8,128)}, f32[2,32,1024]{2,1,0:T(8,128)}, f32[2,32,3072]{...) custom-call(s32[4]{0:T(128)} %pad_add_fusion.meta, ...), custom_call_target="tpu_custom_call" | custom-call | tf_op jit(solution)/shard_map/finish/pallas_call | solution.py:1675
  (2 shorter events, 0.0 us)

commit v3 on v2

--- a/solution.py
+++ b/solution.py
@@ -60,6 +60,14 @@
     first = lax.shift_right_logical(lax.broadcasted_iota(jnp.int32, (width, width), 0), shift)
     second = lax.shift_right_logical(lax.broadcasted_iota(jnp.int32, (width, width), 1), shift)
     return jnp.where(first == second, value, 0.0).astype(bf16)
+
+
+def repeated(ref, block):
+    head = ref.shape[1]
+    lane = lax.broadcasted_iota(jnp.int32, (head, SLAB), 1)
+    place = lax.broadcasted_iota(jnp.int32, (head, SLAB), 0)
+    copies = jnp.where(lax.rem(lane, head) == place, 1.0, 0.0).astype(bf16)
+    return nn(ref[...], copies)[block : block + 1, :]
 
 
 def seg_dot(value, matrix):
@@ -145,7 +153,7 @@
 
 
 def joint_body(
-    block, packed, head, meta, x_ref, gain_ref, shift_ref, pattern_ref, w_ref, b_ref,
+    block, packed, head, meta, x_ref, gain_ref, shift_ref, q_gain_ref, q_shift_ref, k_gain_ref, w_ref, b_ref,
     own_ref, other_ref, pre_ref, out_ref, normed_ref, *stage
 ):
     step = pl.program_id(0)
@@ -159,23 +167,24 @@
         normed = (hat * row(gain_ref, block) + row(shift_ref, block)).astype(bf16)
         normed_ref[...] = normed
 
-        @pl.when(meta[0] == 0)
+        scene = lax.axis_index("scene")
+
+        @pl.when(scene == 0)
         def _():
             own_ref[...] = normed[:, : width // 2]
             other_ref[...] = normed[:, width // 2 :]
 
-        @pl.when(meta[0] != 0)
+        @pl.when(scene != 0)
         def _():
             own_ref[...] = normed[:, width // 2 :]
             other_ref[...] = normed[:, : width // 2]
 
         if packed:
-            count = jnp.full((8, LANES), meta[3], jnp.int32).astype(f32)
+            count = jnp.full((8, LANES), meta[0], jnp.int32).astype(f32)
             for place in range(stage[0].shape[0]):
                 stage[0][place, 3 * half : 3 * half + 8, :] = count
 
     joined = nn(normed_ref[...], w_ref[0]) + row(b_ref, block)
-    pattern = pattern_ref[...]
 
     def emit(part, values):
         if packed:
@@ -201,14 +210,14 @@
     def _():
         pre_ref[...] = joined
         emit(0, normed_heads(
-            pattern[3 * block : 3 * block + 1] * scale,
-            pattern[3 * block + 1 : 3 * block + 2] * scale,
+            repeated(q_gain_ref, block) * scale,
+            repeated(q_shift_ref, block) * scale,
         ))
 
     @pl.when((step >= per_part) & (step < 2 * per_part))
     def _():
         pre_ref[...] = joined
-        emit(1, normed_heads(pattern[3 * block + 2 : 3 * block + 3], None))
+        emit(1, normed_heads(repeated(k_gain_ref, block), None))
 
     @pl.when(step >= 2 * per_part)
     def _():
@@ -241,7 +250,7 @@
             full((rows, width)),
             full(gain.shape),
             full(shift.shape),
-            full(pattern.shape),
+            full(pattern[0].shape), full(pattern[1].shape), full(pattern[2].shape),
             pl.BlockSpec((1, width, CHUNK), lambda j, m: (block, 0, j)),
             pl.BlockSpec((2, CHUNK), lambda j, m: (0, j)),
         ],
@@ -260,7 +269,7 @@
         [pltpu.VMEM((rows, width), bf16)] + extra,
         2 * rows * width * 3 * width,
         6 * width * width + 16 * rows * width,
-    )(meta, x, gain, shift, pattern, weight, bias)
+    )(meta, x, gain, shift, *pattern, weight, bias)
 
 
 def lane_picks():
@@ -271,7 +280,7 @@
 
 def open_row(meta, rows):
     place = lax.broadcasted_iota(jnp.int32, (1, rows), 1)
-    return jnp.where(place < meta[3] + SPECIAL, 0.0, closed_score)
+    return jnp.where(place < meta[0] + SPECIAL, 0.0, closed_score)
 
 
 def frame_body(meta, qkv_ref, out_ref):
@@ -370,11 +379,10 @@
     return core, core_peer, scene_peer, cross_peer, bits[1:]
 
 
-def enter(targets):
+def greet(targets):
     barrier = pltpu.get_barrier_semaphore()
     for target in targets:
         pl.semaphore_signal(barrier, inc=1, device_id=target, device_id_type=MESH)
-    pl.semaphore_wait(barrier, len(targets))
 
 
 def enter_scene(frames):
@@ -817,7 +825,7 @@
     rows, width = middle_ref.shape
     hidden_half = own_ref.shape[1] - width
     half_steps = hidden_half // CHUNK
-    mine = meta[0]
+    mine = lax.axis_index("scene")
 
     def split(value, at):
         first, second = value[:, : width // 2], value[:, width // 2 :]
@@ -877,7 +885,7 @@
         result = middle_ref[...] + row(outer_scale, block) * feed
         if packed:
             place = lax.broadcasted_iota(jnp.int32, result.shape, 0)
-            result = jnp.where(place < meta[3] + SPECIAL, result, 0.0)
+            result = jnp.where(place < meta[0] + SPECIAL, result, 0.0)
         out_ref[...] = result.astype(out_ref.dtype)
 
 
@@ -926,7 +934,7 @@
         g = g_ref[...].astype(f32)
         if packed:
             place = lax.broadcasted_iota(jnp.int32, g.shape, 0)
-            g = jnp.where(place < meta[3] + SPECIAL, g, 0.0)
+            g = jnp.where(place < meta[0] + SPECIAL, g, 0.0)
         return g
 
     @pl.when(step == 0)
@@ -1017,7 +1025,7 @@
 
 
 def joint_back_core(
-    block, head, step, steps, chunk, g, pre_ref, x_ref, g_middle_ref, gain_ref, pattern_ref, w_ref,
+    block, head, step, steps, chunk, g, pre_ref, x_ref, g_middle_ref, gain_ref, q_gain_ref, k_gain_ref, w_ref,
     grads_ref, at_joined, out_ref, vector_ref, total_ref
 ):
     rows, width = total_ref.shape
@@ -1028,7 +1036,6 @@
     def _():
         total_ref[...] = jnp.zeros_like(total_ref)
 
-    pattern = pattern_ref[...]
     in_row = pl.ds(pl.multiple_of(lax.rem(chunk, per_part) * CHUNK, CHUNK), CHUNK)
 
     def finish(g_joined):
@@ -1061,11 +1068,11 @@
 
     @pl.when(chunk < per_part)
     def _():
-        head_back(pattern[3 * block : 3 * block + 1], 5, 6)
+        head_back(repeated(q_gain_ref, block), 5, 6)
 
     @pl.when((chunk >= per_part) & (chunk < 2 * per_part))
     def _():
-        head_back(pattern[3 * block + 2 : 3 * block + 3], 7, None)
+        head_back(repeated(k_gain_ref, block), 7, None)
 
     @pl.when(chunk >= 2 * per_part)
     def _():
@@ -1141,28 +1148,29 @@
         self.ring = 12
         self.lags = [LAG * (stage + 1) for stage in range(self.stages)]
         self.end_lag = self.lags[-1] + 2
-        self.n_vector = 2 + self.stages
-        self.slots = max(
-            self.first + self.total + self.end_lag, self.compute_end + VECTOR_LAG * self.n_vector + 1
-        )
+        self.n_vector = 4 + self.stages
+        self.vector_at = [self.compute_end]
+        for wait in [1, 2] + [VECTOR_LAG] * self.stages + [1, 1]:
+            self.vector_at.append(self.vector_at[-1] + wait)
+        self.slots = max(self.first + self.total + self.end_lag, self.vector_at[-1] + 1)
 
 
 def rear_body(plan, frames, head, meta, *refs):
     (
-        back_ref, pre1_ref, x1_ref, g_middle1_ref, gain_ref, pattern_ref, joint_ref,
+        back_ref, pre1_ref, x1_ref, g_middle1_ref, gain_ref, q_gain_ref, k_gain_ref, joint_ref,
         outer_scale, second_gain, mixer_scale, outer_ref, inner_ref, slope_ref, pre0_ref,
         mixer_in, feed_in, middle_in, branch_in, qkv_in, x0_in,
         feed_g, came_in, feed_x1, feed_three1, joint_x1, joint_three1, feed_x0, feed_three0, joint_x0, joint_three0,
         vector_in,
-    ) = refs[:31]
-    tokens_ref, outer_out, inner_out, mixer_out, joint_out, vector_out = refs[31:37]
+    ) = refs[:32]
+    tokens_ref, outer_out, inner_out, mixer_out, joint_out, vector_out = refs[32:38]
     (
-        own, came, acts, hids, act_turned, hid_turned, parts, last, sums,
+        own, came, acts, hids, act_turned, hid_turned, parts, last, sums, v_half, v_part,
         mixer, feed0, middle0, branch0, qkv0, x0,
         g1, g_middle0, g_att0, g_feed, g_qkv, total_sum,
-    ) = refs[37:58]
-    steps = refs[58 : 58 + plan.stages]
-    load_sem, act_sem, hid_sem, g_send, g_recv, p_send, p_recv, f_send, f_recv, v_send, v_recv = refs[58 + plan.stages :]
+    ) = refs[38:61]
+    steps = refs[61 : 61 + plan.stages]
+    load_sem, act_sem, hid_sem, g_send, g_recv, p_send, p_recv, f_send, f_recv, v_send, v_recv = refs[61 + plan.stages :]
     slot = pl.program_id(0)
     rows = own.shape[2]
     half, hidden_half, chips, total = plan.half, plan.hidden_half, plan.chips, plan.total
@@ -1226,6 +1234,8 @@
             (scene_peer, core_peer, cross_peer)[which],
         )
 
+    targets = [core_peer, scene_peer, cross_peer] + [peer for _, peer in bits]
+
     @pl.when(slot == 0)
     def _():
         load(0).start()
@@ -1239,13 +1249,7 @@
         sums[0] = jnp.zeros(sums.shape[1:], f32)
         for index in range(vector_rows):
             sums[0, section + index : section + index + 1, :] = vector_in[index : index + 1, :]
-        enter([core_peer, scene_peer, cross_peer] + [peer for _, peer in bits])
-        load(0).wait()
-        for copy in hid_loads(0):
-            copy.wait()
-        load(1).wait()
-        for copy in act_loads(0):
-            copy.wait()
+        greet(targets)
 
     def spread(step, steps_of):
         return lax.rem(step, 2) * (steps_of // 2) + step // 2
@@ -1259,7 +1263,7 @@
             )
         joint_back_core(
             1, head, slot, plan.joint_steps, spread(slot, plan.joint_steps), jnp.concatenate(pieces, axis=1),
-            pre1_ref, x1_ref, g_middle1_ref, gain_ref, pattern_ref, joint_ref,
+            pre1_ref, x1_ref, g_middle1_ref, gain_ref, q_gain_ref, k_gain_ref, joint_ref,
             own.at[0], at_joined, g1, Rows(sums, 0, section + vector_rows), total_sum,
         )
 
@@ -1291,7 +1295,7 @@
         joint_back_core(
             0, head, step, plan.joint_steps, chunk,
             g_qkv[:, pl.ds(pl.multiple_of(chunk * CHUNK, CHUNK), CHUNK)],
-            pre0_ref, x0, g_middle0, gain_ref, pattern_ref, joint_ref,
+            pre0_ref, x0, g_middle0, gain_ref, q_gain_ref, k_gain_ref, joint_ref,
             own.at[1], at_joined, tokens_ref, Rows(sums, 0, vector_rows), total_sum,
         )
 
@@ -1431,12 +1435,58 @@
         def _():
             action(index)
 
-    vector_peers = [core_peer, scene_peer] + [peer for _, peer in bits]
+    scene = lax.axis_index("scene")
+    wide, narrow = width // 2, width // 4
+
+    def lanes_of(side, size):
+        return pl.ds(pl.multiple_of(side * size, size), size)
+
+    n_chip = plan.stages
+    vector_peers = [core_peer, scene_peer] + [peer for _, peer in bits] + [scene_peer, core_peer]
 
     def vector_copy(stage):
-        return remote(
-            sums.at[2 * stage], sums.at[2 * stage + 1], v_send.at[stage], v_recv.at[stage], vector_peers[stage]
-        )
+        if stage == 0:
+            source, target = sums.at[0, :, lanes_of(1 - core, wide)], v_half.at[0]
+        elif stage == 1:
+            source, target = v_half.at[1, :, lanes_of(1 - scene, narrow)], v_part.at[0]
+        elif stage < 2 + n_chip:
+            source, target = v_part.at[2 * stage - 3], v_part.at[2 * stage - 2]
+        elif stage == 2 + n_chip:
+            source, target = v_part.at[2 * stage - 3], v_part.at[2 * stage - 2]
+        else:
+            source, target = v_half.at[2], v_half.at[3]
+        return remote(source, target, v_send.at[stage], v_recv.at[stage], vector_peers[stage])
+
+    def vector_step(stage):
+        vector_copy(stage).wait()
+        if stage == 0:
+            v_half[1] = sums[0, :, lanes_of(core, wide)] + v_half[0]
+        elif stage == 1:
+            v_part[1] = v_half[1, :, lanes_of(scene, narrow)] + v_part[0]
+        elif stage < 2 + n_chip:
+            v_part[2 * stage - 1] = v_part[2 * stage - 3] + v_part[2 * stage - 2]
+        elif stage == 2 + n_chip:
+            v_half[2, :, lanes_of(scene, narrow)] = v_part[2 * stage - 3]
+            v_half[2, :, lanes_of(1 - scene, narrow)] = v_part[2 * stage - 2]
+        else:
+            vector_out[:, lanes_of(core, wide)] = v_half[2]
+            vector_out[:, lanes_of(1 - core, wide)] = v_half[3]
+
+    @pl.when(slot == 0)
+    def _():
+        pl.semaphore_wait(pltpu.get_barrier_semaphore(), len(targets))
+        load(0).wait()
+
+    @pl.when(slot == plan.first)
+    def _():
+        load(1).wait()
+        for copy in hid_loads(0):
+            copy.wait()
+
+    @pl.when(slot == plan.first + n_outer)
+    def _():
+        for copy in act_loads(0):
+            copy.wait()
 
     when_due(0, multiply)
     for stage in range(plan.stages):
@@ -1445,14 +1495,9 @@
 
     for stage in range(plan.n_vector):
 
-        @pl.when(slot == plan.compute_end + VECTOR_LAG * (stage + 1))
+        @pl.when(slot == plan.vector_at[stage + 1])
         def _():
-            vector_copy(stage).wait()
-            result = sums[2 * stage] + sums[2 * stage + 1]
-            if stage + 1 < plan.n_vector:
-                sums[2 * stage + 2] = result
-            else:
-                vector_out[...] = result
+            vector_step(stage)
 
     for stage in range(plan.stages - 1):
         when_due(plan.lags[stage], partial(stage_start, stage + 1))
@@ -1468,7 +1513,7 @@
 
     for stage in range(plan.n_vector):
 
-        @pl.when(slot == plan.compute_end + VECTOR_LAG * stage)
+        @pl.when(slot == plan.vector_at[stage])
         def _():
             vector_copy(stage).start()
 
@@ -1555,7 +1600,7 @@
                 single(x1.shape),
                 single(g_middle1.shape),
                 single(gain.shape),
-                single(pattern.shape),
+                single(pattern[0].shape), single(pattern[2].shape),
                 pl.BlockSpec((1, width, CHUNK), joint_map),
                 single(outer_scale.shape),
                 single(second_gain.shape),
@@ -1577,7 +1622,9 @@
                 pltpu.VMEM((plan.hidden_half, 4 * rows), bf16),
                 pltpu.VMEM(container, bf16),
                 pltpu.VMEM((plan.ring, plan.deep, CHUNK), bf16),
-                pltpu.VMEM((2 * plan.n_vector, n_vector_rows, width), f32),
+                pltpu.VMEM((1, n_vector_rows, width), f32),
+                pltpu.VMEM((4, n_vector_rows, half), f32),
+                pltpu.VMEM((2 * plan.stages + 3, n_vector_rows, half // 2), f32),
                 pltpu.VMEM((1, width, width), bf16),
                 pltpu.VMEM((rows, width), f32),
                 pltpu.VMEM((rows, width), f32),
@@ -1611,7 +1658,7 @@
         ),
         cost_estimate=pl.CostEstimate(flops=2 * rows * width * hidden * 20, bytes_accessed=60 * width * hidden, transcendentals=0),
     )(
-        meta, back, pre1, x1, g_middle1, gain, pattern, joint, outer_scale, second_gain, mixer_scale, outer, inner, slope0, pre0,
+        meta, back, pre1, x1, g_middle1, gain, pattern[0], pattern[2], joint, outer_scale, second_gain, mixer_scale, outer, inner, slope0, pre0,
         mixer, feed0, middle0, branch0, qkv0, x0, feed_g1, came1, *shares, vector1,
     )
 
@@ -1693,14 +1740,8 @@
     heads = width // head
     hidden = inner_weight.shape[2]
     chips = frames // 2
-    scene = lax.axis_index("scene")
-    frame = lax.axis_index("frame")
-    core = lax.rem(frame, 2)
-    meta = jnp.stack([scene, core, lax.rem(frame // 2, 2), patch_counts[0, 0]]).astype(jnp.int32)
-    pattern = jnp.tile(
-        jnp.stack([vector[block] for block in range(2) for vector in (query_gain, query_shift, key_gain)]).astype(f32),
-        (1, SLAB // head),
-    )
+    meta = patch_counts.reshape(1)
+    pattern = (query_gain, query_shift, key_gain)
 
     x0 = tokens[0]
     feed_params = (mixer_weight, mixer_bias, mixer_scale, second_gain, second_shift, inner_weight, inner_bias, outer_weight, outer_bias, outer_scale)

time: 336 us -> 320 us (0.952)
  Pallas kernels: 330 us -> 317 us
    pallas_call x1, Pallas kernels: 160 us -> 153 us  [rear(): pl.pallas_call(partial(rear_body, plan, frames, head), name='rear', out_s...]
where the time goes in v3:
time: 320 us; the launch traced here: 319 us
  Pallas kernels  317 us (99%)
    pallas_call x1, Pallas kernels, rear(): pl.pallas_call(partial(rear_body, plan, frames, head), name='rear', out_s...  153 us
    pallas_call x1, Pallas kernels, scene_backward(): pl.pallas_call(partial(scene_back_body, frames, half, span, len(pairs), s...  50.8 us
    pallas_call x1, Pallas kernels, scene_forward(): pl.pallas_call(partial(scene_body, frames, half, span, len(pairs)), name=...  40.5 us
    pallas_call x2, Pallas kernels, feed_forward(): call(partial(feed_body, block, packed), f'feed_forward_{block}', (steps,)...  32.1 us
    pallas_call x2, Pallas kernels, joint_forward(): call(partial(joint_body, block, packed, head), f'joint_forward_{block}',...  17.3 us
    pallas_call x1, Pallas kernels, feed_backward(): call(partial(feed_back_body, block, packed), f'feed_backward_{block}', (s...  16.3 us

profile of v3, /device:TPU:0, one launch (start us, length us, event | category | flops | bytes accessed | tf_op | source)
XLA Modules:
  0.0 318.6 jit_solution(6924264275325803822)
XLA Ops:
  1.3 8.3 %joint_forward_0.1 = (bf16[144,512]{1,0:T(8,128)(2,1)}, bf16[144,512]{1,0:T(8,128)(2,1)}, f32[144,2048]{1,0:T(8,128)}, bf16[144,3072]{1,0:T(8,128)(2,1)}) custom-call(s32[1]{0:T(128)} %bitcast.5.meta, bf16[144,1024]{1,0:T(8,128)(2,1)} %bitcast.15, bf16[2,1024]{1,0:T(2,128)(2,1)} %refs_4_.1, bf16[2,1024]{1,0:T(2,128)(2,1)} %shift_ref.6, ...), custom_call_target="tpu_custom_call" | custom-call | flops 905969664 | bytes 8650752 | tf_op jit(solution)/shard_map/joint_forward_0/pallas_call | solution.py:245
  9.6 3.1 frame_forward.1.att_ref
  12.7 16.0 %feed_forward_0.1 = (bf16[144,3072]{1,0:T(8,128)(2,1)}, bf16[144,3072]{1,0:T(8,128)(2,1)}, f32[144,1024]{1,0:T(8,128)}, f32[144,1024]{1,0:T(8,128)}, f32[144,102...) custom-call(s32[1]{0:T(128)} %bitcast.7.meta, bf16[144,1024]{1,0:T(8,128)(2,1)} %frame_forward.1.att_ref, ...), custom_call_target="tpu_custom_call" | custom-call | flops 2717908992 | bytes 23560192 | tf_op jit(solution)/shard_map/feed_forward_0/pallas_call | solution.py:898
  28.8 9.0 %joint_forward_1.1 = (bf16[144,512]{1,0:T(8,128)(2,1)}, bf16[144,512]{1,0:T(8,128)(2,1)}, f32[144,2048]{1,0:T(8,128)}, bf16[16,224,128]{2,1,0:T(8,128)(2,1)}) custom-call(s32[1]{0:T(128)} %bitcast.8.meta, f32[144,1024]{1,0:T(8,128)} %get-tuple-element.80.x_ref.refs_2_, bf16[2,1024]{1,0:T(2,128)(2,1)} %refs_4_.1, bf16[2,1024]{1,0:T(2,128)(2,1)} %shift_ref.6, ...), custom_call_target="tpu_custom_call" | custom-call | flops 905969664 | bytes 8650752 | tf_op jit(solution)/shard_map/joint_forward_1/pallas_call | solution.py:245
  37.8 40.5 %scene_forward.1 = (bf16[16,72,128]{2,1,0:T(8,128)(2,1)}, bf16[16,224,128]{2,1,0:T(8,128)(2,1)}, f32[1152,128]{1,0:T(8,128)}, f32[1152,128]{1,0:T(8,128)}, bf16[...) custom-call(s32[1]{0:T(128)} %bitcast.9.meta, ...), custom_call_target="tpu_custom_call" | custom-call | flops 2717908992 | bytes 2949120 | tf_op jit(solution)/shard_map/scene_forward/pallas_call | solution.py:560
  78.3 16.0 %feed_forward_1.1 = (bf16[144,3072]{1,0:T(8,128)(2,1)}, bf16[144,3072]{1,0:T(8,128)(2,1)}, f32[144,1024]{1,0:T(8,128)}, f32[144,1024]{1,0:T(8,128)}, f32[144,102...) custom-call(s32[1]{0:T(128)} %bitcast.10.meta, bf16[16,72,128]{2,1,0:T(8,128)(2,1)} %get-tuple-element.88.att_ref, ...), custom_call_target="tpu_custom_call" | custom-call | flops 2717908992 | bytes 23560192 | tf_op jit(solution)/shard_map/feed_forward_1/pallas_call | solution.py:898
  94.3 16.3 %feed_backward_1.1 = (bf16[2,144,3072]{2,1,0:T(8,128)(2,1)}, f32[144,1024]{1,0:T(8,128)}, bf16[16,72,128]{2,1,0:T(8,128)(2,1)}, f32[10,1024]{1,0:T(8,128)}) custom-call(s32[1]{0:T(128)} %bitcast.11.meta, bf16[144,1024]{1,0:T(8,128)(2,1)} %bitcast.18, f32[144,1024]{1,0:T(8,128)} %get-tuple-element.91.refs_1_, f32[144,4096]{1,0:T(8,128)} %get-tuple-element.92.refs_2_, ...), custom_call_target="tpu_custom_call" | custom-call | flops 2717908992 | bytes 24444928 | tf_op jit(solution)/shard_map/feed_backward_1/pallas_call | solution.py:994
  110.6 50.8 %scene_backward.1 = (bf16[16,3,72,128]{3,2,1,0:T(8,128)(2,1)}, bf16[3,144,3072]{2,1,0:T(8,128)(2,1)}, bf16[3,144,3072]{2,1,0:T(8,128)(2,1)}) custom-call(s32[1]{0:T(128)} %bitcast.12.meta, bf16[16,224,128]{2,1,0:T(8,128)(2,1)} %get-tuple-element.90.kept_ref, bf16[16,72,128]{2,1,0:T(8,128)(2,1)} %get-tuple-element.95.grad_ref, ...), custom_call_target="tpu_custom_call" | custom-call | flops 6794772480 | bytes 4423680 | tf_op jit(solution)/shard_map/scene_backward/pallas_call | solution.py:775
  161.3 152.6 %rear.1 = (bf16[144,1024]{1,0:T(8,128)(2,1)}, f32[2,128,1024]{2,1,0:T(8,128)}, f32[2,32,4096]{2,1,0:T(8,128)}, f32[2,32,1024]{2,1,0:T(8,128)}, f32[2,32,3072]{2,1,0:T(8,128)}, /*index=5*/f32[36,1024]{1,0:T(8,128)}) custom-call(s32[1]{0:T(128)} %bitcast.13.meta, bf16[16,3,72,128]{3,2,1,0:T(8,128)(2,1)} %get-tuple-element.101.refs_0_, ...), custom_call_target="tpu_custom_call" | custom-call | flops 24159191040 | bytes 251658240 | tf_op jit(solution)/shard_map/rear/pallas_call | solution.py:1590
  314.0 4.5 %finish.1 = (bf16[144,1024]{1,0:T(8,128)(2,1)}, f32[2,128,1024]{2,1,0:T(8,128)}, f32[2,32,4096]{2,1,0:T(8,128)}, f32[2,32,1024]{2,1,0:T(8,128)}, f32[2,32,3072]{...) custom-call(s32[1]{0:T(128)} %bitcast.14.meta, ...), custom_call_target="tpu_custom_call" | custom-call | tf_op jit(solution)/shard_map/finish/pallas_call | solution.py:1722

commit v4 on v3

--- a/solution.py
+++ b/solution.py
@@ -9,11 +9,14 @@
 
 SPECIAL = 5
 CHUNK = 512
+WIDE = 1024
 LANES = 128
 SLAB = 256
 SHARED_PIECES = 3
 SWAP_EVERY = 3
 AHEAD = 2
+LEAD = 6
+DOUBLED = 0
 LAG = 3
 VECTOR_LAG = 3
 norm_eps = 1e-06
@@ -158,7 +161,7 @@
 ):
     step = pl.program_id(0)
     rows, width = normed_ref.shape
-    per_part = width // CHUNK
+    per_part = width // WIDE
     half = rows // 2
 
     @pl.when(step == 0)
@@ -188,8 +191,8 @@
 
     def emit(part, values):
         if packed:
-            base = (step - part * per_part) * (CHUNK // head)
-            for slab in range(CHUNK // LANES):
+            base = (step - part * per_part) * (WIDE // head)
+            for slab in range(WIDE // LANES):
                 even, odd = pack_pair(values[:, slab * LANES : (slab + 1) * LANES])
                 stage[0][base + 2 * slab, part * half : (part + 1) * half, :] = even
                 stage[0][base + 2 * slab + 1, part * half : (part + 1) * half, :] = odd
@@ -199,7 +202,7 @@
     def normed_heads(gain, shift):
         mean_matrix = seg_matrix(SLAB, head, 1.0 / head)
         pieces = []
-        for slab in range(CHUNK // SLAB):
+        for slab in range(WIDE // SLAB):
             hat, _ = seg_norm(joined[:, slab * SLAB : (slab + 1) * SLAB], mean_matrix)
             pieces.append(hat * gain if shift is None else hat * gain + shift)
         return jnp.concatenate(pieces, axis=1)
@@ -232,14 +235,14 @@
 
 def joint_forward(block, packed, head, meta, x, gain, shift, pattern, weight, bias):
     rows, width = x.shape
-    per_part = width // CHUNK
+    per_part = width // WIDE
     heads = width // head
     packed_rows = 3 * (rows // 2) + 8
     if packed:
         out_spec, out = full((heads, packed_rows, LANES)), sds((heads, packed_rows, LANES), bf16)
         extra = [pltpu.VMEM((heads, packed_rows, LANES), f32)]
     else:
-        out_spec = pl.BlockSpec((rows, CHUNK), lambda j, m: (0, j))
+        out_spec = pl.BlockSpec((rows, WIDE), lambda j, m: (0, j))
         out = sds((rows, 3 * width), bf16)
         extra = []
     return call(
@@ -251,13 +254,13 @@
             full(gain.shape),
             full(shift.shape),
             full(pattern[0].shape), full(pattern[1].shape), full(pattern[2].shape),
-            pl.BlockSpec((1, width, CHUNK), lambda j, m: (block, 0, j)),
-            pl.BlockSpec((2, CHUNK), lambda j, m: (0, j)),
+            pl.BlockSpec((1, width, WIDE), lambda j, m: (block, 0, j)),
+            pl.BlockSpec((2, WIDE), lambda j, m: (0, j)),
         ],
         [
             full((rows, width // 2)),
             full((rows, width // 2)),
-            pl.BlockSpec((rows, CHUNK), lambda j, m: (0, jnp.minimum(j, 2 * per_part - 1))),
+            pl.BlockSpec((rows, WIDE), lambda j, m: (0, jnp.minimum(j, 2 * per_part - 1))),
             out_spec,
         ],
         [
@@ -824,7 +827,7 @@
     steps = pl.num_programs(0)
     rows, width = middle_ref.shape
     hidden_half = own_ref.shape[1] - width
-    half_steps = hidden_half // CHUNK
+    half_steps = hidden_half // WIDE
     mine = lax.axis_index("scene")
 
     def split(value, at):
@@ -866,15 +869,15 @@
     share = 0.5 * (1.0 + erf(pre * (2.0 ** (-0.5))))
     slope_ref[...] = share + pre * jnp.exp(-0.5 * pre * pre) * 0.3989422804014327
     hidden = (pre * share).astype(bf16)
-    place = pl.multiple_of(lax.rem(step, half_steps) * CHUNK, CHUNK)
+    place = pl.multiple_of(lax.rem(step, half_steps) * WIDE, WIDE)
 
     @pl.when(step // half_steps == mine)
     def _():
-        own_ref[:, pl.ds(place, CHUNK)] = hidden
+        own_ref[:, pl.ds(place, WIDE)] = hidden
 
     @pl.when(step // half_steps != mine)
     def _():
-        other_ref[:, pl.ds(place, CHUNK)] = hidden
+        other_ref[:, pl.ds(place, WIDE)] = hidden
 
     total_ref[...] += nn(hidden, outer_ref[0])
 
@@ -893,7 +896,7 @@
     rows, width = x.shape
     hidden = inner.shape[2]
     kept = hidden // 2 + width
-    steps = hidden // CHUNK
+    steps = hidden // WIDE
     vector = full(gain.shape)
     return call(
         partial(feed_body, block, packed),
@@ -904,14 +907,14 @@
             full((rows, width)),
             pl.BlockSpec((1, width, width), lambda j, m: (block, 0, 0)),
             vector, vector, vector, vector,
-            pl.BlockSpec((1, width, CHUNK), lambda j, m: (block, 0, j)),
-            pl.BlockSpec((2, CHUNK), lambda j, m: (0, j)),
-            pl.BlockSpec((1, CHUNK, width), lambda j, m: (block, j, 0)),
+            pl.BlockSpec((1, width, WIDE), lambda j, m: (block, 0, j)),
+            pl.BlockSpec((2, WIDE), lambda j, m: (0, j)),
+            pl.BlockSpec((1, WIDE, width), lambda j, m: (block, j, 0)),
             vector, vector,
         ],
         [full((rows, kept))] * 2
         + [full((rows, width))] * 3
-        + [pl.BlockSpec((rows, CHUNK), lambda j, m: (0, j)), full((rows, width))],
+        + [pl.BlockSpec((rows, WIDE), lambda j, m: (0, j)), full((rows, width))],
         [sds((rows, kept), bf16)] * 2
         + [sds((rows, width), f32)] * 3
         + [sds((rows, hidden), f32), sds((rows, width), bf16 if packed else f32)],
@@ -927,8 +930,9 @@
     grads_ref, g_middle_ref, g_att_ref, vector_ref, g_feed_ref, total_ref
 ):
     rows, width = total_ref.shape
+    size = inner_ref.shape[2]
     half_steps = steps // 2
-    at_branch = width // 2 + half_steps * CHUNK
+    at_branch = width // 2 + half_steps * size
 
     def incoming():
         g = g_ref[...].astype(f32)
@@ -949,10 +953,10 @@
         total_ref[...] = jnp.zeros_like(total_ref)
 
     g_pre = (nt(g_feed_ref[...], outer_ref[0]) * slope_ref[...]).astype(bf16)
-    place = pl.multiple_of(width // 2 + lax.rem(chunk, half_steps) * CHUNK, CHUNK)
-    grads_ref[chunk // half_steps, :, pl.ds(place, CHUNK)] = g_pre
-    per_row = width // CHUNK
-    lanes = pl.ds(pl.multiple_of(lax.rem(chunk, per_row) * CHUNK, CHUNK), CHUNK)
+    place = pl.multiple_of(width // 2 + lax.rem(chunk, half_steps) * size, CHUNK)
+    grads_ref[chunk // half_steps, :, pl.ds(place, size)] = g_pre
+    per_row = width // size
+    lanes = pl.ds(pl.multiple_of(lax.rem(chunk, per_row) * size, size), size)
     vector_ref[pl.ds(6 + chunk // per_row, 1), lanes] = col_sum(g_pre.astype(f32))
     total_ref[...] += nt(g_pre, inner_ref[0])
 
@@ -987,7 +991,7 @@
 def feed_backward(block, packed, heads, meta, g, feed, slope, middle, branch, outer_scale, gain, mixer_scale, outer, inner, mixer):
     rows, width = middle.shape
     hidden = inner.shape[2]
-    steps = hidden // CHUNK
+    steps = hidden // WIDE
     vector = full(gain.shape)
     vector_rows = 6 + hidden // width
     att_shape = (heads, rows // 2, LANES) if packed else (rows, width)
@@ -998,12 +1002,12 @@
         [
             full((rows, width)),
             full((rows, width)),
-            pl.BlockSpec((rows, CHUNK), lambda j, m: (0, j)),
+            pl.BlockSpec((rows, WIDE), lambda j, m: (0, j)),
             full((rows, width)),
             full((rows, width)),
             vector, vector, vector,
-            pl.BlockSpec((1, CHUNK, width), lambda j, m: (block, j, 0)),
-            pl.BlockSpec((1, width, CHUNK), lambda j, m: (block, 0, j)),
+            pl.BlockSpec((1, WIDE, width), lambda j, m: (block, j, 0)),
+            pl.BlockSpec((1, width, WIDE), lambda j, m: (block, 0, j)),
             pl.BlockSpec((1, width, width), lambda j, m: (block, 0, 0)),
         ],
         [
@@ -1140,11 +1144,15 @@
         self.leave.append((self.frame_at + 1, 1, 1 + self.n_inner))
         for piece in range(self.n_joint):
             self.leave.append((self.joint_at + 2 + 2 * piece, 1, at_joined + piece))
-        first = 1
+        self.doubled = DOUBLED
+        first = 0
         for slot, block, piece in self.leave:
-            unit = 0 if piece == 0 else piece + self.n_outer - 1
-            first = max(first, slot + AHEAD - block * self.per_block - unit)
+            first = max(first, self.turn_of(slot) + AHEAD - self.index_of(block, piece))
         self.first = first
+        self.leave = [
+            (max(slot, self.slot_of(first + self.index_of(block, piece) - LEAD)), block, piece)
+            for slot, block, piece in self.leave
+        ]
         self.ring = 12
         self.lags = [LAG * (stage + 1) for stage in range(self.stages)]
         self.end_lag = self.lags[-1] + 2
@@ -1152,7 +1160,16 @@
         self.vector_at = [self.compute_end]
         for wait in [1, 2] + [VECTOR_LAG] * self.stages + [1, 1]:
             self.vector_at.append(self.vector_at[-1] + wait)
-        self.slots = max(self.first + self.total + self.end_lag, self.vector_at[-1] + 1)
+        self.slots = max(self.slot_of(self.first + self.total + self.end_lag), self.vector_at[-1] + 1)
+
+    def index_of(self, block, piece):
+        return block * self.per_block + (0 if piece == 0 else piece + self.n_outer - 1)
+
+    def turn_of(self, slot):
+        return slot // 2 if slot < 2 * self.doubled else slot - self.doubled
+
+    def slot_of(self, turn):
+        return 2 * turn + 1 if turn < self.doubled else turn + self.doubled
 
 
 def rear_body(plan, frames, head, meta, *refs):
@@ -1428,10 +1445,17 @@
         last_copy(index).wait()
         put(index, 1 - core, last[lax.rem(index, plan.ring)].astype(f32))
 
+    early = slot < 2 * plan.doubled
+    turn_now = jnp.where(early, slot // 2, slot - plan.doubled)
+    active = jnp.logical_not(early) | (lax.rem(slot, 2) == 1)
+
+    def when_turn(at):
+        return pl.when(active & (turn_now == at))
+
     def when_due(lag, action):
-        index = slot - plan.first - lag
-
-        @pl.when((index >= 0) & (index < total))
+        index = turn_now - plan.first - lag
+
+        @pl.when(active & (index >= 0) & (index < total))
         def _():
             action(index)
 
@@ -1477,13 +1501,13 @@
         pl.semaphore_wait(pltpu.get_barrier_semaphore(), len(targets))
         load(0).wait()
 
-    @pl.when(slot == plan.first)
+    @when_turn(plan.first)
     def _():
         load(1).wait()
         for copy in hid_loads(0):
             copy.wait()
 
-    @pl.when(slot == plan.first + n_outer)
+    @when_turn(plan.first + n_outer)
     def _():
         for copy in act_loads(0):
             copy.wait()
@@ -1517,22 +1541,22 @@
         def _():
             vector_copy(stage).start()
 
-    @pl.when(slot == plan.first + 1)
+    @when_turn(plan.first + 1)
     def _():
         for copy in hid_loads(1):
             copy.start()
 
-    @pl.when(slot == plan.first + per_block - 1)
+    @when_turn(plan.first + per_block - 1)
     def _():
         for copy in hid_loads(1):
             copy.wait()
 
-    @pl.when(slot == plan.first + n_outer + n_inner + 1)
+    @when_turn(plan.first + n_outer + n_inner + 1)
     def _():
         for copy in act_loads(1):
             copy.start()
 
-    @pl.when(slot == plan.first + per_block + n_outer - 1)
+    @when_turn(plan.first + per_block + n_outer - 1)
     def _():
         for copy in act_loads(1):
             copy.wait()

time: 320 us -> 310 us (0.969)
  Pallas kernels: 317 us -> 308 us
    pallas_call x2, Pallas kernels: 32.1 us -> 27.9 us  [feed_forward(): call(partial(feed_body, block, packed), f'feed_forward_{block}', (steps,)...]
    pallas_call x2, Pallas kernels: 17.3 us -> 13.9 us  [joint_forward(): call(partial(joint_body, block, packed, head), f'joint_forward_{block}',...]
where the time goes in v4:
time: 310 us
  Pallas kernels  308 us (99%)
    pallas_call x1, Pallas kernels, rear(): pl.pallas_call(partial(rear_body, plan, frames, head), name='rear', out_s...  153 us
    pallas_call x1, Pallas kernels, scene_backward(): pl.pallas_call(partial(scene_back_body, frames, half, span, len(pairs), s...  50.8 us
    pallas_call x1, Pallas kernels, scene_forward(): pl.pallas_call(partial(scene_body, frames, half, span, len(pairs)), name=...  40.5 us
    pallas_call x2, Pallas kernels, feed_forward(): call(partial(feed_body, block, packed), f'feed_forward_{block}', (steps,)...  27.9 us
    pallas_call x1, Pallas kernels, feed_backward(): call(partial(feed_back_body, block, packed), f'feed_backward_{block}', (s...  14.8 us
    pallas_call x2, Pallas kernels, joint_forward(): call(partial(joint_body, block, packed, head), f'joint_forward_{block}',...  13.9 us

profile of v4, /device:TPU:0, one launch (start us, length us, event | category | flops | bytes accessed | tf_op | source)
XLA Modules:
  0.0 309.7 jit_solution(14013545343426975566)
XLA Ops:
  1.3 6.7 %joint_forward_0.1 = (bf16[144,512]{1,0:T(8,128)(2,1)}, bf16[144,512]{1,0:T(8,128)(2,1)}, f32[144,2048]{1,0:T(8,128)}, bf16[144,3072]{1,0:T(8,128)(2,1)}) custom-call(s32[1]{0:T(128)} %bitcast.5.meta, bf16[144,1024]{1,0:T(8,128)(2,1)} %bitcast.15, bf16[2,1024]{1,0:T(2,128)(2,1)} %refs_4_.1, bf16[2,1024]{1,0:T(2,128)(2,1)} %shift_ref.6, ...), custom_call_target="tpu_custom_call" | custom-call | flops 905969664 | bytes 8650752 | tf_op jit(solution)/shard_map/joint_forward_0/pallas_call | solution.py:248
  8.0 3.1 frame_forward.1.att_ref
  11.0 14.0 %feed_forward_0.1 = (bf16[144,3072]{1,0:T(8,128)(2,1)}, bf16[144,3072]{1,0:T(8,128)(2,1)}, f32[144,1024]{1,0:T(8,128)}, f32[144,1024]{1,0:T(8,128)}, f32[144,102...) custom-call(s32[1]{0:T(128)} %bitcast.7.meta, bf16[144,1024]{1,0:T(8,128)(2,1)} %frame_forward.1.att_ref, ...), custom_call_target="tpu_custom_call" | custom-call | flops 2717908992 | bytes 23560192 | tf_op jit(solution)/shard_map/feed_forward_0/pallas_call | solution.py:901
  25.0 7.2 %joint_forward_1.1 = (bf16[144,512]{1,0:T(8,128)(2,1)}, bf16[144,512]{1,0:T(8,128)(2,1)}, f32[144,2048]{1,0:T(8,128)}, bf16[16,224,128]{2,1,0:T(8,128)(2,1)}) custom-call(s32[1]{0:T(128)} %bitcast.8.meta, f32[144,1024]{1,0:T(8,128)} %get-tuple-element.80.x_ref.refs_2_, bf16[2,1024]{1,0:T(2,128)(2,1)} %refs_4_.1, bf16[2,1024]{1,0:T(2,128)(2,1)} %shift_ref.6, ...), custom_call_target="tpu_custom_call" | custom-call | flops 905969664 | bytes 8650752 | tf_op jit(solution)/shard_map/joint_forward_1/pallas_call | solution.py:248
  32.2 40.5 %scene_forward.1 = (bf16[16,72,128]{2,1,0:T(8,128)(2,1)}, bf16[16,224,128]{2,1,0:T(8,128)(2,1)}, f32[1152,128]{1,0:T(8,128)}, f32[1152,128]{1,0:T(8,128)}, bf16[...) custom-call(s32[1]{0:T(128)} %bitcast.9.meta, ...), custom_call_target="tpu_custom_call" | custom-call | flops 2717908992 | bytes 2949120 | tf_op jit(solution)/shard_map/scene_forward/pallas_call | solution.py:563
  72.7 13.9 %feed_forward_1.1 = (bf16[144,3072]{1,0:T(8,128)(2,1)}, bf16[144,3072]{1,0:T(8,128)(2,1)}, f32[144,1024]{1,0:T(8,128)}, f32[144,1024]{1,0:T(8,128)}, f32[144,102...) custom-call(s32[1]{0:T(128)} %bitcast.10.meta, bf16[16,72,128]{2,1,0:T(8,128)(2,1)} %get-tuple-element.88.att_ref, ...), custom_call_target="tpu_custom_call" | custom-call | flops 2717908992 | bytes 23560192 | tf_op jit(solution)/shard_map/feed_forward_1/pallas_call | solution.py:901
  86.6 14.8 %feed_backward_1.1 = (bf16[2,144,3072]{2,1,0:T(8,128)(2,1)}, f32[144,1024]{1,0:T(8,128)}, bf16[16,72,128]{2,1,0:T(8,128)(2,1)}, f32[10,1024]{1,0:T(8,128)}) custom-call(s32[1]{0:T(128)} %bitcast.11.meta, bf16[144,1024]{1,0:T(8,128)(2,1)} %bitcast.18, f32[144,1024]{1,0:T(8,128)} %get-tuple-element.91.refs_1_, f32[144,4096]{1,0:T(8,128)} %get-tuple-element.92.refs_2_, ...), custom_call_target="tpu_custom_call" | custom-call | flops 2717908992 | bytes 24444928 | tf_op jit(solution)/shard_map/feed_backward_1/pallas_call | solution.py:998
  101.4 50.8 %scene_backward.1 = (bf16[16,3,72,128]{3,2,1,0:T(8,128)(2,1)}, bf16[3,144,3072]{2,1,0:T(8,128)(2,1)}, bf16[3,144,3072]{2,1,0:T(8,128)(2,1)}) custom-call(s32[1]{0:T(128)} %bitcast.12.meta, bf16[16,224,128]{2,1,0:T(8,128)(2,1)} %get-tuple-element.90.kept_ref, bf16[16,72,128]{2,1,0:T(8,128)(2,1)} %get-tuple-element.95.grad_ref, ...), custom_call_target="tpu_custom_call" | custom-call | flops 6794772480 | bytes 4423680 | tf_op jit(solution)/shard_map/scene_backward/pallas_call | solution.py:778
  152.2 152.8 %rear.1 = (bf16[144,1024]{1,0:T(8,128)(2,1)}, f32[2,128,1024]{2,1,0:T(8,128)}, f32[2,32,4096]{2,1,0:T(8,128)}, f32[2,32,1024]{2,1,0:T(8,128)}, f32[2,32,3072]{2,1,0:T(8,128)}, /*index=5*/f32[36,1024]{1,0:T(8,128)}) custom-call(s32[1]{0:T(128)} %bitcast.13.meta, bf16[16,3,72,128]{3,2,1,0:T(8,128)(2,1)} %get-tuple-element.101.refs_0_, ...), custom_call_target="tpu_custom_call" | custom-call | flops 24159191040 | bytes 251658240 | tf_op jit(solution)/shard_map/rear/pallas_call | solution.py:1614
  305.0 4.5 %finish.1 = (bf16[144,1024]{1,0:T(8,128)(2,1)}, f32[2,128,1024]{2,1,0:T(8,128)}, f32[2,32,4096]{2,1,0:T(8,128)}, f32[2,32,1024]{2,1,0:T(8,128)}, f32[2,32,3072]{...) custom-call(s32[1]{0:T(128)} %bitcast.14.meta, ...), custom_call_target="tpu_custom_call" | custom-call | tf_op jit(solution)/shard_map/finish/pallas_call | solution.py:1746
